TPU v7x, 32 devices: a whole 2x2x4 slice. The times are simulated.
32 devices in a mesh: section: 2 (over y), expert: 16 (over z, x, core).
Axes of the slice: x: 2, y: 2, z: 4, core: 2. Of those that a mesh axis runs over, the one named last changes fastest.
Arguments:
- forward_input: bfloat16 [128, 3584], P('expert', 'section'), may hold values from -6 to 6
- forward_route: int32 [128, 8], P('expert'), may hold values from 0 to 15, all different within a row; in each aligned block of 8 rows (0 to 7, 8 to 15, ...) at most 8 rows name the same one
- forward_weight: float32 [128, 8], P('expert'), may hold values from 0.05 to 0.5
- output_grad: bfloat16 [128, 3584], P('expert', 'section'), may hold values from -6 to 6
- backward_route: int32 [128, 8], P('expert'), may hold values from 0 to 15, all different within a row; in each aligned block of 8 rows (0 to 7, 8 to 15, ...) at most 8 rows name the same one
- backward_weight: float32 [128, 8], P('expert'), may hold values from 0.05 to 0.5
- gate_stash: bfloat16 [16, 128, 2560], P('expert', None, 'section'), may hold values from -6 to 6
- up_stash: bfloat16 [16, 128, 2560], P('expert', None, 'section'), may hold values from -6 to 6
- gate_matrix: bfloat16 [16, 2560, 3584], P('expert', 'section'), may hold values from -0.125 to 0.125
- up_matrix: bfloat16 [16, 2560, 3584], P('expert', 'section'), may hold values from -0.125 to 0.125
- down_matrix: bfloat16 [16, 2560, 3584], P('expert', 'section'), may hold values from -0.15625 to 0.15625
Outputs:
- forward_output: bfloat16 [128, 3584], P('expert', 'section')
- input_grad: bfloat16 [128, 3584], P('expert', 'section')
Inputs may be any that keep to these rules, and one draw needn't show every extreme that they name: `forward_route`: each row names 8 different experts. In each aligned block of 8 rows (the rows of one index of expert) no expert is named by more than 8 rows, a bound that some block reaches. `backward_route`: as for forward_route.
All inputs are finite; a program needn't handle non-finite values.
Results may differ from a plain program's by a relative error of at most 0.0072.
Values may be sent and summed in bfloat16 or wider, within the bound.
No kernel may reach another device: no remote copies, remote signals or barrier semaphores. Data moves between devices by JAX's collectives and lax.ppermute only.
A program may use at most 128 MiB of HBM per device.

v0:
```python
import jax
import jax.numpy as jnp
from jax import lax
from jax.sharding import PartitionSpec as P


def slot_columns(routes, expert_count, capacity):
    chosen = (
        routes[:, :, None] == jnp.arange(expert_count, dtype=jnp.int32)[None, None, :]
    ).astype(jnp.int32)
    per_token = jnp.sum(chosen, axis=1, dtype=jnp.int32)
    earlier = jnp.cumsum(per_token, axis=0, dtype=jnp.int32) - per_token
    position = jnp.sum(chosen * earlier[:, None, :], axis=2, dtype=jnp.int32)
    return routes * capacity + position


def placement_matrix(columns, weights, total_cols):
    matches = (
        columns[:, :, None] == jnp.arange(total_cols, dtype=jnp.int32)[None, None, :]
    ).astype(jnp.float32)
    return jnp.sum(matches * weights[:, :, None], axis=1)


def contract_last(first_operand, second_operand):
    return lax.dot_general(
        first_operand, second_operand, (((1,), (1,)), ((), ())), preferred_element_type=jnp.float32
    )


def contract_first(first_operand, second_operand):
    return lax.dot_general(
        first_operand, second_operand, (((0,), (1,)), ((), ())), preferred_element_type=jnp.float32
    )


def combine_rows(mixing, returned):
    return lax.dot_general(
        mixing,
        returned.astype(jnp.float32),
        (((1,), (1,)), ((), ())),
        precision=lax.Precision.HIGHEST,
        preferred_element_type=jnp.float32,
    )


def shards(
    forward_input,
    forward_route,
    forward_weight,
    output_grad,
    backward_route,
    backward_weight,
    gate_stash,
    up_stash,
    gate_matrix,
    up_matrix,
    down_matrix,
):
    expert_count = lax.axis_size("expert")
    slot_rows = gate_stash.shape[1]
    capacity = slot_rows // expert_count
    feature_cols = forward_input.shape[1]
    gate_weights = gate_matrix[0]
    up_weights = up_matrix[0]
    down_weights = down_matrix[0]
    unit_weight = jnp.ones(forward_weight.shape, jnp.float32)
    forward_cols = slot_columns(forward_route, expert_count, capacity)
    forward_select = placement_matrix(forward_cols, unit_weight, slot_rows)
    forward_mix = placement_matrix(forward_cols, forward_weight, slot_rows)
    backward_cols = slot_columns(backward_route, expert_count, capacity)
    backward_select = placement_matrix(backward_cols, unit_weight, slot_rows)
    backward_mix = placement_matrix(backward_cols, backward_weight, slot_rows)
    select_rows = forward_select.T.astype(jnp.bfloat16)
    sent = jnp.dot(select_rows, forward_input, preferred_element_type=jnp.float32).astype(
        jnp.bfloat16
    )
    arrived = lax.all_to_all(
        sent.reshape(expert_count, capacity, feature_cols),
        "expert",
        split_axis=0,
        concat_axis=0,
        tiled=True,
    )
    arrived = arrived.reshape(slot_rows, feature_cols)
    portion = lax.all_gather(arrived, "section", axis=1, tiled=True)
    gate_part = gate_weights
    up_part = up_weights
    gate_value = contract_last(portion, gate_part)
    up_value = contract_last(portion, up_part)
    hidden = (jax.nn.silu(gate_value) * up_value).astype(jnp.bfloat16)
    down_part = down_weights
    summed = lax.psum_scatter(
        contract_first(down_part, hidden).astype(jnp.bfloat16),
        "section",
        scatter_dimension=0,
        tiled=True,
    )
    expert_output = summed.reshape(feature_cols, expert_count, capacity)
    returned = lax.all_to_all(
        expert_output, "expert", split_axis=1, concat_axis=1, tiled=True
    ).reshape(feature_cols, slot_rows)
    forward_output = combine_rows(forward_mix, returned).astype(jnp.bfloat16)
    sent_grad = jnp.dot(
        backward_mix.T,
        output_grad.astype(jnp.float32),
        precision=lax.Precision.HIGHEST,
        preferred_element_type=jnp.float32,
    ).astype(jnp.bfloat16)
    arrived_grad = lax.all_to_all(
        sent_grad.reshape(expert_count, capacity, feature_cols),
        "expert",
        split_axis=0,
        concat_axis=0,
        tiled=True,
    )
    arrived_grad = arrived_grad.reshape(slot_rows, feature_cols)
    down_part = down_weights
    grad_hidden = contract_last(
        lax.all_gather(arrived_grad, "section", axis=1, tiled=True), down_part
    )
    gate_saved = gate_stash[0].astype(jnp.float32)
    up_saved = up_stash[0].astype(jnp.float32)
    sigmoid_gate = jax.nn.sigmoid(gate_saved)
    grad_gate = (
        grad_hidden * up_saved * sigmoid_gate * (1.0 + gate_saved * (1.0 - sigmoid_gate))
    ).astype(jnp.bfloat16)
    grad_up = (grad_hidden * gate_saved * sigmoid_gate).astype(jnp.bfloat16)
    gate_part = gate_weights
    up_part = up_weights
    summed_grad = lax.psum_scatter(
        (contract_first(gate_part, grad_gate) + contract_first(up_part, grad_up)).astype(
            jnp.bfloat16
        ),
        "section",
        scatter_dimension=0,
        tiled=True,
    )
    expert_grad = summed_grad.reshape(feature_cols, expert_count, capacity)
    returned_grad = lax.all_to_all(
        expert_grad, "expert", split_axis=1, concat_axis=1, tiled=True
    ).reshape(feature_cols, slot_rows)
    input_grad = combine_rows(backward_select, returned_grad).astype(jnp.bfloat16)
    return (forward_output, input_grad)


def solution(mesh):
    in_specs = (
        P("expert", "section"),
        P("expert", None),
        P("expert", None),
        P("expert", "section"),
        P("expert", None),
        P("expert", None),
        P("expert", None, "section"),
        P("expert", None, "section"),
        P("expert", "section", None),
        P("expert", "section", None),
        P("expert", "section", None),
    )
    out_specs = (P("expert", "section"), P("expert", "section"))
    return jax.shard_map(shards, mesh=mesh, in_specs=in_specs, out_specs=out_specs, check_vma=False)
```

profile of v0, /device:TPU:0, one launch (start us, length us, event | category | flops | bytes accessed | tf_op | source)
XLA Modules:
  0.0 145.0 jit_solution(15437782882217925766)
XLA Ops:
  7.2 0.0 copy-start
  7.2 0.0 copy-start.2
  7.2 0.8 convert_reduce_fusion.1
  8.0 1.0 select_reduce_fusion.1
  9.0 0.7 multiply_add_fusion
  9.7 0.8 select_reduce_fusion
  10.5 0.0 copy-done
  10.5 1.3 fusion.33
  11.8 7.4 %all-to-all-start.2 = ((bf16[16,8,1792]{2,1,0:T(8,128)(2,1)}), bf16[16,8,1792]{2,1,0:T(8,128)(2,1)S(1)}, u32[]{:S(2)}, u32[]{:S(2)}) async-start(bf16[16,8,1792]{2,1,0:T(8,128)(2,1)} %fusion.33), calls=%async_computation.3 | async-start | bytes 917504 | tf_op jit(solution)/shard_map/all_to_all | solution.py:109
  19.2 0.8 convert_reduce_fusion.3
  20.0 1.0 select_reduce_fusion.3
  21.0 0.7 multiply_add_fusion.1
  21.7 0.8 convert_reduce_fusion.2
  22.5 1.9 %fusion.34 = bf16[16,8,1792]{2,1,0:T(8,128)(2,1)} fusion(bf16[8,1792]{1,0:T(8,128)(2,1)} %param.11, bf16[8,128]{1,0:T(8,128)(2,1)S(1)} %get-tuple-element.4), kind=kOutput, calls=%fused_computation.22 | convolution fusion | flops 3899392 | bytes 489472 | tf_op jit(solution)/shard_map/dot_general | solution.py:74
  24.3 8.1 %all-to-all-done.2 = bf16[16,8,1792]{2,1,0:T(8,128)(2,1)S(1)} async-done(((bf16[16,8,1792]{2,1,0:T(8,128)(2,1)}), bf16[16,8,1792]{2,1,0:T(8,128)(2,1)S(1)}, u32[]{:S(2)}, u32[]{:S(2)}) %all-to-all-start.2) | async-done | bytes 458784 | tf_op jit(solution)/shard_map/all_to_all | solution.py:109
  32.5 3.9 %all-to-all-start = ((bf16[16,8,1792]{2,1,0:T(8,128)(2,1)}), bf16[16,8,1792]{2,1,0:T(8,128)(2,1)S(1)}, u32[]{:S(2)}, u32[]{:S(2)}) async-start(bf16[16,8,1792]{2,1,0:T(8,128)(2,1)} %fusion.34), calls=%async_computation | async-start | bytes 917504 | tf_op jit(solution)/shard_map/all_to_all | solution.py:77
  36.4 0.0 reduce-scatter.5.cloned.1.call-start
  36.4 0.0 copy-start.1
  36.4 13.7 %all_gather.7 = bf16[128,3584]{1,0:T(8,128)(2,1)S(1)} all-gather(bf16[128,1792]{1,0:T(8,128)(2,1)S(1)} %bitcast.76), channel_id=1, replica_groups=mesh['section'=2,'expert'=16] {'section'}, dimensions={1}, use_global_device_ids=true | all-gather | bytes 1376256 | tf_op jit(solution)/shard_map/all_gather | solution.py:119
  50.1 0.0 slice-start
  50.1 0.0 slice-start.1
  50.1 6.7 %fusion = f32[128,1280]{1,0:T(8,128)S(1)} fusion(bf16[128,3584]{1,0:T(8,128)(2,1)S(1)} %all_gather.7, bf16[1,1280,3584]{2,1,0:T(8,128)(2,1)} %param.21), kind=kOutput, calls=%fused_computation | convolution fusion | flops 1174405120 | bytes 10747904 | tf_op jit(solution)/shard_map/dot_general | solution.py:25
  56.8 0.0 copy-done.2
  56.8 0.0 copy-done.1
  56.8 0.0 slice-start.2
  56.9 0.0 copy-start.3
  56.9 1.4 fusion.4
  58.3 0.0 slice-done
  58.3 0.0 slice-done.1
  58.3 0.0 slice-done.2
  58.3 0.0 copy-done.3
  58.4 2.5 %fusion.24 = bf16[3584,128]{0,1:T(8,128)(2,1)} fusion(f32[128,3584]{1,0:T(8,128)S(1)} %fusion.4, bf16[1,1280,3584]{2,1,0:T(8,128)(2,1)S(1)} %bitcast.75, f32[128,1280]{1,0:T(8,128)S(1)} %fusion, bf16[1,128,1280]{2,1,0:T(8,128)(2,1)S(1)} %copy-done.3, bf16[1,128,1280]{2,1,0:T(8,128)(2,1)S(1)} %copy-done.2), kind=kOutput, calls=%fused_computation.16 | convolution fusion | flops 1177288704 | bytes 13238272 | tf_op jit(solution)/shard_map/dot_general | solution.py:31
  60.8 0.0 reduce-scatter.5.cloned.1.call-update
  60.9 0.0 reduce-scatter.3.cloned.1.call-start
  60.9 0.0 all-to-all-done
  60.9 17.9 %all_gather.6 = bf16[128,3584]{1,0:T(8,128)(2,1)S(1)} all-gather(bf16[128,1792]{1,0:T(8,128)(2,1)S(1)} %bitcast.77), channel_id=1, replica_groups=mesh['section'=2,'expert'=16] {'section'}, dimensions={1}, use_global_device_ids=true | all-gather | bytes 1376256 | tf_op jit(solution)/shard_map/all_gather | solution.py:85
  78.8 6.6 %fusion.10 = f32[128,1280]{1,0:T(8,128)S(1)} fusion(bf16[128,3584]{1,0:T(8,128)(2,1)S(1)} %all_gather.6, bf16[1,1280,3584]{2,1,0:T(8,128)(2,1)} %param.19), kind=kOutput, calls=%fused_computation.10 | convolution fusion | flops 1174405120 | bytes 10747904 | tf_op jit(solution)/shard_map/dot_general | solution.py:25
  85.4 12.3 %fusion.21 = bf16[3584,128]{0,1:T(8,128)(2,1)} fusion(bf16[1,1280,3584]{2,1,0:T(8,128)(2,1)} %param.21, bf16[128,3584]{1,0:T(8,128)(2,1)S(1)} %all_gather.6, bf16[1,1280,3584]{2,1,0:T(8,128)(2,1)} %param.20, f32[128,1280]{1,0:T(8,128)S(1)} %fusion.10), kind=kOutput, calls=%fused_computation.15 | convolution fusion | flops 2350252032 | bytes 20840448 | tf_op jit(solution)/shard_map/dot_general | solution.py:31
  97.7 0.0 reduce-scatter.3.cloned.1.call-update
  97.8 0.0 reduce-scatter.5.cloned.1.call-done
  97.8 5.3 %all-to-all-start.3 = ((bf16[1792,16,8]{0,2,1:T(8,128)(2,1)}), bf16[1792,16,8]{0,2,1:T(8,128)(2,1)S(1)}, u32[]{:S(2)}, u32[]{:S(2)}) async-start(bf16[1792,16,8]{0,2,1:T(8,128)(2,1)} %bitcast.78), calls=%async_computation.5 | async-start | bytes 917504 | tf_op jit(solution)/shard_map/all_to_all | solution.py:139
  103.1 15.3 %reduce-scatter.3.cloned.1.call-done = bf16[1792,128]{0,1:T(8,128)(2,1)} async-done(((bf16[3584,128]{0,1:T(8,128)(2,1)}), bf16[1792,128]{0,1:T(8,128)(2,1)}) %reduce-scatter.3.cloned.1.call-update) | async-done | bytes 458768 | tf_op jit(solution)/shard_map/reduce_scatter | solution.py:92
  118.4 0.0 all-to-all-done.3
  118.4 5.6 %all-to-all-start.1 = ((bf16[1792,16,8]{0,2,1:T(8,128)(2,1)}), bf16[1792,16,8]{0,2,1:T(8,128)(2,1)S(1)}, u32[]{:S(2)}, u32[]{:S(2)}) async-start(bf16[1792,16,8]{0,2,1:T(8,128)(2,1)} %bitcast.79), calls=%async_computation.2 | async-start | bytes 917504 | tf_op jit(solution)/shard_map/all_to_all | solution.py:99
  124.0 0.9 convolution_convert_fusion.2
  124.9 12.3 %all-to-all-done.1 = bf16[1792,16,8]{0,2,1:T(8,128)(2,1)S(1)} async-done(((bf16[1792,16,8]{0,2,1:T(8,128)(2,1)}), bf16[1792,16,8]{0,2,1:T(8,128)(2,1)S(1)}, u32[]{:S(2)}, u32[]{:S(2)}) %all-to-all-start.1) | async-done | bytes 458784 | tf_op jit(solution)/shard_map/all_to_all | solution.py:99
  137.3 0.9 convolution_convert_fusion.3
  (5 shorter events, 0.1 us)
Async XLA Ops:
  7.2 3.3 %copy-start = (bf16[8,1792]{1,0:T(8,128)(2,1)S(1)}, bf16[8,1792]{1,0:T(8,128)(2,1)}, u32[]{:S(2)}) copy-start(bf16[8,1792]{1,0:T(8,128)(2,1)} %param.14) | copy-start | bytes 86020
  7.2 49.6 %copy-start.2 = (bf16[1,128,1280]{2,1,0:T(8,128)(2,1)S(1)}, bf16[1,128,1280]{2,1,0:T(8,128)(2,1)}, u32[]{:S(2)}) copy-start(bf16[1,128,1280]{2,1,0:T(8,128)(2,1)} %param.17) | copy-start | bytes 983044
  11.8 20.6 %all-to-all-start.2 = ((bf16[16,8,1792]{2,1,0:T(8,128)(2,1)}), bf16[16,8,1792]{2,1,0:T(8,128)(2,1)S(1)}, u32[]{:S(2)}, u32[]{:S(2)}) async-start(bf16[16,8,1792]{2,1,0:T(8,128)(2,1)} %fusion.33), calls=%async_computation.3 | async-start | bytes 917504 | tf_op jit(solution)/shard_map/all_to_all | solution.py:109
  32.5 28.5 %all-to-all-start = ((bf16[16,8,1792]{2,1,0:T(8,128)(2,1)}), bf16[16,8,1792]{2,1,0:T(8,128)(2,1)S(1)}, u32[]{:S(2)}, u32[]{:S(2)}) async-start(bf16[16,8,1792]{2,1,0:T(8,128)(2,1)} %fusion.34), calls=%async_computation | async-start | bytes 917504 | tf_op jit(solution)/shard_map/all_to_all | solution.py:77
  36.4 61.4 %reduce-scatter.5.cloned.1.call-start = ((), (), s32[]{:S(2)}) async-start(), calls=%async_computation.7 | async-start | bytes 1376256 | tf_op jit(solution)/shard_map/reduce_scatter | solution.py:130
  36.4 20.4 %copy-start.1 = (bf16[1,1280,3584]{2,1,0:T(8,128)(2,1)S(1)}, bf16[1,1280,3584]{2,1,0:T(8,128)(2,1)}, u32[]{:S(2)}) copy-start(bf16[1,1280,3584]{2,1,0:T(8,128)(2,1)} %param.20) | copy-start | bytes 27525124
  50.1 8.2 %slice-start = ((s8[9175040]{0:T(1024)(128)(4,1)}), s8[4194304]{0:T(1024)(128)(4,1)S(1)}, s32[]{:S(2)}) async-start(s8[9175040]{0:T(1024)(128)(4,1)} %bitcast.74), calls=%async_computation.8 | async-start | bytes 8388608
  50.1 8.2 %slice-start.1 = ((s8[9175040]{0:T(1024)(128)(4,1)}), s8[4194304]{0:T(1024)(128)(4,1)S(1)}, s32[]{:S(2)}) async-start(s8[9175040]{0:T(1024)(128)(4,1)} %bitcast.74), calls=%async_computation.9 | async-start | bytes 8388608
  56.8 1.5 %slice-start.2 = ((s8[9175040]{0:T(1024)(128)(4,1)}), s8[786432]{0:T(1024)(128)(4,1)S(1)}, s32[]{:S(2)}) async-start(s8[9175040]{0:T(1024)(128)(4,1)} %bitcast.74), calls=%async_computation.10 | async-start | bytes 1572864
  56.9 1.5 %copy-start.3 = (bf16[1,128,1280]{2,1,0:T(8,128)(2,1)S(1)}, bf16[1,128,1280]{2,1,0:T(8,128)(2,1)}, u32[]{:S(2)}) copy-start(bf16[1,128,1280]{2,1,0:T(8,128)(2,1)} %param.18) | copy-start | bytes 983044
  60.9 57.5 %reduce-scatter.3.cloned.1.call-start = ((), (), s32[]{:S(2)}) async-start(), calls=%async_computation.6 | async-start | bytes 1376256 | tf_op jit(solution)/shard_map/reduce_scatter | solution.py:92
  97.8 20.6 %all-to-all-start.3 = ((bf16[1792,16,8]{0,2,1:T(8,128)(2,1)}), bf16[1792,16,8]{0,2,1:T(8,128)(2,1)S(1)}, u32[]{:S(2)}, u32[]{:S(2)}) async-start(bf16[1792,16,8]{0,2,1:T(8,128)(2,1)} %bitcast.78), calls=%async_computation.5 | async-start | bytes 917504 | tf_op jit(solution)/shard_map/all_to_all | solution.py:139
  118.4 18.9 %all-to-all-start.1 = ((bf16[1792,16,8]{0,2,1:T(8,128)(2,1)}), bf16[1792,16,8]{0,2,1:T(8,128)(2,1)S(1)}, u32[]{:S(2)}, u32[]{:S(2)}) async-start(bf16[1792,16,8]{0,2,1:T(8,128)(2,1)} %bitcast.79), calls=%async_computation.2 | async-start | bytes 917504 | tf_op jit(solution)/shard_map/all_to_all | solution.py:99
Sparse Core Ops, SparseCore 0:
  61.0 23.5 reduce-scatter.4
  97.9 20.4 reduce-scatter.2
where the time goes:
time: 146 us; the launch traced here: 145 us
  waiting for transfers between devices  35.8 us (25%)
  matrix products  34.6 us (24%)
  blocking collectives  31.5 us (22%)
  starting transfers between devices  22.2 us (15%)
  between operations  14.3 us (10%)
  other arithmetic  6.52 us (4%)
    all_gather x1, blocking collectives, shards(): portion = lax.all_gather(arrived, 'section', axis=1, tiled=True)  17.9 us
    dot_general x3, matrix products, contract_first(): lax.dot_general(first_operand, second_operand, (((0,), (1,)), ((), ())),...  16.2 us
    reduce_scatter x1, waiting for transfers between devices, shards(): lax.psum_scatter(contract_first(down_part, hidden).astype(jnp.bfloat16),...  15.3 us
    all_gather x1, blocking collectives, shards(): lax.all_gather(arrived_grad, 'section', axis=1, tiled=True)  13.7 us
    dot_general x2, matrix products, contract_last(): lax.dot_general(first_operand, second_operand, (((1,), (1,)), ((), ())),...  13.3 us
    all_to_all x1, waiting for transfers between devices, shards(): lax.all_to_all(expert_output, 'expert', split_axis=1, concat_axis=1, tile...  12.3 us
    all_to_all x1, waiting for transfers between devices, shards(): lax.all_to_all(sent_grad.reshape(expert_count, capacity, feature_cols), '...  8.14 us
    all_to_all x1, starting transfers between devices, shards(): lax.all_to_all(sent_grad.reshape(expert_count, capacity, feature_cols), '...  7.36 us
  transfers between devices with their start and end apart: 6, of which 3 were waited for; matrix products, arithmetic and copies ran while one was open for 25% of the time, Pallas kernels for 0%

commit v1 on v0

v1 whole, which is shorter than its diff:
```python
import functools

import jax
import jax.numpy as jnp
from jax import lax
from jax.experimental import pallas as pl
from jax.experimental.pallas import tpu as pltpu
from jax.sharding import PartitionSpec as P

LANES = 128
AXES = ("section", "expert")
VMEM = pltpu.MemorySpace.VMEM


def last_last(a, b):
    return lax.dot_general(a, b, (((1,), (1,)), ((), ())), preferred_element_type=jnp.float32)


def last_first(a, b):
    return lax.dot_general(a, b, (((1,), (0,)), ((), ())), preferred_element_type=jnp.float32)


def pack_kernel(expert_count, xf, rf, wf, xb, rb, wb, of, ob):
    tokens, topk = rf.shape
    cols = xf.shape[1]
    lane = lax.broadcasted_iota(jnp.int32, (tokens, LANES), 1)
    row = lax.broadcasted_iota(jnp.int32, (tokens, LANES), 0)
    expert, field = lane % expert_count, lane // expert_count
    for x, r, w, o in ((xf, rf, wf, of), (xb, rb, wb, ob)):
        weight = jnp.zeros((tokens, LANES), jnp.float32)
        named = jnp.zeros((tokens, LANES), jnp.float32)
        for k in range(topk):
            hit = expert == r[:, k : k + 1]
            weight = jnp.where(hit, w[:, k : k + 1], weight)
            named = jnp.where(hit, 1.0, named)
        earlier = jnp.zeros((tokens, LANES), jnp.float32)
        for t in range(tokens - 1):
            earlier = earlier + jnp.where(row > t, named[t : t + 1, :], 0.0)
        high = weight.astype(jnp.bfloat16).astype(jnp.float32)
        low = weight - high
        extra = jnp.where(field == 0, high, jnp.where(field == 1, low, jnp.where(field == 2, earlier, 0.0)))
        o[:, :cols] = x[...]
        o[:, cols:] = extra.astype(jnp.bfloat16)


def pack(expert_count, xf, rf, wf, xb, rb, wb):
    shape = jax.ShapeDtypeStruct((xf.shape[0], xf.shape[1] + LANES), jnp.bfloat16)
    return pl.pallas_call(
        functools.partial(pack_kernel, expert_count), out_shape=(shape, shape), name="pack"
    )(xf, rf, wf, xb, rb, wb)


def chunks(total, size):
    return [(at, min(size, total - at)) for at in range(0, total, size)]


def section_start(j, width, sections):
    if sections == 1:
        return 0
    return pl.multiple_of((lax.axis_index("section") ^ j) * width, LANES)


def field_of(meta, index):
    lane = lax.broadcasted_iota(jnp.int32, meta.shape, 1)
    return jnp.sum(jnp.where(lane == index, meta, 0.0), axis=1, keepdims=True)


def load_rows(groups, sections, width, pieces, rows, held):
    at, metas = 0, []
    for g in range(groups):
        count = pieces[g * sections].shape[0]
        for j in range(sections):
            start = section_start(j, width, sections)
            held[at : at + count, pl.ds(start, width)] = pieces[g * sections + j][:, :width]
        metas.append(pieces[g * sections][:, width:].astype(jnp.float32))
        at += count
    return metas[0] if groups == 1 else jnp.concatenate(metas, axis=0)


def store_rows(groups, sections, width, outs, product):
    for j in range(sections):
        start = section_start(j, width, sections)
        for at, size in chunks(width, 256):
            y = product(start + at, size).astype(jnp.bfloat16)
            row = 0
            for g in range(groups):
                out = outs[g * sections + j]
                out[:, at : at + size] = y[row : row + out.shape[0], :]
                row += out.shape[0]


def forward_kernel(groups, sections, width, experts, *refs):
    n = groups * sections
    pieces, (gate, up, down), outs, (held, hidden) = refs[:n], refs[n : n + 3], refs[n + 3 : 2 * n + 3], refs[2 * n + 3 :]
    meta = load_rows(groups, sections, width, pieces, None, held)
    me = lax.axis_index("expert")
    weight = field_of(meta, me) + field_of(meta, me + experts)
    for at, size in chunks(hidden.shape[1], 256):
        g = last_last(held[...], gate[at : at + size, :])
        u = last_last(held[...], up[at : at + size, :])
        hidden[:, at : at + size] = (g / (1.0 + jnp.exp(-g)) * u).astype(jnp.bfloat16)
    store_rows(
        groups, sections, width, outs,
        lambda start, size: last_first(hidden[...], down[:, pl.ds(start, size)]) * weight,
    )


def backward_kernel(groups, sections, width, experts, capacity, *refs):
    n = groups * sections
    pieces, (block, gate_saved, up_saved, gate, up, down) = refs[:n], refs[n : n + 6]
    outs, (held, grad_gate, grad_up) = refs[n + 6 : 2 * n + 6], refs[2 * n + 6 :]
    meta = load_rows(groups, sections, width, pieces, None, held)
    me = lax.axis_index("expert")
    weight = field_of(meta, me) + field_of(meta, me + experts)
    slot = block[...] * capacity + field_of(meta, me + 2 * experts).astype(jnp.int32)
    slot = jnp.where(weight > 0.0, slot, -1)
    place = lax.broadcasted_iota(jnp.int32, (held.shape[0], gate_saved.shape[0]), 1)
    pick = jnp.where(place == slot, 1.0, 0.0).astype(jnp.bfloat16)
    for at, size in chunks(grad_gate.shape[1], 256):
        part = slice(at, at + size)
        grad = last_last(held[...], down[part, :]) * weight
        g = last_first(pick, gate_saved[:, part])
        u = last_first(pick, up_saved[:, part])
        q = 1.0 / (1.0 + jnp.exp(-g))
        grad_gate[:, part] = (grad * u * q * (1.0 + g * (1.0 - q))).astype(jnp.bfloat16)
        grad_up[:, part] = (grad * g * q).astype(jnp.bfloat16)
    store_rows(
        groups, sections, width, outs,
        lambda start, size: last_first(grad_gate[...], gate[:, pl.ds(start, size)])
        + last_first(grad_up[...], up[:, pl.ds(start, size)]),
    )


def expert_call(kernel, name, pieces, sections, width, extra, weights, scratch):
    outs = tuple(jax.ShapeDtypeStruct((p.shape[0], width), jnp.bfloat16) for p in pieces)
    weights = [pltpu.with_memory_space_constraint(w, VMEM) for w in weights]
    return pl.pallas_call(
        kernel,
        out_shape=outs,
        scratch_shapes=scratch,
        compiler_params=pltpu.CompilerParams(vmem_limit_bytes=24 << 20),
        name=name,
    )(*pieces, *extra, *weights)


def experts_forward(pieces, sections, width, experts, weights):
    rows = sum(p.shape[0] for p in pieces) // sections
    units, features = weights[0].shape
    return expert_call(
        functools.partial(forward_kernel, len(pieces) // sections, sections, width, experts),
        "experts_forward", pieces, sections, width, [], weights,
        [pltpu.VMEM((rows, features), jnp.bfloat16), pltpu.VMEM((rows, units), jnp.bfloat16)],
    )


def experts_backward(pieces, sections, width, experts, capacity, block, stash, weights):
    rows = sum(p.shape[0] for p in pieces) // sections
    units, features = weights[0].shape
    return expert_call(
        functools.partial(backward_kernel, len(pieces) // sections, sections, width, experts, capacity),
        "experts_backward", pieces, sections, width, [block, *stash], weights,
        [pltpu.VMEM((rows, features), jnp.bfloat16)] + [pltpu.VMEM((rows, units), jnp.bfloat16)] * 2,
    )


def move(value, mask, devices):
    return lax.ppermute(value, AXES, [(i, i ^ mask) for i in range(devices)])


Z = (8, 4, 12)
X, Y, CORE = 2, 16, 1


def spread(message):
    tokens, cols = message.shape
    held = message[None]
    for mask in Z[:2]:
        held = jnp.concatenate([held, move(held, mask, 32)], axis=0)
    held = held.reshape(4 * tokens, cols)
    own = [held, move(held, Y, 32), move(held, X, 32), move(held, X ^ Y, 32)]
    return own + [move(p, CORE, 32) for p in own]


def collect(pieces, tokens):
    other = [move(p, CORE, 32) for p in pieces[4:]]
    own = [
        (a.astype(jnp.float32) + b.astype(jnp.float32)).astype(jnp.bfloat16) for a, b in zip(pieces[:4], other)
    ]
    parts = [own[0], move(own[1], Y, 32), move(own[2], X, 32), move(own[3], X ^ Y, 32)]
    total = sum(p.astype(jnp.float32) for p in parts).astype(jnp.bfloat16)
    rows = [total[k * tokens : (k + 1) * tokens] for k in range(4)]
    parts = [rows[0]] + [move(rows[k + 1], Z[k], 32) for k in range(3)]
    return sum(p.astype(jnp.float32) for p in parts).astype(jnp.bfloat16)


def spread_any(message, width):
    held = lax.all_gather(message, "expert", axis=0, tiled=True)
    whole = lax.all_gather(held[:, :width], "section", axis=1, tiled=True)
    return [jnp.concatenate([whole, held[:, width:]], axis=1)]


def collect_any(pieces):
    summed = lax.psum_scatter(pieces[0], "section", scatter_dimension=1, tiled=True)
    return lax.psum_scatter(summed, "expert", scatter_dimension=0, tiled=True)


def shards(
    forward_input, forward_route, forward_weight, output_grad, backward_route, backward_weight,
    gate_stash, up_stash, gate_matrix, up_matrix, down_matrix,
):
    expert_count, section_count = lax.axis_size("expert"), lax.axis_size("section")
    tokens, width = forward_input.shape
    capacity = gate_stash.shape[1] // expert_count
    weights = (gate_matrix[0], up_matrix[0], down_matrix[0])
    stash = (gate_stash[0], up_stash[0])
    message_f, message_b = pack(
        expert_count, forward_input, forward_route, forward_weight, output_grad, backward_route, backward_weight
    )
    if (section_count, expert_count) == (2, 16):
        sections = 2
        mask = jnp.array([c ^ x ^ z for c in (0, CORE) for x in (0, X) for z in (0, 8, 4, 12)], jnp.int32)
        order = lax.axis_index("expert") ^ mask
        pieces_f, pieces_b = spread(message_f), spread(message_b)
        gather = functools.partial(collect, tokens=tokens)
    else:
        sections = 1
        order = jnp.arange(expert_count, dtype=jnp.int32)
        pieces_f, pieces_b = spread_any(message_f, width), spread_any(message_b, width)
        width, gather = width * section_count, collect_any
    block = jnp.repeat(order, tokens)[:, None]
    done_f = experts_forward(pieces_f, sections, width, expert_count, weights)
    done_b = experts_backward(pieces_b, sections, width, expert_count, capacity, block, stash, weights)
    return gather(list(done_f)), gather(list(done_b))


def solution(mesh):
    split, rows, stash, matrix = (
        P("expert", "section"), P("expert", None), P("expert", None, "section"), P("expert", "section", None)
    )
    in_specs = (split, rows, rows, split, rows, rows, stash, stash, matrix, matrix, matrix)
    return jax.shard_map(shards, mesh=mesh, in_specs=in_specs, out_specs=(split, split), check_vma=False)
```

time: 146 us -> 93.2 us (0.64)
  matrix products: 34.6 us -> 0 us
  blocking collectives: 31.5 us -> 0 us
  waiting for transfers between devices: 35.8 us -> 13.9 us
  local copies, waits for them, and re-layouts: 0.04 us -> 21.8 us
  Pallas kernels: 0 us -> 15.1 us
  between operations: 14.3 us -> 0.83 us
  starting transfers between devices: 22.2 us -> 35.2 us
    ppermute x0 -> x38, starting transfers between devices: none -> 35.2 us  [move(): return lax.ppermute(value, AXES, [(i, i ^ mask) for i in range(devices)])]
    dot_general x9 -> x0, matrix products: 34.6 us -> none  [the longest x3 16.2 us: contract_first(): lax.dot_general(first_operand, second_operand, (((0,), (1,)), ((), ())),...]
    all_gather x2 -> x0, blocking collectives: 31.5 us -> none  [the longest x1 17.9 us: shards(): portion = lax.all_gather(arrived, 'section', axis=1, tiled=True)]
    all_to_all x4 -> x0, starting transfers between devices: 22.2 us -> none  [the longest x1 7.36 us: shards(): lax.all_to_all(sent_grad.reshape(expert_count, capacity, feature_cols), '...]
    unnamed x14 -> x18, local copies, waits for them, and re-layouts: 0.04 us -> 21.6 us
    all_to_all x4 -> x0, waiting for transfers between devices: 20.5 us -> none  [the longest x1 12.3 us: shards(): lax.all_to_all(expert_output, 'expert', split_axis=1, concat_axis=1, tile...]
    reduce_scatter x2 -> x0, waiting for transfers between devices: 15.3 us -> none  [the longest x1 15.3 us: shards(): lax.psum_scatter(contract_first(down_part, hidden).astype(jnp.bfloat16),...]
    pallas_call x0 -> x3, Pallas kernels: none -> 15.1 us  [the longest x2 13.6 us: expert_call(): pl.pallas_call(kernel, out_shape=outs, scratch_shapes=scratch, compiler_p...]
  transfers between devices with their start and end apart: 6 -> 38, of which waited for: 3 -> 12; matrix products, arithmetic and copies ran while one was open for 25% -> 6% of each run, Pallas kernels for 0% -> 15%
where the time goes in v1:
time: 93.2 us; the launch traced here: 92.5 us
  starting transfers between devices  35.2 us (38%)
  local copies, waits for them, and re-layouts  21.8 us (23%)
  Pallas kernels  15.1 us (16%)
  waiting for transfers between devices  13.9 us (15%)
  other arithmetic  5.56 us (6%)
    ppermute x38, starting transfers between devices, move(): return lax.ppermute(value, AXES, [(i, i ^ mask) for i in range(devices)])  35.2 us
    unnamed x18, local copies, waits for them, and re-layouts  21.6 us
    ppermute x38, waiting for transfers between devices, move(): return lax.ppermute(value, AXES, [(i, i ^ mask) for i in range(devices)])  13.9 us
    pallas_call x2, Pallas kernels, expert_call(): pl.pallas_call(kernel, out_shape=outs, scratch_shapes=scratch, compiler_p...  13.6 us
  transfers between devices with their start and end apart: 38, of which 12 were waited for; matrix products, arithmetic and copies ran while one was open for 6% of the time, Pallas kernels for 15%

profile of v1, /device:TPU:0, one launch (start us, length us, event | category | flops | bytes accessed | tf_op | source)
XLA Modules:
  0.0 92.5 jit_solution(15530528979364915628)
XLA Ops:
  0.6 1.5 %pack.1 = (bf16[8,1920]{1,0:T(8,128)(2,1)}, bf16[8,1920]{1,0:T(8,128)(2,1)}) custom-call(bf16[8,1792]{1,0:T(8,128)(2,1)} %xf.1, s32[8,8]{1,0:T(8,128)} %rf.1, f32[8,8]{1,0:T(8,128)} %wf.1, bf16[8,1792]{1,0:T(8,128)(2,1)} %xb.1, s32[8,8]{1,0:T(8,128)} %rb.1, f32[8,8]{1,0:T(8,128)} %wb.1), custom_call_target="tpu_custom_call" | custom-call | tf_op jit(solution)/shard_map/pack/pallas_call | solution.py:48
  2.2 4.0 %collective-permute-start = (bf16[1,8,1920]{2,1,0:T(8,128)(2,1)}, bf16[1,8,1920]{2,1,0:T(8,128)(2,1)S(1)}, u32[]{:S(2)}, u32[]{:S(2)}) collective-permute-start(bf16[1,8,1920]{2,1,0:T(8,128)(2,1)} %bitcast.22), channel_id=1, source_target_pairs={{0,8},{1,9},{2,10},{3,11},{4,12},{5,13},{6,14},{7,15},{8,0},{9,1},... | collective-permute-start | bytes 92168 | tf_op jit(solution)/shard_map/ppermute | solution.py:167
  6.2 0.0 collective-permute-start.19
  6.2 2.4 %collective-permute-done = bf16[1,8,1920]{2,1,0:T(8,128)(2,1)S(1)} collective-permute-done((bf16[1,8,1920]{2,1,0:T(8,128)(2,1)}, bf16[1,8,1920]{2,1,0:T(8,128)(2,1)S(1)}, u32[]{:S(2)}, u32[]{:S(2)}) %collective-permute-start) | collective-permute-done | bytes 30752 | tf_op jit(solution)/shard_map/ppermute | solution.py:167
  8.6 0.8 pad_maximum_fusion
  9.4 1.7 %collective-permute-start.1 = (bf16[2,8,1920]{2,1,0:T(8,128)(2,1)S(1)}, bf16[2,8,1920]{2,1,0:T(8,128)(2,1)S(1)}, u32[]{:S(2)}, u32[]{:S(2)}) collective-permute-start(bf16[2,8,1920]{2,1,0:T(8,128)(2,1)S(1)} %pad_maximum_fusion), channel_id=1, source_target_pairs={{0,4},{1,5},{2,6},{3,7},{4,0},{5,1},{6,2},{7,3},{8,12},{9,13},{10,... | collective-permute-start | bytes 184328 | tf_op jit(solution)/shard_map/ppermute | solution.py:167
  11.0 0.3 collective-permute-done.19
  11.3 0.8 pad_maximum_fusion.1
  12.1 1.5 %collective-permute-start.20 = (bf16[2,8,1920]{2,1,0:T(8,128)(2,1)S(1)}, bf16[2,8,1920]{2,1,0:T(8,128)(2,1)S(1)}, u32[]{:S(2)}, u32[]{:S(2)}) collective-permute-start(bf16[2,8,1920]{2,1,0:T(8,128)(2,1)S(1)} %pad_maximum_fusion.1), channel_id=1, source_target_pairs={{0,4},{1,5},{2,6},{3,7},{4,0},{5,1},{6,2},{7,3},{8,12},{9,13},{10,... | collective-permute-start | bytes 184328 | tf_op jit(solution)/shard_map/ppermute | solution.py:167
  13.6 0.5 collective-permute-done.1
  14.1 0.8 maximum_bitcast_fusion.refs_0_
  14.9 2.0 %collective-permute-start.2 = (bf16[32,1920]{1,0:T(8,128)(2,1)S(1)}, bf16[32,1920]{1,0:T(8,128)(2,1)S(1)}, u32[]{:S(2)}, u32[]{:S(2)}) collective-permute-start(bf16[32,1920]{1,0:T(8,128)(2,1)S(1)} %maximum_bitcast_fusion.refs_0_), channel_id=1, source_target_pairs={{0,16},{1,17},{2,18},{3,19},{4,20},{5,21},{6,22},{7,23},{8,24},{9,... | collective-permute-start | bytes 368648 | tf_op jit(solution)/shard_map/ppermute | solution.py:167
  16.9 1.5 %collective-permute-start.3 = (bf16[32,1920]{1,0:T(8,128)(2,1)S(1)}, bf16[32,1920]{1,0:T(8,128)(2,1)S(1)}, u32[]{:S(2)}, u32[]{:S(2)}) collective-permute-start(bf16[32,1920]{1,0:T(8,128)(2,1)S(1)} %maximum_bitcast_fusion.refs_0_), channel_id=1, source_target_pairs={{0,2},{1,3},{2,0},{3,1},{4,6},{5,7},{6,4},{7,5},{8,10},{9,11},{10,... | collective-permute-start | bytes 368648 | tf_op jit(solution)/shard_map/ppermute | solution.py:167
  18.4 0.1 collective-permute-start.4
  18.5 0.8 maximum_bitcast_fusion.1.refs_0_
  19.2 2.0 %collective-permute-start.21 = (bf16[32,1920]{1,0:T(8,128)(2,1)S(1)}, bf16[32,1920]{1,0:T(8,128)(2,1)S(1)}, u32[]{:S(2)}, u32[]{:S(2)}) collective-permute-start(bf16[32,1920]{1,0:T(8,128)(2,1)S(1)} %maximum_bitcast_fusion.1.refs_0_), channel_id=1, source_target_pairs={{0,16},{1,17},{2,18},{3,19},{4,20},{5,21},{6,22},{7,23},{8,24},{9,... | collective-permute-start | bytes 368648 | tf_op jit(solution)/shard_map/ppermute | solution.py:167
  21.2 1.5 %collective-permute-start.22 = (bf16[32,1920]{1,0:T(8,128)(2,1)S(1)}, bf16[32,1920]{1,0:T(8,128)(2,1)S(1)}, u32[]{:S(2)}, u32[]{:S(2)}) collective-permute-start(bf16[32,1920]{1,0:T(8,128)(2,1)S(1)} %maximum_bitcast_fusion.1.refs_0_), channel_id=1, source_target_pairs={{0,2},{1,3},{2,0},{3,1},{4,6},{5,7},{6,4},{7,5},{8,10},{9,11},{10,... | collective-permute-start | bytes 368648 | tf_op jit(solution)/shard_map/ppermute | solution.py:167
  22.7 0.6 collective-permute-start.23
  23.3 1.2 %collective-permute-done.4.refs_3_ = bf16[32,1920]{1,0:T(8,128)(2,1)S(1)} collective-permute-done((bf16[32,1920]{1,0:T(8,128)(2,1)S(1)}, bf16[32,1920]{1,0:T(8,128)(2,1)S(1)}, u32[]{:S(2)}, u32[]{:S(2)}) %collective-permute-start.4) | collective-permute-done | bytes 122912 | tf_op jit(solution)/shard_map/ppermute | solution.py:167
  24.5 0.5 collective-permute-start.7
  25.1 1.8 %collective-permute-done.21.refs_1_ = bf16[32,1920]{1,0:T(8,128)(2,1)S(1)} collective-permute-done((bf16[32,1920]{1,0:T(8,128)(2,1)S(1)}, bf16[32,1920]{1,0:T(8,128)(2,1)S(1)}, u32[]{:S(2)}, u32[]{:S(2)}) %collective-permute-start.21) | collective-permute-done | bytes 122912 | tf_op jit(solution)/shard_map/ppermute | solution.py:167
  26.8 0.5 collective-permute-done.22.refs_2_
  27.4 2.1 %collective-permute-done.23.refs_3_ = bf16[32,1920]{1,0:T(8,128)(2,1)S(1)} collective-permute-done((bf16[32,1920]{1,0:T(8,128)(2,1)S(1)}, bf16[32,1920]{1,0:T(8,128)(2,1)S(1)}, u32[]{:S(2)}, u32[]{:S(2)}) %collective-permute-start.23) | collective-permute-done | bytes 122912 | tf_op jit(solution)/shard_map/ppermute | solution.py:167
  29.5 0.5 collective-permute-start.26
  30.0 0.1 collective-permute-start.27
  30.0 3.6 %copy-done = bf16[1,1280,3584]{2,1,0:T(8,128)(2,1)S(1)} copy-done((bf16[1,1280,3584]{2,1,0:T(8,128)(2,1)S(1)}, bf16[1,1280,3584]{2,1,0:T(8,128)(2,1)}, u32[]{:S(2)}) %copy-start) | copy-done | bytes 9175064
  33.7 3.6 %copy-done.2 = bf16[1,1280,3584]{2,1,0:T(8,128)(2,1)S(1)} copy-done((bf16[1,1280,3584]{2,1,0:T(8,128)(2,1)S(1)}, bf16[1,1280,3584]{2,1,0:T(8,128)(2,1)}, u32[]{:S(2)}) %copy-start.2) | copy-done | bytes 9175064
  37.3 3.6 %copy-done.4 = bf16[1,1280,3584]{2,1,0:T(8,128)(2,1)S(1)} copy-done((bf16[1,1280,3584]{2,1,0:T(8,128)(2,1)S(1)}, bf16[1,1280,3584]{2,1,0:T(8,128)(2,1)}, u32[]{:S(2)}) %copy-start.4) | copy-done | bytes 9175064
  40.9 7.1 %experts_forward.1 = (bf16[32,1792]{1,0:T(8,128)(2,1)S(1)}, bf16[32,1792]{1,0:T(8,128)(2,1)S(1)}, bf16[32,1792]{1,0:T(8,128)(2,1)S(1)}, bf16[32,1792]{1,0:T(8,12...) custom-call(bf16[32,1920]{1,0:T(8,128)(2,1)S(1)} %maximum_bitcast_fu, ...), custom_call_target="tpu_custom_call" | custom-call | tf_op jit(solution)/shard_map/experts_forward/pallas_call | solution.py:137
  48.0 0.5 collective-permute-start.14
  48.5 0.1 broadcast_in_dim.11
  48.5 0.1 broadcast_in_dim_reshape.4.refs_8_
  48.6 0.1 collective-permute-start.12
  48.8 0.4 collective-permute-start.10
  49.2 0.1 collective-permute-start.9
  49.3 0.0 copy-start.1
  49.3 3.6 %copy-done.1 = bf16[1,1280,3584]{2,1,0:T(8,128)(2,1)S(1)} copy-done((bf16[1,1280,3584]{2,1,0:T(8,128)(2,1)S(1)}, bf16[1,1280,3584]{2,1,0:T(8,128)(2,1)}, u32[]{:S(2)}) %copy-start.1) | copy-done | bytes 9175064
  52.9 3.6 %copy-done.3 = bf16[1,1280,3584]{2,1,0:T(8,128)(2,1)S(1)} copy-done((bf16[1,1280,3584]{2,1,0:T(8,128)(2,1)S(1)}, bf16[1,1280,3584]{2,1,0:T(8,128)(2,1)}, u32[]{:S(2)}) %copy-start.3) | copy-done | bytes 9175064
  56.5 3.6 %copy-done.5 = bf16[1,1280,3584]{2,1,0:T(8,128)(2,1)S(1)} copy-done((bf16[1,1280,3584]{2,1,0:T(8,128)(2,1)S(1)}, bf16[1,1280,3584]{2,1,0:T(8,128)(2,1)}, u32[]{:S(2)}) %copy-start.5) | copy-done | bytes 9175064
  60.1 6.5 %experts_backward.1 = (bf16[32,1792]{1,0:T(8,128)(2,1)S(1)}, bf16[32,1792]{1,0:T(8,128)(2,1)S(1)}, bf16[32,1792]{1,0:T(8,128)(2,1)S(1)}, bf16[32,1792]{1,0:T(8,1...) custom-call(bf16[32,1920]{1,0:T(8,128)(2,1)S(1)} %maximum_bitcast_fu, ...), custom_call_target="tpu_custom_call" | custom-call | tf_op jit(solution)/shard_map/experts_backward/pallas_call | solution.py:137
  66.7 0.5 collective-permute-start.33
  67.2 0.1 collective-permute-start.31
  67.3 0.9 %add_convert_fusion.6 = bf16[32,1792]{1,0:T(8,128)(2,1)S(1)} fusion(bf16[32,1792]{1,0:T(8,128)(2,1)} %collective-permute-done.14, bf16[32,1792]{1,0:T(8,128)(2,1)S(1)} %get-tuple-element.27), kind=kLoop, calls=%fused_computation.6 | loop fusion | flops 229376 | bytes 344064 | tf_op jit(solution)/shard_map/convert_element_type | solution.py:187
  68.2 0.5 collective-permute-start.29
  68.7 0.2 collective-permute-start.28
  68.9 2.3 %collective-permute-start.15 = (bf16[32,1792]{1,0:T(8,128)(2,1)S(1)}, bf16[32,1792]{1,0:T(8,128)(2,1)S(1)}, u32[]{:S(2)}, u32[]{:S(2)}) collective-permute-start(bf16[32,1792]{1,0:T(8,128)(2,1)S(1)} %add_convert_fusion.6), channel_id=1, source_target_pairs={{0,18},{1,19},{2,16},{3,17},{4,22},{5,23},{6,20},{7,21},{8,26},{9,... | collective-permute-start | bytes 344072 | tf_op jit(solution)/shard_map/ppermute | solution.py:167
  71.3 0.6 collective-permute-start.13
  71.9 0.8 collective-permute-start.11
  72.7 2.3 %collective-permute-start.34 = (bf16[32,1792]{1,0:T(8,128)(2,1)S(1)}, bf16[32,1792]{1,0:T(8,128)(2,1)S(1)}, u32[]{:S(2)}, u32[]{:S(2)}) collective-permute-start(bf16[32,1792]{1,0:T(8,128)(2,1)S(1)} %add_convert_fusion.1), channel_id=1, source_target_pairs={{0,18},{1,19},{2,16},{3,17},{4,22},{5,23},{6,20},{7,21},{8,26},{9,... | collective-permute-start | bytes 344072 | tf_op jit(solution)/shard_map/ppermute | solution.py:167
  75.0 0.8 collective-permute-done.15
  75.8 1.3 %collective-permute-start.32 = (bf16[32,1792]{1,0:T(8,128)(2,1)S(1)}, bf16[32,1792]{1,0:T(8,128)(2,1)S(1)}, u32[]{:S(2)}, u32[]{:S(2)}) collective-permute-start(bf16[32,1792]{1,0:T(8,128)(2,1)S(1)} %add_convert_fusion.2), channel_id=1, source_target_pairs={{0,2},{1,3},{2,0},{3,1},{4,6},{5,7},{6,4},{7,5},{8,10},{9,11},{10,... | collective-permute-start | bytes 344072 | tf_op jit(solution)/shard_map/ppermute | solution.py:167
  77.1 1.0 %collective-permute-done.13 = bf16[32,1792]{1,0:T(8,128)(2,1)S(1)} collective-permute-done((bf16[32,1792]{1,0:T(8,128)(2,1)S(1)}, bf16[32,1792]{1,0:T(8,128)(2,1)S(1)}, u32[]{:S(2)}, u32[]{:S(2)}) %collective-permute-start.13) | collective-permute-done | bytes 114720 | tf_op jit(solution)/shard_map/ppermute | solution.py:167
  78.1 0.7 collective-permute-start.30
  78.9 0.1 add_convert_fusion.5
  79.0 3.5 %collective-permute-start.18 = (bf16[8,1792]{1,0:T(8,128)(2,1)S(1)}, bf16[8,1792]{1,0:T(8,128)(2,1)S(1)}, u32[]{:S(2)}, u32[]{:S(2)}) collective-permute-start(bf16[8,1792]{1,0:T(8,128)(2,1)S(1)} %get-tuple-element.42), channel_id=1, source_target_pairs={{0,12},{1,13},{2,14},{3,15},{4,8},{5,9},{6,10},{7,11},{8,4},{9,5},... | collective-permute-start | bytes 86024 | tf_op jit(solution)/shard_map/ppermute | solution.py:167
  82.5 0.9 collective-permute-start.16
  83.4 0.1 add_convert_fusion
  83.5 3.5 %collective-permute-start.37 = (bf16[8,1792]{1,0:T(8,128)(2,1)S(1)}, bf16[8,1792]{1,0:T(8,128)(2,1)S(1)}, u32[]{:S(2)}, u32[]{:S(2)}) collective-permute-start(bf16[8,1792]{1,0:T(8,128)(2,1)S(1)} %get-tuple-element.39), channel_id=1, source_target_pairs={{0,12},{1,13},{2,14},{3,15},{4,8},{5,9},{6,10},{7,11},{8,4},{9,5},... | collective-permute-start | bytes 86024 | tf_op jit(solution)/shard_map/ppermute | solution.py:167
  87.1 0.9 collective-permute-start.35
  88.0 0.6 add_convert_fusion.11
  88.6 0.7 collective-permute-done.37
  89.3 1.7 %collective-permute-done.36 = bf16[8,1792]{1,0:T(8,128)(2,1)S(1)} collective-permute-done((bf16[8,1792]{1,0:T(8,128)(2,1)S(1)}, bf16[8,1792]{1,0:T(8,128)(2,1)S(1)}, u32[]{:S(2)}, u32[]{:S(2)}) %collective-permute-start.36) | collective-permute-done | bytes 28704 | tf_op jit(solution)/shard_map/ppermute | solution.py:167
  90.9 0.9 collective-permute-done.35
  91.8 0.6 add_convert_fusion.10
  (52 shorter events, 0.3 us)
Async XLA Ops:
  2.2 6.4 %collective-permute-start = (bf16[1,8,1920]{2,1,0:T(8,128)(2,1)}, bf16[1,8,1920]{2,1,0:T(8,128)(2,1)S(1)}, u32[]{:S(2)}, u32[]{:S(2)}) collective-permute-start(bf16[1,8,1920]{2,1,0:T(8,128)(2,1)} %bitcast.22), channel_id=1, source_target_pairs={{0,8},{1,9},{2,10},{3,11},{4,12},{5,13},{6,14},{7,15},{8,0},{9,1},... | collective-permute-start | bytes 92168 | tf_op jit(solution)/shard_map/ppermute | solution.py:167
  6.2 5.1 %collective-permute-start.19 = (bf16[1,8,1920]{2,1,0:T(8,128)(2,1)}, bf16[1,8,1920]{2,1,0:T(8,128)(2,1)S(1)}, u32[]{:S(2)}, u32[]{:S(2)}) collective-permute-start(bf16[1,8,1920]{2,1,0:T(8,128)(2,1)} %bitcast.19), channel_id=1, source_target_pairs={{0,8},{1,9},{2,10},{3,11},{4,12},{5,13},{6,14},{7,15},{8,0},{9,1},... | collective-permute-start | bytes 92168 | tf_op jit(solution)/shard_map/ppermute | solution.py:167
  9.4 4.7 %collective-permute-start.1 = (bf16[2,8,1920]{2,1,0:T(8,128)(2,1)S(1)}, bf16[2,8,1920]{2,1,0:T(8,128)(2,1)S(1)}, u32[]{:S(2)}, u32[]{:S(2)}) collective-permute-start(bf16[2,8,1920]{2,1,0:T(8,128)(2,1)S(1)} %pad_maximum_fusion), channel_id=1, source_target_pairs={{0,4},{1,5},{2,6},{3,7},{4,0},{5,1},{6,2},{7,3},{8,12},{9,13},{10,... | collective-permute-start | bytes 184328 | tf_op jit(solution)/shard_map/ppermute | solution.py:167
  12.1 6.4 %collective-permute-start.20 = (bf16[2,8,1920]{2,1,0:T(8,128)(2,1)S(1)}, bf16[2,8,1920]{2,1,0:T(8,128)(2,1)S(1)}, u32[]{:S(2)}, u32[]{:S(2)}) collective-permute-start(bf16[2,8,1920]{2,1,0:T(8,128)(2,1)S(1)} %pad_maximum_fusion.1), channel_id=1, source_target_pairs={{0,4},{1,5},{2,6},{3,7},{4,0},{5,1},{6,2},{7,3},{8,12},{9,13},{10,... | collective-permute-start | bytes 184328 | tf_op jit(solution)/shard_map/ppermute | solution.py:167
  14.9 6.3 %collective-permute-start.2 = (bf16[32,1920]{1,0:T(8,128)(2,1)S(1)}, bf16[32,1920]{1,0:T(8,128)(2,1)S(1)}, u32[]{:S(2)}, u32[]{:S(2)}) collective-permute-start(bf16[32,1920]{1,0:T(8,128)(2,1)S(1)} %maximum_bitcast_fusion.refs_0_), channel_id=1, source_target_pairs={{0,16},{1,17},{2,18},{3,19},{4,20},{5,21},{6,22},{7,23},{8,24},{9,... | collective-permute-start | bytes 368648 | tf_op jit(solution)/shard_map/ppermute | solution.py:167
  16.9 5.8 %collective-permute-start.3 = (bf16[32,1920]{1,0:T(8,128)(2,1)S(1)}, bf16[32,1920]{1,0:T(8,128)(2,1)S(1)}, u32[]{:S(2)}, u32[]{:S(2)}) collective-permute-start(bf16[32,1920]{1,0:T(8,128)(2,1)S(1)} %maximum_bitcast_fusion.refs_0_), channel_id=1, source_target_pairs={{0,2},{1,3},{2,0},{3,1},{4,6},{5,7},{6,4},{7,5},{8,10},{9,11},{10,... | collective-permute-start | bytes 368648 | tf_op jit(solution)/shard_map/ppermute | solution.py:167
  18.4 6.2 %collective-permute-start.4 = (bf16[32,1920]{1,0:T(8,128)(2,1)S(1)}, bf16[32,1920]{1,0:T(8,128)(2,1)S(1)}, u32[]{:S(2)}, u32[]{:S(2)}) collective-permute-start(bf16[32,1920]{1,0:T(8,128)(2,1)S(1)} %maximum_bitcast_fusion.refs_0_), channel_id=1, source_target_pairs={{0,18},{1,19},{2,16},{3,17},{4,22},{5,23},{6,20},{7,21},{8,26},{9,... | collective-permute-start | bytes 368648 | tf_op jit(solution)/shard_map/ppermute | solution.py:167
  18.4 6.1 %collective-permute-start.5 = (bf16[32,1920]{1,0:T(8,128)(2,1)S(1)}, bf16[32,1920]{1,0:T(8,128)(2,1)S(1)}, u32[]{:S(2)}, u32[]{:S(2)}) collective-permute-start(bf16[32,1920]{1,0:T(8,128)(2,1)S(1)} %maximum_bitcast_fusion.refs_0_), channel_id=1, source_target_pairs={{0,1},{1,0},{2,3},{3,2},{4,5},{5,4},{6,7},{7,6},{8,9},{9,8},{10,11... | collective-permute-start | bytes 368648 | tf_op jit(solution)/shard_map/ppermute | solution.py:167
  19.2 7.6 %collective-permute-start.21 = (bf16[32,1920]{1,0:T(8,128)(2,1)S(1)}, bf16[32,1920]{1,0:T(8,128)(2,1)S(1)}, u32[]{:S(2)}, u32[]{:S(2)}) collective-permute-start(bf16[32,1920]{1,0:T(8,128)(2,1)S(1)} %maximum_bitcast_fusion.1.refs_0_), channel_id=1, source_target_pairs={{0,16},{1,17},{2,18},{3,19},{4,20},{5,21},{6,22},{7,23},{8,24},{9,... | collective-permute-start | bytes 368648 | tf_op jit(solution)/shard_map/ppermute | solution.py:167
  21.2 6.2 %collective-permute-start.22 = (bf16[32,1920]{1,0:T(8,128)(2,1)S(1)}, bf16[32,1920]{1,0:T(8,128)(2,1)S(1)}, u32[]{:S(2)}, u32[]{:S(2)}) collective-permute-start(bf16[32,1920]{1,0:T(8,128)(2,1)S(1)} %maximum_bitcast_fusion.1.refs_0_), channel_id=1, source_target_pairs={{0,2},{1,3},{2,0},{3,1},{4,6},{5,7},{6,4},{7,5},{8,10},{9,11},{10,... | collective-permute-start | bytes 368648 | tf_op jit(solution)/shard_map/ppermute | solution.py:167
  22.7 6.7 %collective-permute-start.23 = (bf16[32,1920]{1,0:T(8,128)(2,1)S(1)}, bf16[32,1920]{1,0:T(8,128)(2,1)S(1)}, u32[]{:S(2)}, u32[]{:S(2)}) collective-permute-start(bf16[32,1920]{1,0:T(8,128)(2,1)S(1)} %maximum_bitcast_fusion.1.refs_0_), channel_id=1, source_target_pairs={{0,18},{1,19},{2,16},{3,17},{4,22},{5,23},{6,20},{7,21},{8,26},{9,... | collective-permute-start | bytes 368648 | tf_op jit(solution)/shard_map/ppermute | solution.py:167
  24.5 4.9 %collective-permute-start.6 = (bf16[32,1920]{1,0:T(8,128)(2,1)S(1)}, bf16[32,1920]{1,0:T(8,128)(2,1)S(1)}, u32[]{:S(2)}, u32[]{:S(2)}) collective-permute-start(bf16[32,1920]{1,0:T(8,128)(2,1)S(1)} %collective-permute-done.2.refs_1_), channel_id=1, source_target_pairs={{0,1},{1,0},{2,3},{3,2},{4,5},{5,4},{6,7},{7,6},{8,9},{9,8},{10,11... | collective-permute-start | bytes 368648 | tf_op jit(solution)/shard_map/ppermute | solution.py:167
  24.5 5.4 %collective-permute-start.7 = (bf16[32,1920]{1,0:T(8,128)(2,1)S(1)}, bf16[32,1920]{1,0:T(8,128)(2,1)S(1)}, u32[]{:S(2)}, u32[]{:S(2)}) collective-permute-start(bf16[32,1920]{1,0:T(8,128)(2,1)S(1)} %collective-permute-done.3.refs_2_), channel_id=1, source_target_pairs={{0,1},{1,0},{2,3},{3,2},{4,5},{5,4},{6,7},{7,6},{8,9},{9,8},{10,11... | collective-permute-start | bytes 368648 | tf_op jit(solution)/shard_map/ppermute | solution.py:167
  26.8 3.2 %collective-permute-start.8 = (bf16[32,1920]{1,0:T(8,128)(2,1)S(1)}, bf16[32,1920]{1,0:T(8,128)(2,1)S(1)}, u32[]{:S(2)}, u32[]{:S(2)}) collective-permute-start(bf16[32,1920]{1,0:T(8,128)(2,1)S(1)} %collective-permute-done.4.refs_3_), channel_id=1, source_target_pairs={{0,1},{1,0},{2,3},{3,2},{4,5},{5,4},{6,7},{7,6},{8,9},{9,8},{10,11... | collective-permute-start | bytes 368648 | tf_op jit(solution)/shard_map/ppermute | solution.py:167
  27.4 21.3 %collective-permute-start.24 = (bf16[32,1920]{1,0:T(8,128)(2,1)S(1)}, bf16[32,1920]{1,0:T(8,128)(2,1)S(1)}, u32[]{:S(2)}, u32[]{:S(2)}) collective-permute-start(bf16[32,1920]{1,0:T(8,128)(2,1)S(1)} %maximum_bitcast_fusion.1.refs_0_), channel_id=1, source_target_pairs={{0,1},{1,0},{2,3},{3,2},{4,5},{5,4},{6,7},{7,6},{8,9},{9,8},{10,11... | collective-permute-start | bytes 368648 | tf_op jit(solution)/shard_map/ppermute | solution.py:167
  29.5 19.3 %collective-permute-start.25 = (bf16[32,1920]{1,0:T(8,128)(2,1)S(1)}, bf16[32,1920]{1,0:T(8,128)(2,1)S(1)}, u32[]{:S(2)}, u32[]{:S(2)}) collective-permute-start(bf16[32,1920]{1,0:T(8,128)(2,1)S(1)} %collective-permute-done.21.refs_1_), channel_id=1, source_target_pairs={{0,1},{1,0},{2,3},{3,2},{4,5},{5,4},{6,7},{7,6},{8,9},{9,8},{10,11... | collective-permute-start | bytes 368648 | tf_op jit(solution)/shard_map/ppermute | solution.py:167
  29.5 19.8 %collective-permute-start.26 = (bf16[32,1920]{1,0:T(8,128)(2,1)S(1)}, bf16[32,1920]{1,0:T(8,128)(2,1)S(1)}, u32[]{:S(2)}, u32[]{:S(2)}) collective-permute-start(bf16[32,1920]{1,0:T(8,128)(2,1)S(1)} %collective-permute-done.22.refs_2_), channel_id=1, source_target_pairs={{0,1},{1,0},{2,3},{3,2},{4,5},{5,4},{6,7},{7,6},{8,9},{9,8},{10,11... | collective-permute-start | bytes 368648 | tf_op jit(solution)/shard_map/ppermute | solution.py:167
  30.0 19.3 %collective-permute-start.27 = (bf16[32,1920]{1,0:T(8,128)(2,1)S(1)}, bf16[32,1920]{1,0:T(8,128)(2,1)S(1)}, u32[]{:S(2)}, u32[]{:S(2)}) collective-permute-start(bf16[32,1920]{1,0:T(8,128)(2,1)S(1)} %collective-permute-done.23.refs_3_), channel_id=1, source_target_pairs={{0,1},{1,0},{2,3},{3,2},{4,5},{5,4},{6,7},{7,6},{8,9},{9,8},{10,11... | collective-permute-start | bytes 368648 | tf_op jit(solution)/shard_map/ppermute | solution.py:167
  30.0 3.6 %copy-start = (bf16[1,1280,3584]{2,1,0:T(8,128)(2,1)S(1)}, bf16[1,1280,3584]{2,1,0:T(8,128)(2,1)}, u32[]{:S(2)}) copy-start(bf16[1,1280,3584]{2,1,0:T(8,128)(2,1)} %param.20) | copy-start | bytes 27525124
  33.7 3.6 %copy-start.2 = (bf16[1,1280,3584]{2,1,0:T(8,128)(2,1)S(1)}, bf16[1,1280,3584]{2,1,0:T(8,128)(2,1)}, u32[]{:S(2)}) copy-start(bf16[1,1280,3584]{2,1,0:T(8,128)(2,1)} %param.21) | copy-start | bytes 27525124
  37.3 3.6 %copy-start.4 = (bf16[1,1280,3584]{2,1,0:T(8,128)(2,1)S(1)}, bf16[1,1280,3584]{2,1,0:T(8,128)(2,1)}, u32[]{:S(2)}) copy-start(bf16[1,1280,3584]{2,1,0:T(8,128)(2,1)} %param.22) | copy-start | bytes 27525124
  40.9 7.6 %copy-start.8 = (s32[16]{0:T(128)S(1)}, s32[16]{0:T(128)}, u32[]{:S(2)}) copy-start(s32[16]{0:T(128)} %constant.6.clone) | copy-start | bytes 196
  40.9 8.4 %copy-start.6 = (bf16[1,128,1280]{2,1,0:T(8,128)(2,1)S(1)}, bf16[1,128,1280]{2,1,0:T(8,128)(2,1)}, u32[]{:S(2)}) copy-start(bf16[1,128,1280]{2,1,0:T(8,128)(2,1)} %param.18) | copy-start | bytes 983044
  40.9 8.5 %copy-start.7 = (bf16[1,128,1280]{2,1,0:T(8,128)(2,1)S(1)}, bf16[1,128,1280]{2,1,0:T(8,128)(2,1)}, u32[]{:S(2)}) copy-start(bf16[1,128,1280]{2,1,0:T(8,128)(2,1)} %param.19) | copy-start | bytes 983044
  48.0 19.2 %collective-permute-start.14 = (bf16[32,1792]{1,0:T(8,128)(2,1)S(1)}, bf16[32,1792]{1,0:T(8,128)(2,1)}, u32[]{:S(2)}, u32[]{:S(2)}) collective-permute-start(bf16[32,1792]{1,0:T(8,128)(2,1)S(1)} %get-tuple-element.28), channel_id=1, source_target_pairs={{0,1},{1,0},{2,3},{3,2},{4,5},{5,4},{6,7},{7,6},{8,9},{9,8},{10,11... | collective-permute-start | bytes 344072 | tf_op jit(solution)/shard_map/ppermute | solution.py:167
  48.6 19.5 %collective-permute-start.12 = (bf16[32,1792]{1,0:T(8,128)(2,1)S(1)}, bf16[32,1792]{1,0:T(8,128)(2,1)S(1)}, u32[]{:S(2)}, u32[]{:S(2)}) collective-permute-start(bf16[32,1792]{1,0:T(8,128)(2,1)S(1)} %get-tuple-element.26), channel_id=1, source_target_pairs={{0,1},{1,0},{2,3},{3,2},{4,5},{5,4},{6,7},{7,6},{8,9},{9,8},{10,11... | collective-permute-start | bytes 344072 | tf_op jit(solution)/shard_map/ppermute | solution.py:167
  48.8 19.9 %collective-permute-start.10 = (bf16[32,1792]{1,0:T(8,128)(2,1)S(1)}, bf16[32,1792]{1,0:T(8,128)(2,1)S(1)}, u32[]{:S(2)}, u32[]{:S(2)}) collective-permute-start(bf16[32,1792]{1,0:T(8,128)(2,1)S(1)} %get-tuple-element.24), channel_id=1, source_target_pairs={{0,1},{1,0},{2,3},{3,2},{4,5},{5,4},{6,7},{7,6},{8,9},{9,8},{10,11... | collective-permute-start | bytes 344072 | tf_op jit(solution)/shard_map/ppermute | solution.py:167
  49.2 23.5 %collective-permute-start.9 = (bf16[32,1792]{1,0:T(8,128)(2,1)S(1)}, bf16[32,1792]{1,0:T(8,128)(2,1)S(1)}, u32[]{:S(2)}, u32[]{:S(2)}) collective-permute-start(bf16[32,1792]{1,0:T(8,128)(2,1)S(1)} %get-tuple-element.22), channel_id=1, source_target_pairs={{0,1},{1,0},{2,3},{3,2},{4,5},{5,4},{6,7},{7,6},{8,9},{9,8},{10,11... | collective-permute-start | bytes 344072 | tf_op jit(solution)/shard_map/ppermute | solution.py:167
  49.3 3.6 %copy-start.1 = (bf16[1,1280,3584]{2,1,0:T(8,128)(2,1)S(1)}, bf16[1,1280,3584]{2,1,0:T(8,128)(2,1)}, u32[]{:S(2)}) copy-start(bf16[1,1280,3584]{2,1,0:T(8,128)(2,1)} %param.20) | copy-start | bytes 27525124
  52.9 3.6 %copy-start.3 = (bf16[1,1280,3584]{2,1,0:T(8,128)(2,1)S(1)}, bf16[1,1280,3584]{2,1,0:T(8,128)(2,1)}, u32[]{:S(2)}) copy-start(bf16[1,1280,3584]{2,1,0:T(8,128)(2,1)} %param.21) | copy-start | bytes 27525124
  56.5 3.6 %copy-start.5 = (bf16[1,1280,3584]{2,1,0:T(8,128)(2,1)S(1)}, bf16[1,1280,3584]{2,1,0:T(8,128)(2,1)}, u32[]{:S(2)}) copy-start(bf16[1,1280,3584]{2,1,0:T(8,128)(2,1)} %param.22) | copy-start | bytes 27525124
  66.7 2.2 %collective-permute-start.33 = (bf16[32,1792]{1,0:T(8,128)(2,1)S(1)}, bf16[32,1792]{1,0:T(8,128)(2,1)S(1)}, u32[]{:S(2)}, u32[]{:S(2)}) collective-permute-start(bf16[32,1792]{1,0:T(8,128)(2,1)S(1)} %get-tuple-element.37), channel_id=1, source_target_pairs={{0,1},{1,0},{2,3},{3,2},{4,5},{5,4},{6,7},{7,6},{8,9},{9,8},{10,11... | collective-permute-start | bytes 344072 | tf_op jit(solution)/shard_map/ppermute | solution.py:167
  67.2 4.1 %collective-permute-start.31 = (bf16[32,1792]{1,0:T(8,128)(2,1)S(1)}, bf16[32,1792]{1,0:T(8,128)(2,1)S(1)}, u32[]{:S(2)}, u32[]{:S(2)}) collective-permute-start(bf16[32,1792]{1,0:T(8,128)(2,1)S(1)} %get-tuple-element.35), channel_id=1, source_target_pairs={{0,1},{1,0},{2,3},{3,2},{4,5},{5,4},{6,7},{7,6},{8,9},{9,8},{10,11... | collective-permute-start | bytes 344072 | tf_op jit(solution)/shard_map/ppermute | solution.py:167
  68.2 3.7 %collective-permute-start.29 = (bf16[32,1792]{1,0:T(8,128)(2,1)S(1)}, bf16[32,1792]{1,0:T(8,128)(2,1)S(1)}, u32[]{:S(2)}, u32[]{:S(2)}) collective-permute-start(bf16[32,1792]{1,0:T(8,128)(2,1)S(1)} %get-tuple-element.33), channel_id=1, source_target_pairs={{0,1},{1,0},{2,3},{3,2},{4,5},{5,4},{6,7},{7,6},{8,9},{9,8},{10,11... | collective-permute-start | bytes 344072 | tf_op jit(solution)/shard_map/ppermute | solution.py:167
  68.7 13.8 %collective-permute-start.28 = (bf16[32,1792]{1,0:T(8,128)(2,1)S(1)}, bf16[32,1792]{1,0:T(8,128)(2,1)S(1)}, u32[]{:S(2)}, u32[]{:S(2)}) collective-permute-start(bf16[32,1792]{1,0:T(8,128)(2,1)S(1)} %get-tuple-element.31), channel_id=1, source_target_pairs={{0,1},{1,0},{2,3},{3,2},{4,5},{5,4},{6,7},{7,6},{8,9},{9,8},{10,11... | collective-permute-start | bytes 344072 | tf_op jit(solution)/shard_map/ppermute | solution.py:167
  68.9 6.9 %collective-permute-start.15 = (bf16[32,1792]{1,0:T(8,128)(2,1)S(1)}, bf16[32,1792]{1,0:T(8,128)(2,1)S(1)}, u32[]{:S(2)}, u32[]{:S(2)}) collective-permute-start(bf16[32,1792]{1,0:T(8,128)(2,1)S(1)} %add_convert_fusion.6), channel_id=1, source_target_pairs={{0,18},{1,19},{2,16},{3,17},{4,22},{5,23},{6,20},{7,21},{8,26},{9,... | collective-permute-start | bytes 344072 | tf_op jit(solution)/shard_map/ppermute | solution.py:167
  71.3 6.9 %collective-permute-start.13 = (bf16[32,1792]{1,0:T(8,128)(2,1)S(1)}, bf16[32,1792]{1,0:T(8,128)(2,1)S(1)}, u32[]{:S(2)}, u32[]{:S(2)}) collective-permute-start(bf16[32,1792]{1,0:T(8,128)(2,1)S(1)} %add_convert_fusion.7), channel_id=1, source_target_pairs={{0,2},{1,3},{2,0},{3,1},{4,6},{5,7},{6,4},{7,5},{8,10},{9,11},{10,... | collective-permute-start | bytes 344072 | tf_op jit(solution)/shard_map/ppermute | solution.py:167
  71.9 7.0 %collective-permute-start.11 = (bf16[32,1792]{1,0:T(8,128)(2,1)S(1)}, bf16[32,1792]{1,0:T(8,128)(2,1)S(1)}, u32[]{:S(2)}, u32[]{:S(2)}) collective-permute-start(bf16[32,1792]{1,0:T(8,128)(2,1)S(1)} %add_convert_fusion.8), channel_id=1, source_target_pairs={{0,16},{1,17},{2,18},{3,19},{4,20},{5,21},{6,22},{7,23},{8,24},{9,... | collective-permute-start | bytes 344072 | tf_op jit(solution)/shard_map/ppermute | solution.py:167
  72.7 9.8 %collective-permute-start.34 = (bf16[32,1792]{1,0:T(8,128)(2,1)S(1)}, bf16[32,1792]{1,0:T(8,128)(2,1)S(1)}, u32[]{:S(2)}, u32[]{:S(2)}) collective-permute-start(bf16[32,1792]{1,0:T(8,128)(2,1)S(1)} %add_convert_fusion.1), channel_id=1, source_target_pairs={{0,18},{1,19},{2,16},{3,17},{4,22},{5,23},{6,20},{7,21},{8,26},{9,... | collective-permute-start | bytes 344072 | tf_op jit(solution)/shard_map/ppermute | solution.py:167
  75.8 7.6 %collective-permute-start.32 = (bf16[32,1792]{1,0:T(8,128)(2,1)S(1)}, bf16[32,1792]{1,0:T(8,128)(2,1)S(1)}, u32[]{:S(2)}, u32[]{:S(2)}) collective-permute-start(bf16[32,1792]{1,0:T(8,128)(2,1)S(1)} %add_convert_fusion.2), channel_id=1, source_target_pairs={{0,2},{1,3},{2,0},{3,1},{4,6},{5,7},{6,4},{7,5},{8,10},{9,11},{10,... | collective-permute-start | bytes 344072 | tf_op jit(solution)/shard_map/ppermute | solution.py:167
  78.1 5.3 %collective-permute-start.30 = (bf16[32,1792]{1,0:T(8,128)(2,1)S(1)}, bf16[32,1792]{1,0:T(8,128)(2,1)S(1)}, u32[]{:S(2)}, u32[]{:S(2)}) collective-permute-start(bf16[32,1792]{1,0:T(8,128)(2,1)S(1)} %add_convert_fusion.3), channel_id=1, source_target_pairs={{0,16},{1,17},{2,18},{3,19},{4,20},{5,21},{6,22},{7,23},{8,24},{9,... | collective-permute-start | bytes 344072 | tf_op jit(solution)/shard_map/ppermute | solution.py:167
  79.0 8.1 %collective-permute-start.18 = (bf16[8,1792]{1,0:T(8,128)(2,1)S(1)}, bf16[8,1792]{1,0:T(8,128)(2,1)S(1)}, u32[]{:S(2)}, u32[]{:S(2)}) collective-permute-start(bf16[8,1792]{1,0:T(8,128)(2,1)S(1)} %get-tuple-element.42), channel_id=1, source_target_pairs={{0,12},{1,13},{2,14},{3,15},{4,8},{5,9},{6,10},{7,11},{8,4},{9,5},... | collective-permute-start | bytes 86024 | tf_op jit(solution)/shard_map/ppermute | solution.py:167
  82.5 5.5 %collective-permute-start.17 = (bf16[8,1792]{1,0:T(8,128)(2,1)S(1)}, bf16[8,1792]{1,0:T(8,128)(2,1)S(1)}, u32[]{:S(2)}, u32[]{:S(2)}) collective-permute-start(bf16[8,1792]{1,0:T(8,128)(2,1)S(1)} %get-tuple-element.43), channel_id=1, source_target_pairs={{0,4},{1,5},{2,6},{3,7},{4,0},{5,1},{6,2},{7,3},{8,12},{9,13},{10,... | collective-permute-start | bytes 86024 | tf_op jit(solution)/shard_map/ppermute | solution.py:167
  82.5 5.5 %collective-permute-start.16 = (bf16[8,1792]{1,0:T(8,128)(2,1)S(1)}, bf16[8,1792]{1,0:T(8,128)(2,1)S(1)}, u32[]{:S(2)}, u32[]{:S(2)}) collective-permute-start(bf16[8,1792]{1,0:T(8,128)(2,1)S(1)} %get-tuple-element.41), channel_id=1, source_target_pairs={{0,8},{1,9},{2,10},{3,11},{4,12},{5,13},{6,14},{7,15},{8,0},{9,1},... | collective-permute-start | bytes 86024 | tf_op jit(solution)/shard_map/ppermute | solution.py:167
  83.5 5.8 %collective-permute-start.37 = (bf16[8,1792]{1,0:T(8,128)(2,1)S(1)}, bf16[8,1792]{1,0:T(8,128)(2,1)S(1)}, u32[]{:S(2)}, u32[]{:S(2)}) collective-permute-start(bf16[8,1792]{1,0:T(8,128)(2,1)S(1)} %get-tuple-element.39), channel_id=1, source_target_pairs={{0,12},{1,13},{2,14},{3,15},{4,8},{5,9},{6,10},{7,11},{8,4},{9,5},... | collective-permute-start | bytes 86024 | tf_op jit(solution)/shard_map/ppermute | solution.py:167
  87.1 3.9 %collective-permute-start.36 = (bf16[8,1792]{1,0:T(8,128)(2,1)S(1)}, bf16[8,1792]{1,0:T(8,128)(2,1)S(1)}, u32[]{:S(2)}, u32[]{:S(2)}) collective-permute-start(bf16[8,1792]{1,0:T(8,128)(2,1)S(1)} %get-tuple-element.40), channel_id=1, source_target_pairs={{0,4},{1,5},{2,6},{3,7},{4,0},{5,1},{6,2},{7,3},{8,12},{9,13},{10,... | collective-permute-start | bytes 86024 | tf_op jit(solution)/shard_map/ppermute | solution.py:167
  87.1 4.8 %collective-permute-start.35 = (bf16[8,1792]{1,0:T(8,128)(2,1)S(1)}, bf16[8,1792]{1,0:T(8,128)(2,1)S(1)}, u32[]{:S(2)}, u32[]{:S(2)}) collective-permute-start(bf16[8,1792]{1,0:T(8,128)(2,1)S(1)} %get-tuple-element.38), channel_id=1, source_target_pairs={{0,8},{1,9},{2,10},{3,11},{4,12},{5,13},{6,14},{7,15},{8,0},{9,1},... | collective-permute-start | bytes 86024 | tf_op jit(solution)/shard_map/ppermute | solution.py:167

commit v2 on v1

--- a/solution.py
+++ b/solution.py
@@ -20,7 +20,14 @@
     return lax.dot_general(a, b, (((1,), (0,)), ((), ())), preferred_element_type=jnp.float32)
 
 
-def pack_kernel(expert_count, xf, rf, wf, xb, rb, wb, of, ob):
+def pack_kernel(expert_count, *refs):
+    given, (of, ob), held, arrived = refs[:6], refs[6:8], refs[8:14], refs[14]
+    copies = [pltpu.make_async_copy(a, b, arrived.at[i]) for i, (a, b) in enumerate(zip(given, held))]
+    for copy in copies:
+        copy.start()
+    for copy in copies:
+        copy.wait()
+    xf, rf, wf, xb, rb, wb = held
     tokens, topk = rf.shape
     cols = xf.shape[1]
     lane = lax.broadcasted_iota(jnp.int32, (tokens, LANES), 1)
@@ -43,11 +50,19 @@
         o[:, cols:] = extra.astype(jnp.bfloat16)
 
 
-def pack(expert_count, xf, rf, wf, xb, rb, wb):
-    shape = jax.ShapeDtypeStruct((xf.shape[0], xf.shape[1] + LANES), jnp.bfloat16)
+def pack(expert_count, *given):
+    tokens, cols = given[0].shape
+    shape = jax.ShapeDtypeStruct((tokens, cols + LANES), jnp.bfloat16)
+    given = [pltpu.with_memory_space_constraint(a, pltpu.MemorySpace.HBM) for a in given]
     return pl.pallas_call(
-        functools.partial(pack_kernel, expert_count), out_shape=(shape, shape), name="pack"
-    )(xf, rf, wf, xb, rb, wb)
+        functools.partial(pack_kernel, expert_count),
+        out_shape=(shape, shape),
+        in_specs=[pl.BlockSpec(memory_space=pltpu.MemorySpace.HBM)] * 6,
+        scratch_shapes=[pltpu.VMEM(a.shape, a.dtype) for a in given] + [pltpu.SemaphoreType.DMA((6,))],
+        compiler_params=pltpu.CompilerParams(vmem_limit_bytes=2 << 20),
+        cost_estimate=pl.CostEstimate(flops=40_000_000_000, bytes_accessed=100_000_000, transcendentals=0),
+        name="pack",
+    )(*given)
 
 
 def chunks(total, size):
@@ -65,7 +80,7 @@
     return jnp.sum(jnp.where(lane == index, meta, 0.0), axis=1, keepdims=True)
 
 
-def load_rows(groups, sections, width, pieces, rows, held):
+def load_rows(groups, sections, width, pieces, held):
     at, metas = 0, []
     for g in range(groups):
         count = pieces[g * sections].shape[0]
@@ -89,30 +104,42 @@
                 row += out.shape[0]
 
 
-def forward_kernel(groups, sections, width, experts, *refs):
+def hidden_kernel(groups, sections, width, experts, *refs):
     n = groups * sections
-    pieces, (gate, up, down), outs, (held, hidden) = refs[:n], refs[n : n + 3], refs[n + 3 : 2 * n + 3], refs[2 * n + 3 :]
-    meta = load_rows(groups, sections, width, pieces, None, held)
+    pieces, (gate, up), (hidden, scale), (held,) = refs[:n], refs[n : n + 2], refs[n + 2 : n + 4], refs[n + 4 :]
+    meta = load_rows(groups, sections, width, pieces, held)
     me = lax.axis_index("expert")
-    weight = field_of(meta, me) + field_of(meta, me + experts)
+    scale[...] = field_of(meta, me) + field_of(meta, me + experts)
     for at, size in chunks(hidden.shape[1], 256):
         g = last_last(held[...], gate[at : at + size, :])
         u = last_last(held[...], up[at : at + size, :])
         hidden[:, at : at + size] = (g / (1.0 + jnp.exp(-g)) * u).astype(jnp.bfloat16)
+
+
+def down_kernel(groups, sections, width, hidden, scale, down, *outs):
     store_rows(
         groups, sections, width, outs,
-        lambda start, size: last_first(hidden[...], down[:, pl.ds(start, size)]) * weight,
-    )
-
-
-def backward_kernel(groups, sections, width, experts, capacity, *refs):
+        lambda start, size: last_first(hidden[...], down[:, pl.ds(start, size)]) * scale[...],
+    )
+
+
+def sender_of_rows(rows, tokens, order, me):
+    place = lax.broadcasted_iota(jnp.int32, (rows, 1), 0) // tokens
+    block = jnp.zeros((rows, 1), jnp.int32) if order is None else jnp.full((rows, 1), me)
+    for bit in range((rows // tokens - 1).bit_length()):
+        block = block ^ (place >> bit & 1) * (1 << bit if order is None else order[1 << bit])
+    return block
+
+
+def backward_kernel(groups, sections, width, experts, capacity, tokens, order, *refs):
     n = groups * sections
-    pieces, (block, gate_saved, up_saved, gate, up, down) = refs[:n], refs[n : n + 6]
-    outs, (held, grad_gate, grad_up) = refs[n + 6 : 2 * n + 6], refs[2 * n + 6 :]
-    meta = load_rows(groups, sections, width, pieces, None, held)
+    pieces, (gate_saved, up_saved, gate, up, down) = refs[:n], refs[n : n + 5]
+    outs, (held, grad_gate, grad_up) = refs[n + 5 : 2 * n + 5], refs[2 * n + 5 :]
+    meta = load_rows(groups, sections, width, pieces, held)
     me = lax.axis_index("expert")
     weight = field_of(meta, me) + field_of(meta, me + experts)
-    slot = block[...] * capacity + field_of(meta, me + 2 * experts).astype(jnp.int32)
+    block = sender_of_rows(held.shape[0], tokens, order, me)
+    slot = block * capacity + field_of(meta, me + 2 * experts).astype(jnp.int32)
     slot = jnp.where(weight > 0.0, slot, -1)
     place = lax.broadcasted_iota(jnp.int32, (held.shape[0], gate_saved.shape[0]), 1)
     pick = jnp.where(place == slot, 1.0, 0.0).astype(jnp.bfloat16)
@@ -131,34 +158,54 @@
     )
 
 
-def expert_call(kernel, name, pieces, sections, width, extra, weights, scratch):
-    outs = tuple(jax.ShapeDtypeStruct((p.shape[0], width), jnp.bfloat16) for p in pieces)
+def expert_call(kernel, name, shapes, weights, given, scratch=()):
+    rows = given[0].shape[0]
     weights = [pltpu.with_memory_space_constraint(w, VMEM) for w in weights]
+    cost = pl.CostEstimate(
+        flops=sum(256 * w.size for w in weights), bytes_accessed=sum(2 * w.size for w in weights), transcendentals=0
+    )
     return pl.pallas_call(
         kernel,
-        out_shape=outs,
+        out_shape=shapes,
         scratch_shapes=scratch,
         compiler_params=pltpu.CompilerParams(vmem_limit_bytes=24 << 20),
+        cost_estimate=cost,
         name=name,
-    )(*pieces, *extra, *weights)
-
-
-def experts_forward(pieces, sections, width, experts, weights):
-    rows = sum(p.shape[0] for p in pieces) // sections
-    units, features = weights[0].shape
+    )(*given, *weights)
+
+
+def like_pieces(pieces, width):
+    return tuple(jax.ShapeDtypeStruct((p.shape[0], width), jnp.bfloat16) for p in pieces)
+
+
+def rows_of(pieces, sections):
+    return sum(p.shape[0] for p in pieces) // sections
+
+
+def forward_hidden(pieces, sections, width, experts, weights):
+    rows, (units, features) = rows_of(pieces, sections), weights[0].shape
     return expert_call(
-        functools.partial(forward_kernel, len(pieces) // sections, sections, width, experts),
-        "experts_forward", pieces, sections, width, [], weights,
-        [pltpu.VMEM((rows, features), jnp.bfloat16), pltpu.VMEM((rows, units), jnp.bfloat16)],
-    )
-
-
-def experts_backward(pieces, sections, width, experts, capacity, block, stash, weights):
-    rows = sum(p.shape[0] for p in pieces) // sections
-    units, features = weights[0].shape
+        functools.partial(hidden_kernel, len(pieces) // sections, sections, width, experts),
+        "forward_hidden",
+        (jax.ShapeDtypeStruct((rows, units), jnp.bfloat16), jax.ShapeDtypeStruct((rows, 1), jnp.float32)),
+        weights, pieces, [pltpu.VMEM((rows, features), jnp.bfloat16)],
+    )
+
+
+def forward_down(pieces, sections, width, hidden, scale, weight):
     return expert_call(
-        functools.partial(backward_kernel, len(pieces) // sections, sections, width, experts, capacity),
-        "experts_backward", pieces, sections, width, [block, *stash], weights,
+        functools.partial(down_kernel, len(pieces) // sections, sections, width),
+        "forward_down", like_pieces(pieces, width), [weight], [hidden, scale],
+    )
+
+
+def experts_backward(pieces, sections, width, experts, capacity, tokens, order, stash, weights):
+    rows, (units, features) = rows_of(pieces, sections), weights[0].shape
+    return expert_call(
+        functools.partial(
+            backward_kernel, len(pieces) // sections, sections, width, experts, capacity, tokens, order
+        ),
+        "experts_backward", like_pieces(pieces, width), weights, [*pieces, *stash],
         [pltpu.VMEM((rows, features), jnp.bfloat16)] + [pltpu.VMEM((rows, units), jnp.bfloat16)] * 2,
     )
 
@@ -171,26 +218,37 @@
 X, Y, CORE = 2, 16, 1
 
 
-def spread(message):
+def after(value, *others):
+    return lax.optimization_barrier((value, *others))[0]
+
+
+def spread_line(message):
     tokens, cols = message.shape
     held = message[None]
     for mask in Z[:2]:
         held = jnp.concatenate([held, move(held, mask, 32)], axis=0)
-    held = held.reshape(4 * tokens, cols)
-    own = [held, move(held, Y, 32), move(held, X, 32), move(held, X ^ Y, 32)]
-    return own + [move(p, CORE, 32) for p in own]
-
-
-def collect(pieces, tokens):
-    other = [move(p, CORE, 32) for p in pieces[4:]]
-    own = [
-        (a.astype(jnp.float32) + b.astype(jnp.float32)).astype(jnp.bfloat16) for a, b in zip(pieces[:4], other)
-    ]
-    parts = [own[0], move(own[1], Y, 32), move(own[2], X, 32), move(own[3], X ^ Y, 32)]
-    total = sum(p.astype(jnp.float32) for p in parts).astype(jnp.bfloat16)
+    return held.reshape(4 * tokens, cols)
+
+
+def spread_plane(held):
+    return [held, move(held, Y, 32), move(held, X, 32), move(held, X ^ Y, 32)]
+
+
+def swap(pieces):
+    return [move(p, CORE, 32) for p in pieces]
+
+
+def add(*parts):
+    return sum(p.astype(jnp.float32) for p in parts).astype(jnp.bfloat16)
+
+
+def collect_plane(own):
+    return add(own[0], move(own[1], Y, 32), move(own[2], X, 32), move(own[3], X ^ Y, 32))
+
+
+def collect_line(total, tokens):
     rows = [total[k * tokens : (k + 1) * tokens] for k in range(4)]
-    parts = [rows[0]] + [move(rows[k + 1], Z[k], 32) for k in range(3)]
-    return sum(p.astype(jnp.float32) for p in parts).astype(jnp.bfloat16)
+    return add(rows[0], *[move(rows[k + 1], Z[k], 32) for k in range(3)])
 
 
 def spread_any(message, width):
@@ -216,21 +274,27 @@
     message_f, message_b = pack(
         expert_count, forward_input, forward_route, forward_weight, output_grad, backward_route, backward_weight
     )
-    if (section_count, expert_count) == (2, 16):
-        sections = 2
-        mask = jnp.array([c ^ x ^ z for c in (0, CORE) for x in (0, X) for z in (0, 8, 4, 12)], jnp.int32)
-        order = lax.axis_index("expert") ^ mask
-        pieces_f, pieces_b = spread(message_f), spread(message_b)
-        gather = functools.partial(collect, tokens=tokens)
-    else:
-        sections = 1
-        order = jnp.arange(expert_count, dtype=jnp.int32)
+    if (section_count, expert_count) != (2, 16):
+        whole = width * section_count
         pieces_f, pieces_b = spread_any(message_f, width), spread_any(message_b, width)
-        width, gather = width * section_count, collect_any
-    block = jnp.repeat(order, tokens)[:, None]
-    done_f = experts_forward(pieces_f, sections, width, expert_count, weights)
-    done_b = experts_backward(pieces_b, sections, width, expert_count, capacity, block, stash, weights)
-    return gather(list(done_f)), gather(list(done_b))
+        hidden, scale = forward_hidden(pieces_f, 1, whole, expert_count, weights[:2])
+        done_f = forward_down(pieces_f, 1, whole, hidden, scale, weights[2])
+        done_b = experts_backward(pieces_b, 1, whole, expert_count, capacity, tokens, None, stash, weights)
+        return collect_any(done_f), collect_any(done_b)
+    order = [c ^ x ^ z for c in (0, CORE) for x in (0, X) for z in (0, *Z)]
+    line_b, line_f = spread_line(message_b), spread_line(message_f)
+    plane_b = spread_plane(line_b)
+    plane_f = spread_plane(line_f)
+    pieces_b = plane_b + swap(plane_b)
+    done_b = experts_backward(pieces_b, 2, width, expert_count, capacity, tokens, order, stash, weights)
+    plane_f = [line_f] + [after(p, done_b[0]) for p in plane_f[1:]]
+    pieces_f = plane_f + swap(plane_f)
+    hidden, scale = forward_hidden(pieces_f, 2, width, expert_count, weights[:2])
+    own_b = [add(a, b) for a, b in zip(done_b[:4], swap(done_b[4:]))]
+    done_f0 = None
+    done_f = forward_down(pieces_f, 2, width, hidden, scale, weights[2])
+    own_f = [add(a, b) for a, b in zip(done_f[:4], swap(done_f[4:]))]
+    return collect_line(collect_plane(own_f), tokens), collect_line(collect_plane(own_b), tokens)
 
 
 def solution(mesh):

time: 93.2 us -> 66.1 us (0.71)
  local copies, waits for them, and re-layouts: 21.8 us -> 0.05 us
  other arithmetic: 5.56 us -> 1.65 us
  waiting for transfers between devices: 13.9 us -> 11.3 us
  starting transfers between devices: 35.2 us -> 37.2 us
    unnamed x18 -> x16, local copies, waits for them, and re-layouts: 21.6 us -> 0.04 us
    ppermute x38, waiting for transfers between devices: 13.9 us -> 11.3 us  [move(): return lax.ppermute(value, AXES, [(i, i ^ mask) for i in range(devices)])]
    ppermute x38, starting transfers between devices: 35.2 us -> 37.2 us  [move(): return lax.ppermute(value, AXES, [(i, i ^ mask) for i in range(devices)])]
    concatenate x2, other arithmetic: 1.53 us -> 0.02 us  [spread_line(): held = jnp.concatenate([held, move(held, mask, 32)], axis=0)]
    reshape x2, other arithmetic: 1.54 us -> 0.04 us  [spread_line(): return held.reshape(4 * tokens, cols)]
    pallas_call x2 -> x3, Pallas kernels: 13.6 us -> 13.7 us  [expert_call(): pl.pallas_call(kernel, out_shape=shapes, scratch_shapes=scratch, compiler...]
  transfers between devices with their start and end apart: 38 -> 38, of which waited for: 12 -> 12; matrix products, arithmetic and copies ran while one was open for 6% -> 2% of each run, Pallas kernels for 15% -> 21%
where the time goes in v2:
time: 66.1 us; the launch traced here: 65.9 us
  starting transfers between devices  37.2 us (56%)
  Pallas kernels  14.8 us (22%)
  waiting for transfers between devices  11.3 us (17%)
  other arithmetic  1.65 us (2%)
  between operations  0.92 us (1%)
    ppermute x38, starting transfers between devices, move(): return lax.ppermute(value, AXES, [(i, i ^ mask) for i in range(devices)])  37.2 us
    pallas_call x3, Pallas kernels, expert_call(): pl.pallas_call(kernel, out_shape=shapes, scratch_shapes=scratch, compiler...  13.7 us
    ppermute x38, waiting for transfers between devices, move(): return lax.ppermute(value, AXES, [(i, i ^ mask) for i in range(devices)])  11.3 us
    convert_element_type x10, other arithmetic, add(): return sum((p.astype(jnp.float32) for p in parts)).astype(jnp.bfloat16)  1.59 us
  transfers between devices with their start and end apart: 38, of which 12 were waited for; matrix products, arithmetic and copies ran while one was open for 2% of the time, Pallas kernels for 21%

profile of v2, /device:TPU:0, one launch (start us, length us, event | category | flops | bytes accessed | tf_op | source)
XLA Modules:
  0.0 65.9 jit_solution(4162303778141935174)
XLA Ops:
  0.7 0.0 copy-start.2
  0.7 1.1 %pack.1 = (bf16[8,1920]{1,0:T(8,128)(2,1)S(1)}, bf16[8,1920]{1,0:T(8,128)(2,1)S(1)}) custom-call(bf16[8,1792]{1,0:T(8,128)(2,1)} %refs_0_.1, s32[8,8]{1,0:T(8,128)} %refs_1_.1, f32[8,8]{1,0:T(8,128)} %refs_2_.1, bf16[8,1792]{1,0:T(8,128)(2,1)} %refs_3_.1, s32[8,8]{1,0:T(8,128)} %refs_4_.1, f32[8,8]{1,0:T(8,128)} %refs_5_.1), custom_call_target="tpu_custom_call" | custom-call | flops 40000000000 | bytes 100000000 | tf_op jit(solution)/shard_map/pack/pallas_call | solution.py:57
  1.8 4.1 %collective-permute-start.3 = (bf16[1,8,1920]{2,1,0:T(8,128)(2,1)S(1)}, bf16[1,8,1920]{2,1,0:T(8,128)(2,1)S(1)}, u32[]{:S(2)}, u32[]{:S(2)}) collective-permute-start(bf16[1,8,1920]{2,1,0:T(8,128)(2,1)S(1)} %bitcast.24), channel_id=1, source_target_pairs={{0,8},{1,9},{2,10},{3,11},{4,12},{5,13},{6,14},{7,15},{8,0},{9,1},... | collective-permute-start | bytes 92168 | tf_op jit(solution)/shard_map/ppermute | solution.py:214
  5.9 2.2 %collective-permute-done.3 = bf16[1,8,1920]{2,1,0:T(8,128)(2,1)S(1)} collective-permute-done((bf16[1,8,1920]{2,1,0:T(8,128)(2,1)S(1)}, bf16[1,8,1920]{2,1,0:T(8,128)(2,1)S(1)}, u32[]{:S(2)}, u32[]{:S(2)}) %collective-permute-start.3) | collective-permute-done | bytes 30752 | tf_op jit(solution)/shard_map/ppermute | solution.py:214
  8.1 1.6 %collective-permute-start.4 = (bf16[2,8,1920]{2,1,0:T(8,128)(2,1)S(1)}, bf16[2,8,1920]{2,1,0:T(8,128)(2,1)S(1)}, u32[]{:S(2)}, u32[]{:S(2)}) collective-permute-start(bf16[2,8,1920]{2,1,0:T(8,128)(2,1)S(1)} %pad_maximum_fusion.1), channel_id=1, source_target_pairs={{0,4},{1,5},{2,6},{3,7},{4,0},{5,1},{6,2},{7,3},{8,12},{9,13},{10,... | collective-permute-start | bytes 184328 | tf_op jit(solution)/shard_map/ppermute | solution.py:214
  9.8 2.8 %collective-permute-start = (bf16[1,8,1920]{2,1,0:T(8,128)(2,1)S(1)}, bf16[1,8,1920]{2,1,0:T(8,128)(2,1)S(1)}, u32[]{:S(2)}, u32[]{:S(2)}) collective-permute-start(bf16[1,8,1920]{2,1,0:T(8,128)(2,1)S(1)} %bitcast.21), channel_id=1, source_target_pairs={{0,8},{1,9},{2,10},{3,11},{4,12},{5,13},{6,14},{7,15},{8,0},{9,1},... | collective-permute-start | bytes 92168 | tf_op jit(solution)/shard_map/ppermute | solution.py:214
  12.6 0.2 collective-permute-done.4
  12.8 1.6 %collective-permute-start.6 = (bf16[32,1920]{1,0:T(8,128)(2,1)S(1)}, bf16[32,1920]{1,0:T(8,128)(2,1)S(1)}, u32[]{:S(2)}, u32[]{:S(2)}) collective-permute-start(bf16[32,1920]{1,0:T(8,128)(2,1)S(1)} %maximum_bitcast_fusion.1.refs_0_), channel_id=1, source_target_pairs={{0,2},{1,3},{2,0},{3,1},{4,6},{5,7},{6,4},{7,5},{8,10},{9,11},{10,... | collective-permute-start | bytes 368648 | tf_op jit(solution)/shard_map/ppermute | solution.py:214
  14.4 1.5 %collective-permute-start.7 = (bf16[32,1920]{1,0:T(8,128)(2,1)S(1)}, bf16[32,1920]{1,0:T(8,128)(2,1)S(1)}, u32[]{:S(2)}, u32[]{:S(2)}) collective-permute-start(bf16[32,1920]{1,0:T(8,128)(2,1)S(1)} %maximum_bitcast_fusion.1.refs_0_), channel_id=1, source_target_pairs={{0,18},{1,19},{2,16},{3,17},{4,22},{5,23},{6,20},{7,21},{8,26},{9,... | collective-permute-start | bytes 368648 | tf_op jit(solution)/shard_map/ppermute | solution.py:214
  15.9 0.4 collective-permute-start.5
  16.4 1.6 %collective-permute-start.1 = (bf16[2,8,1920]{2,1,0:T(8,128)(2,1)S(1)}, bf16[2,8,1920]{2,1,0:T(8,128)(2,1)S(1)}, u32[]{:S(2)}, u32[]{:S(2)}) collective-permute-start(bf16[2,8,1920]{2,1,0:T(8,128)(2,1)S(1)} %pad_maximum_fusion), channel_id=1, source_target_pairs={{0,4},{1,5},{2,6},{3,7},{4,0},{5,1},{6,2},{7,3},{8,12},{9,13},{10,... | collective-permute-start | bytes 184328 | tf_op jit(solution)/shard_map/ppermute | solution.py:214
  18.0 0.0 collective-permute-start.8
  18.0 0.2 collective-permute-done.6.refs_2_
  18.2 0.3 collective-permute-start.10
  18.5 1.8 %collective-permute-done.7.refs_3_ = bf16[32,1920]{1,0:T(8,128)(2,1)S(1)} collective-permute-done((bf16[32,1920]{1,0:T(8,128)(2,1)S(1)}, bf16[32,1920]{1,0:T(8,128)(2,1)S(1)}, u32[]{:S(2)}, u32[]{:S(2)}) %collective-permute-start.7) | collective-permute-done | bytes 122912 | tf_op jit(solution)/shard_map/ppermute | solution.py:214
  20.3 0.0 collective-permute-start.11
  20.3 1.2 %collective-permute-done.5.refs_1_ = bf16[32,1920]{1,0:T(8,128)(2,1)S(1)} collective-permute-done((bf16[32,1920]{1,0:T(8,128)(2,1)S(1)}, bf16[32,1920]{1,0:T(8,128)(2,1)S(1)}, u32[]{:S(2)}, u32[]{:S(2)}) %collective-permute-start.5) | collective-permute-done | bytes 122912 | tf_op jit(solution)/shard_map/ppermute | solution.py:214
  21.5 0.0 collective-permute-start.9
  21.5 0.0 collective-permute-done.1
  21.5 1.7 %collective-permute-start.13 = (bf16[32,1920]{1,0:T(8,128)(2,1)S(1)}, bf16[32,1920]{1,0:T(8,128)(2,1)S(1)}, u32[]{:S(2)}, u32[]{:S(2)}) collective-permute-start(bf16[32,1920]{1,0:T(8,128)(2,1)S(1)} %maximum_bitcast_fusion.refs_0_), channel_id=1, source_target_pairs={{0,18},{1,19},{2,16},{3,17},{4,22},{5,23},{6,20},{7,21},{8,26},{9,... | collective-permute-start | bytes 368648 | tf_op jit(solution)/shard_map/ppermute | solution.py:214
  23.2 0.0 collective-permute-done.8.refs_4_
  23.3 0.8 %collective-permute-start.12 = (bf16[32,1920]{1,0:T(8,128)(2,1)S(1)}, bf16[32,1920]{1,0:T(8,128)(2,1)S(1)}, u32[]{:S(2)}, u32[]{:S(2)}) collective-permute-start(bf16[32,1920]{1,0:T(8,128)(2,1)S(1)} %maximum_bitcast_fusion.refs_0_), channel_id=1, source_target_pairs={{0,2},{1,3},{2,0},{3,1},{4,6},{5,7},{6,4},{7,5},{8,10},{9,11},{10,... | collective-permute-start | bytes 368648 | tf_op jit(solution)/shard_map/ppermute | solution.py:214
  24.1 0.0 collective-permute-done.10.refs_6_
  24.1 1.0 %collective-permute-start.2 = (bf16[32,1920]{1,0:T(8,128)(2,1)S(1)}, bf16[32,1920]{1,0:T(8,128)(2,1)S(1)}, u32[]{:S(2)}, u32[]{:S(2)}) collective-permute-start(bf16[32,1920]{1,0:T(8,128)(2,1)S(1)} %maximum_bitcast_fusion.refs_0_), channel_id=1, source_target_pairs={{0,16},{1,17},{2,18},{3,19},{4,20},{5,21},{6,22},{7,23},{8,24},{9,... | collective-permute-start | bytes 368648 | tf_op jit(solution)/shard_map/ppermute | solution.py:214
  25.1 0.0 collective-permute-done.9.refs_5_
  25.2 6.4 %experts_backward.1 = (bf16[32,1792]{1,0:T(8,128)(2,1)S(1)}, bf16[32,1792]{1,0:T(8,128)(2,1)S(1)}, bf16[32,1792]{1,0:T(8,128)(2,1)S(1)}, bf16[32,1792]{1,0:T(8,1...) custom-call(bf16[32,1920]{1,0:T(8,128)(2,1)S(1)} %maximum_bitcast_fu, ...), custom_call_target="tpu_custom_call" | custom-call | flops 3523215360 | bytes 27525120 | tf_op jit(solution)/shard_map/experts_backward/pallas_call | solution.py:167
  31.6 0.1 collective-permute-start.29
  31.6 0.5 collective-permute-start.14
  32.1 0.1 collective-permute-start.31
  32.2 0.4 collective-permute-start.33
  32.7 0.1 collective-permute-start.28
  32.7 0.2 collective-permute-done.29
  33.0 0.2 collective-permute-start.17
  33.2 0.3 collective-permute-done.31
  33.5 0.2 collective-permute-start.16
  33.7 0.4 collective-permute-start.15
  34.1 0.0 slice-start.1
  34.2 1.1 %collective-permute-start.30 = (bf16[32,1792]{1,0:T(8,128)(2,1)S(1)}, bf16[32,1792]{1,0:T(8,128)(2,1)S(1)}, u32[]{:S(2)}, u32[]{:S(2)}) collective-permute-start(bf16[32,1792]{1,0:T(8,128)(2,1)S(1)} %add_convert_fusion.3), channel_id=1, source_target_pairs={{0,16},{1,17},{2,18},{3,19},{4,20},{5,21},{6,22},{7,23},{8,24},{9,... | collective-permute-start | bytes 344072 | tf_op jit(solution)/shard_map/ppermute | solution.py:214
  35.3 1.2 %collective-permute-start.32 = (bf16[32,1792]{1,0:T(8,128)(2,1)S(1)}, bf16[32,1792]{1,0:T(8,128)(2,1)S(1)}, u32[]{:S(2)}, u32[]{:S(2)}) collective-permute-start(bf16[32,1792]{1,0:T(8,128)(2,1)S(1)} %add_convert_fusion.2), channel_id=1, source_target_pairs={{0,2},{1,3},{2,0},{3,1},{4,6},{5,7},{6,4},{7,5},{8,10},{9,11},{10,... | collective-permute-start | bytes 344072 | tf_op jit(solution)/shard_map/ppermute | solution.py:214
  36.5 1.2 %collective-permute-start.34 = (bf16[32,1792]{1,0:T(8,128)(2,1)S(1)}, bf16[32,1792]{1,0:T(8,128)(2,1)S(1)}, u32[]{:S(2)}, u32[]{:S(2)}) collective-permute-start(bf16[32,1792]{1,0:T(8,128)(2,1)S(1)} %add_convert_fusion.1), channel_id=1, source_target_pairs={{0,18},{1,19},{2,16},{3,17},{4,22},{5,23},{6,20},{7,21},{8,26},{9,... | collective-permute-start | bytes 344072 | tf_op jit(solution)/shard_map/ppermute | solution.py:214
  37.7 5.9 %forward_hidden.1 = (bf16[128,1280]{1,0:T(8,128)(2,1)S(1)}, f32[128,1]{1,0:T(8,128)S(1)}) custom-call(bf16[32,1920]{1,0:T(8,128)(2,1)S(1)} %maximum_bitcast_fusion.refs_0_, bf16[32,1920]{1,0:T(8,128)(2,1)S(1)} %collective-permute-done.2.refs_1_, bf16[32,1920]{1,0:T(8,128)(2,1)S(1)} %collective-permute-done.12.refs_2_, ...), custom_call_target="tpu_custom_call" | custom-call | flops 2348810240 | bytes 18350080 | tf_op jit(solution)/shard_map/forward_hidden/pallas_call | solution.py:167
  43.6 1.4 %forward_down.1 = (bf16[32,1792]{1,0:T(8,128)(2,1)S(1)}, bf16[32,1792]{1,0:T(8,128)(2,1)S(1)}, bf16[32,1792]{1,0:T(8,128)(2,1)S(1)}, bf16[32,1792]{1,0:T(8,128)(...) custom-call(bf16[128,1280]{1,0:T(8,128)(2,1)S(1)} %get-tuple-element, ...), custom_call_target="tpu_custom_call" | custom-call | flops 1174405120 | bytes 9175040 | tf_op jit(solution)/shard_map/forward_down/pallas_call | solution.py:167
  45.0 0.1 collective-permute-start.19
  45.1 0.5 collective-permute-start.21
  45.6 0.1 collective-permute-start.23
  45.7 0.4 collective-permute-start.18
  46.1 0.1 add_convert_fusion
  46.2 0.2 collective-permute-done.19
  46.5 1.1 %collective-permute-start.20 = (bf16[32,1792]{1,0:T(8,128)(2,1)S(1)}, bf16[32,1792]{1,0:T(8,128)(2,1)S(1)}, u32[]{:S(2)}, u32[]{:S(2)}) collective-permute-start(bf16[32,1792]{1,0:T(8,128)(2,1)S(1)} %add_convert_fusion.8), channel_id=1, source_target_pairs={{0,16},{1,17},{2,18},{3,19},{4,20},{5,21},{6,22},{7,23},{8,24},{9,... | collective-permute-start | bytes 344072 | tf_op jit(solution)/shard_map/ppermute | solution.py:214
  47.6 1.3 %collective-permute-start.22 = (bf16[32,1792]{1,0:T(8,128)(2,1)S(1)}, bf16[32,1792]{1,0:T(8,128)(2,1)S(1)}, u32[]{:S(2)}, u32[]{:S(2)}) collective-permute-start(bf16[32,1792]{1,0:T(8,128)(2,1)S(1)} %add_convert_fusion.7), channel_id=1, source_target_pairs={{0,2},{1,3},{2,0},{3,1},{4,6},{5,7},{6,4},{7,5},{8,10},{9,11},{10,... | collective-permute-start | bytes 344072 | tf_op jit(solution)/shard_map/ppermute | solution.py:214
  48.9 1.3 %collective-permute-start.24 = (bf16[32,1792]{1,0:T(8,128)(2,1)S(1)}, bf16[32,1792]{1,0:T(8,128)(2,1)S(1)}, u32[]{:S(2)}, u32[]{:S(2)}) collective-permute-start(bf16[32,1792]{1,0:T(8,128)(2,1)S(1)} %add_convert_fusion.6), channel_id=1, source_target_pairs={{0,18},{1,19},{2,16},{3,17},{4,22},{5,23},{6,20},{7,21},{8,26},{9,... | collective-permute-start | bytes 344072 | tf_op jit(solution)/shard_map/ppermute | solution.py:214
  50.2 2.2 %collective-permute-start.35 = (bf16[8,1792]{1,0:T(8,128)(2,1)S(1)}, bf16[8,1792]{1,0:T(8,128)(2,1)S(1)}, u32[]{:S(2)}, u32[]{:S(2)}) collective-permute-start(bf16[8,1792]{1,0:T(8,128)(2,1)S(1)} %get-tuple-element.48), channel_id=1, source_target_pairs={{0,8},{1,9},{2,10},{3,11},{4,12},{5,13},{6,14},{7,15},{8,0},{9,1},... | collective-permute-start | bytes 86024 | tf_op jit(solution)/shard_map/ppermute | solution.py:214
  52.4 1.8 %collective-permute-start.36 = (bf16[8,1792]{1,0:T(8,128)(2,1)S(1)}, bf16[8,1792]{1,0:T(8,128)(2,1)S(1)}, u32[]{:S(2)}, u32[]{:S(2)}) collective-permute-start(bf16[8,1792]{1,0:T(8,128)(2,1)S(1)} %get-tuple-element.50), channel_id=1, source_target_pairs={{0,4},{1,5},{2,6},{3,7},{4,0},{5,1},{6,2},{7,3},{8,12},{9,13},{10,... | collective-permute-start | bytes 86024 | tf_op jit(solution)/shard_map/ppermute | solution.py:214
  54.2 0.9 %collective-permute-start.37 = (bf16[8,1792]{1,0:T(8,128)(2,1)S(1)}, bf16[8,1792]{1,0:T(8,128)(2,1)S(1)}, u32[]{:S(2)}, u32[]{:S(2)}) collective-permute-start(bf16[8,1792]{1,0:T(8,128)(2,1)S(1)} %get-tuple-element.49), channel_id=1, source_target_pairs={{0,12},{1,13},{2,14},{3,15},{4,8},{5,9},{6,10},{7,11},{8,4},{9,5},... | collective-permute-start | bytes 86024 | tf_op jit(solution)/shard_map/ppermute | solution.py:214
  55.1 0.3 collective-permute-done.24
  55.5 0.1 add_convert_fusion.5
  55.6 2.3 %collective-permute-start.25 = (bf16[8,1792]{1,0:T(8,128)(2,1)S(1)}, bf16[8,1792]{1,0:T(8,128)(2,1)S(1)}, u32[]{:S(2)}, u32[]{:S(2)}) collective-permute-start(bf16[8,1792]{1,0:T(8,128)(2,1)S(1)} %get-tuple-element.51), channel_id=1, source_target_pairs={{0,8},{1,9},{2,10},{3,11},{4,12},{5,13},{6,14},{7,15},{8,0},{9,1},... | collective-permute-start | bytes 86024 | tf_op jit(solution)/shard_map/ppermute | solution.py:214
  57.8 1.8 %collective-permute-start.26 = (bf16[8,1792]{1,0:T(8,128)(2,1)S(1)}, bf16[8,1792]{1,0:T(8,128)(2,1)S(1)}, u32[]{:S(2)}, u32[]{:S(2)}) collective-permute-start(bf16[8,1792]{1,0:T(8,128)(2,1)S(1)} %get-tuple-element.53), channel_id=1, source_target_pairs={{0,4},{1,5},{2,6},{3,7},{4,0},{5,1},{6,2},{7,3},{8,12},{9,13},{10,... | collective-permute-start | bytes 86024 | tf_op jit(solution)/shard_map/ppermute | solution.py:214
  59.6 0.4 collective-permute-start.27
  60.0 0.1 collective-permute-done.37
  60.1 0.6 add_convert_fusion.10
  60.7 1.0 %collective-permute-done.26 = bf16[8,1792]{1,0:T(8,128)(2,1)S(1)} collective-permute-done((bf16[8,1792]{1,0:T(8,128)(2,1)S(1)}, bf16[8,1792]{1,0:T(8,128)(2,1)S(1)}, u32[]{:S(2)}, u32[]{:S(2)}) %collective-permute-start.26) | collective-permute-done | bytes 28704 | tf_op jit(solution)/shard_map/ppermute | solution.py:214
  61.7 3.6 %collective-permute-done.27 = bf16[8,1792]{1,0:T(8,128)(2,1)S(1)} collective-permute-done((bf16[8,1792]{1,0:T(8,128)(2,1)S(1)}, bf16[8,1792]{1,0:T(8,128)(2,1)S(1)}, u32[]{:S(2)}, u32[]{:S(2)}) %collective-permute-start.27) | collective-permute-done | bytes 28704 | tf_op jit(solution)/shard_map/ppermute | solution.py:214
  65.3 0.6 add_convert_fusion.11
  (49 shorter events, 0.3 us)
Async XLA Ops:
  0.6 24.5 %copy-start = (bf16[1,1280,3584]{2,1,0:T(8,128)(2,1)S(1)}, bf16[1,1280,3584]{2,1,0:T(8,128)(2,1)}, u32[]{:S(2)}) copy-start(bf16[1,1280,3584]{2,1,0:T(8,128)(2,1)} %param.19) | copy-start | bytes 27525124
  0.6 24.5 %copy-start.1 = (bf16[1,1280,3584]{2,1,0:T(8,128)(2,1)S(1)}, bf16[1,1280,3584]{2,1,0:T(8,128)(2,1)}, u32[]{:S(2)}) copy-start(bf16[1,1280,3584]{2,1,0:T(8,128)(2,1)} %param.20) | copy-start | bytes 27525124
  0.7 24.5 %copy-start.2 = (bf16[1,1280,3584]{2,1,0:T(8,128)(2,1)S(1)}, bf16[1,1280,3584]{2,1,0:T(8,128)(2,1)}, u32[]{:S(2)}) copy-start(bf16[1,1280,3584]{2,1,0:T(8,128)(2,1)} %param.21) | copy-start | bytes 27525124
  0.7 24.5 %copy-start.3 = (bf16[1,128,1280]{2,1,0:T(8,128)(2,1)S(1)}, bf16[1,128,1280]{2,1,0:T(8,128)(2,1)}, u32[]{:S(2)}) copy-start(bf16[1,128,1280]{2,1,0:T(8,128)(2,1)} %param.17) | copy-start | bytes 983044
  0.7 24.5 %copy-start.4 = (bf16[1,128,1280]{2,1,0:T(8,128)(2,1)S(1)}, bf16[1,128,1280]{2,1,0:T(8,128)(2,1)}, u32[]{:S(2)}) copy-start(bf16[1,128,1280]{2,1,0:T(8,128)(2,1)} %param.18) | copy-start | bytes 983044
  1.8 6.3 %collective-permute-start.3 = (bf16[1,8,1920]{2,1,0:T(8,128)(2,1)S(1)}, bf16[1,8,1920]{2,1,0:T(8,128)(2,1)S(1)}, u32[]{:S(2)}, u32[]{:S(2)}) collective-permute-start(bf16[1,8,1920]{2,1,0:T(8,128)(2,1)S(1)} %bitcast.24), channel_id=1, source_target_pairs={{0,8},{1,9},{2,10},{3,11},{4,12},{5,13},{6,14},{7,15},{8,0},{9,1},... | collective-permute-start | bytes 92168 | tf_op jit(solution)/shard_map/ppermute | solution.py:214
  8.1 4.6 %collective-permute-start.4 = (bf16[2,8,1920]{2,1,0:T(8,128)(2,1)S(1)}, bf16[2,8,1920]{2,1,0:T(8,128)(2,1)S(1)}, u32[]{:S(2)}, u32[]{:S(2)}) collective-permute-start(bf16[2,8,1920]{2,1,0:T(8,128)(2,1)S(1)} %pad_maximum_fusion.1), channel_id=1, source_target_pairs={{0,4},{1,5},{2,6},{3,7},{4,0},{5,1},{6,2},{7,3},{8,12},{9,13},{10,... | collective-permute-start | bytes 184328 | tf_op jit(solution)/shard_map/ppermute | solution.py:214
  9.8 6.6 %collective-permute-start = (bf16[1,8,1920]{2,1,0:T(8,128)(2,1)S(1)}, bf16[1,8,1920]{2,1,0:T(8,128)(2,1)S(1)}, u32[]{:S(2)}, u32[]{:S(2)}) collective-permute-start(bf16[1,8,1920]{2,1,0:T(8,128)(2,1)S(1)} %bitcast.21), channel_id=1, source_target_pairs={{0,8},{1,9},{2,10},{3,11},{4,12},{5,13},{6,14},{7,15},{8,0},{9,1},... | collective-permute-start | bytes 92168 | tf_op jit(solution)/shard_map/ppermute | solution.py:214
  12.8 5.4 %collective-permute-start.6 = (bf16[32,1920]{1,0:T(8,128)(2,1)S(1)}, bf16[32,1920]{1,0:T(8,128)(2,1)S(1)}, u32[]{:S(2)}, u32[]{:S(2)}) collective-permute-start(bf16[32,1920]{1,0:T(8,128)(2,1)S(1)} %maximum_bitcast_fusion.1.refs_0_), channel_id=1, source_target_pairs={{0,2},{1,3},{2,0},{3,1},{4,6},{5,7},{6,4},{7,5},{8,10},{9,11},{10,... | collective-permute-start | bytes 368648 | tf_op jit(solution)/shard_map/ppermute | solution.py:214
  14.4 5.9 %collective-permute-start.7 = (bf16[32,1920]{1,0:T(8,128)(2,1)S(1)}, bf16[32,1920]{1,0:T(8,128)(2,1)S(1)}, u32[]{:S(2)}, u32[]{:S(2)}) collective-permute-start(bf16[32,1920]{1,0:T(8,128)(2,1)S(1)} %maximum_bitcast_fusion.1.refs_0_), channel_id=1, source_target_pairs={{0,18},{1,19},{2,16},{3,17},{4,22},{5,23},{6,20},{7,21},{8,26},{9,... | collective-permute-start | bytes 368648 | tf_op jit(solution)/shard_map/ppermute | solution.py:214
  15.9 5.6 %collective-permute-start.5 = (bf16[32,1920]{1,0:T(8,128)(2,1)S(1)}, bf16[32,1920]{1,0:T(8,128)(2,1)S(1)}, u32[]{:S(2)}, u32[]{:S(2)}) collective-permute-start(bf16[32,1920]{1,0:T(8,128)(2,1)S(1)} %maximum_bitcast_fusion.1.refs_0_), channel_id=1, source_target_pairs={{0,16},{1,17},{2,18},{3,19},{4,20},{5,21},{6,22},{7,23},{8,24},{9,... | collective-permute-start | bytes 368648 | tf_op jit(solution)/shard_map/ppermute | solution.py:214
  16.4 5.2 %collective-permute-start.1 = (bf16[2,8,1920]{2,1,0:T(8,128)(2,1)S(1)}, bf16[2,8,1920]{2,1,0:T(8,128)(2,1)S(1)}, u32[]{:S(2)}, u32[]{:S(2)}) collective-permute-start(bf16[2,8,1920]{2,1,0:T(8,128)(2,1)S(1)} %pad_maximum_fusion), channel_id=1, source_target_pairs={{0,4},{1,5},{2,6},{3,7},{4,0},{5,1},{6,2},{7,3},{8,12},{9,13},{10,... | collective-permute-start | bytes 184328 | tf_op jit(solution)/shard_map/ppermute | solution.py:214
  18.0 5.3 %collective-permute-start.8 = (bf16[32,1920]{1,0:T(8,128)(2,1)S(1)}, bf16[32,1920]{1,0:T(8,128)(2,1)S(1)}, u32[]{:S(2)}, u32[]{:S(2)}) collective-permute-start(bf16[32,1920]{1,0:T(8,128)(2,1)S(1)} %maximum_bitcast_fusion.1.refs_0_), channel_id=1, source_target_pairs={{0,1},{1,0},{2,3},{3,2},{4,5},{5,4},{6,7},{7,6},{8,9},{9,8},{10,11... | collective-permute-start | bytes 368648 | tf_op jit(solution)/shard_map/ppermute | solution.py:214
  18.2 5.9 %collective-permute-start.10 = (bf16[32,1920]{1,0:T(8,128)(2,1)S(1)}, bf16[32,1920]{1,0:T(8,128)(2,1)S(1)}, u32[]{:S(2)}, u32[]{:S(2)}) collective-permute-start(bf16[32,1920]{1,0:T(8,128)(2,1)S(1)} %collective-permute-done.6.refs_2_), channel_id=1, source_target_pairs={{0,1},{1,0},{2,3},{3,2},{4,5},{5,4},{6,7},{7,6},{8,9},{9,8},{10,11... | collective-permute-start | bytes 368648 | tf_op jit(solution)/shard_map/ppermute | solution.py:214
  20.3 4.8 %collective-permute-start.11 = (bf16[32,1920]{1,0:T(8,128)(2,1)S(1)}, bf16[32,1920]{1,0:T(8,128)(2,1)S(1)}, u32[]{:S(2)}, u32[]{:S(2)}) collective-permute-start(bf16[32,1920]{1,0:T(8,128)(2,1)S(1)} %collective-permute-done.7.refs_3_), channel_id=1, source_target_pairs={{0,1},{1,0},{2,3},{3,2},{4,5},{5,4},{6,7},{7,6},{8,9},{9,8},{10,11... | collective-permute-start | bytes 368648 | tf_op jit(solution)/shard_map/ppermute | solution.py:214
  21.5 3.6 %collective-permute-start.9 = (bf16[32,1920]{1,0:T(8,128)(2,1)S(1)}, bf16[32,1920]{1,0:T(8,128)(2,1)S(1)}, u32[]{:S(2)}, u32[]{:S(2)}) collective-permute-start(bf16[32,1920]{1,0:T(8,128)(2,1)S(1)} %collective-permute-done.5.refs_1_), channel_id=1, source_target_pairs={{0,1},{1,0},{2,3},{3,2},{4,5},{5,4},{6,7},{7,6},{8,9},{9,8},{10,11... | collective-permute-start | bytes 368648 | tf_op jit(solution)/shard_map/ppermute | solution.py:214
  21.5 10.6 %collective-permute-start.13 = (bf16[32,1920]{1,0:T(8,128)(2,1)S(1)}, bf16[32,1920]{1,0:T(8,128)(2,1)S(1)}, u32[]{:S(2)}, u32[]{:S(2)}) collective-permute-start(bf16[32,1920]{1,0:T(8,128)(2,1)S(1)} %maximum_bitcast_fusion.refs_0_), channel_id=1, source_target_pairs={{0,18},{1,19},{2,16},{3,17},{4,22},{5,23},{6,20},{7,21},{8,26},{9,... | collective-permute-start | bytes 368648 | tf_op jit(solution)/shard_map/ppermute | solution.py:214
  23.3 9.0 %collective-permute-start.12 = (bf16[32,1920]{1,0:T(8,128)(2,1)S(1)}, bf16[32,1920]{1,0:T(8,128)(2,1)S(1)}, u32[]{:S(2)}, u32[]{:S(2)}) collective-permute-start(bf16[32,1920]{1,0:T(8,128)(2,1)S(1)} %maximum_bitcast_fusion.refs_0_), channel_id=1, source_target_pairs={{0,2},{1,3},{2,0},{3,1},{4,6},{5,7},{6,4},{7,5},{8,10},{9,11},{10,... | collective-permute-start | bytes 368648 | tf_op jit(solution)/shard_map/ppermute | solution.py:214
  24.1 8.6 %collective-permute-start.2 = (bf16[32,1920]{1,0:T(8,128)(2,1)S(1)}, bf16[32,1920]{1,0:T(8,128)(2,1)S(1)}, u32[]{:S(2)}, u32[]{:S(2)}) collective-permute-start(bf16[32,1920]{1,0:T(8,128)(2,1)S(1)} %maximum_bitcast_fusion.refs_0_), channel_id=1, source_target_pairs={{0,16},{1,17},{2,18},{3,19},{4,20},{5,21},{6,22},{7,23},{8,24},{9,... | collective-permute-start | bytes 368648 | tf_op jit(solution)/shard_map/ppermute | solution.py:214
  31.6 1.4 %collective-permute-start.29 = (bf16[32,1792]{1,0:T(8,128)(2,1)S(1)}, bf16[32,1792]{1,0:T(8,128)(2,1)S(1)}, u32[]{:S(2)}, u32[]{:S(2)}) collective-permute-start(bf16[32,1792]{1,0:T(8,128)(2,1)S(1)} %get-tuple-element.43), channel_id=1, source_target_pairs={{0,1},{1,0},{2,3},{3,2},{4,5},{5,4},{6,7},{7,6},{8,9},{9,8},{10,11... | collective-permute-start | bytes 344072 | tf_op jit(solution)/shard_map/ppermute | solution.py:214
  31.6 2.5 %collective-permute-start.14 = (bf16[32,1920]{1,0:T(8,128)(2,1)S(1)}, bf16[32,1920]{1,0:T(8,128)(2,1)S(1)}, u32[]{:S(2)}, u32[]{:S(2)}) collective-permute-start(bf16[32,1920]{1,0:T(8,128)(2,1)S(1)} %maximum_bitcast_fusion.refs_0_), channel_id=1, source_target_pairs={{0,1},{1,0},{2,3},{3,2},{4,5},{5,4},{6,7},{7,6},{8,9},{9,8},{10,11... | collective-permute-start | bytes 368648 | tf_op jit(solution)/shard_map/ppermute | solution.py:214
  32.1 1.3 %collective-permute-start.31 = (bf16[32,1792]{1,0:T(8,128)(2,1)S(1)}, bf16[32,1792]{1,0:T(8,128)(2,1)S(1)}, u32[]{:S(2)}, u32[]{:S(2)}) collective-permute-start(bf16[32,1792]{1,0:T(8,128)(2,1)S(1)} %get-tuple-element.45), channel_id=1, source_target_pairs={{0,1},{1,0},{2,3},{3,2},{4,5},{5,4},{6,7},{7,6},{8,9},{9,8},{10,11... | collective-permute-start | bytes 344072 | tf_op jit(solution)/shard_map/ppermute | solution.py:214
  32.2 1.5 %collective-permute-start.33 = (bf16[32,1792]{1,0:T(8,128)(2,1)S(1)}, bf16[32,1792]{1,0:T(8,128)(2,1)S(1)}, u32[]{:S(2)}, u32[]{:S(2)}) collective-permute-start(bf16[32,1792]{1,0:T(8,128)(2,1)S(1)} %get-tuple-element.47), channel_id=1, source_target_pairs={{0,1},{1,0},{2,3},{3,2},{4,5},{5,4},{6,7},{7,6},{8,9},{9,8},{10,11... | collective-permute-start | bytes 344072 | tf_op jit(solution)/shard_map/ppermute | solution.py:214
  32.7 12.5 %collective-permute-start.28 = (bf16[32,1792]{1,0:T(8,128)(2,1)S(1)}, bf16[32,1792]{1,0:T(8,128)(2,1)S(1)}, u32[]{:S(2)}, u32[]{:S(2)}) collective-permute-start(bf16[32,1792]{1,0:T(8,128)(2,1)S(1)} %get-tuple-element.41), channel_id=1, source_target_pairs={{0,1},{1,0},{2,3},{3,2},{4,5},{5,4},{6,7},{7,6},{8,9},{9,8},{10,11... | collective-permute-start | bytes 344072 | tf_op jit(solution)/shard_map/ppermute | solution.py:214
  33.0 2.3 %collective-permute-start.17 = (bf16[32,1920]{1,0:T(8,128)(2,1)S(1)}, bf16[32,1920]{1,0:T(8,128)(2,1)S(1)}, u32[]{:S(2)}, u32[]{:S(2)}) collective-permute-start(bf16[32,1920]{1,0:T(8,128)(2,1)S(1)} %collective-permute-done.13.refs_3_), channel_id=1, source_target_pairs={{0,1},{1,0},{2,3},{3,2},{4,5},{5,4},{6,7},{7,6},{8,9},{9,8},{10,11... | collective-permute-start | bytes 368648 | tf_op jit(solution)/shard_map/ppermute | solution.py:214
  33.5 3.0 %collective-permute-start.16 = (bf16[32,1920]{1,0:T(8,128)(2,1)S(1)}, bf16[32,1920]{1,0:T(8,128)(2,1)S(1)}, u32[]{:S(2)}, u32[]{:S(2)}) collective-permute-start(bf16[32,1920]{1,0:T(8,128)(2,1)S(1)} %collective-permute-done.12.refs_2_), channel_id=1, source_target_pairs={{0,1},{1,0},{2,3},{3,2},{4,5},{5,4},{6,7},{7,6},{8,9},{9,8},{10,11... | collective-permute-start | bytes 368648 | tf_op jit(solution)/shard_map/ppermute | solution.py:214
  33.7 4.0 %collective-permute-start.15 = (bf16[32,1920]{1,0:T(8,128)(2,1)S(1)}, bf16[32,1920]{1,0:T(8,128)(2,1)S(1)}, u32[]{:S(2)}, u32[]{:S(2)}) collective-permute-start(bf16[32,1920]{1,0:T(8,128)(2,1)S(1)} %collective-permute-done.2.refs_1_), channel_id=1, source_target_pairs={{0,1},{1,0},{2,3},{3,2},{4,5},{5,4},{6,7},{7,6},{8,9},{9,8},{10,11... | collective-permute-start | bytes 368648 | tf_op jit(solution)/shard_map/ppermute | solution.py:214
  34.1 9.5 %slice-start = ((s8[9175040]{0:T(1024)(128)(4,1)}), s8[4194304]{0:T(1024)(128)(4,1)S(1)}, s32[]{:S(2)}) async-start(s8[9175040]{0:T(1024)(128)(4,1)} %bitcast.16), calls=%async_computation | async-start | bytes 8388608
  34.1 9.5 %slice-start.1 = ((s8[9175040]{0:T(1024)(128)(4,1)}), s8[4194304]{0:T(1024)(128)(4,1)S(1)}, s32[]{:S(2)}) async-start(s8[9175040]{0:T(1024)(128)(4,1)} %bitcast.16), calls=%async_computation.1 | async-start | bytes 8388608
  34.1 9.5 %slice-start.2 = ((s8[9175040]{0:T(1024)(128)(4,1)}), s8[786432]{0:T(1024)(128)(4,1)S(1)}, s32[]{:S(2)}) async-start(s8[9175040]{0:T(1024)(128)(4,1)} %bitcast.16), calls=%async_computation.2 | async-start | bytes 1572864
  34.2 11.5 %collective-permute-start.30 = (bf16[32,1792]{1,0:T(8,128)(2,1)S(1)}, bf16[32,1792]{1,0:T(8,128)(2,1)S(1)}, u32[]{:S(2)}, u32[]{:S(2)}) collective-permute-start(bf16[32,1792]{1,0:T(8,128)(2,1)S(1)} %add_convert_fusion.3), channel_id=1, source_target_pairs={{0,16},{1,17},{2,18},{3,19},{4,20},{5,21},{6,22},{7,23},{8,24},{9,... | collective-permute-start | bytes 344072 | tf_op jit(solution)/shard_map/ppermute | solution.py:214
  35.3 10.4 %collective-permute-start.32 = (bf16[32,1792]{1,0:T(8,128)(2,1)S(1)}, bf16[32,1792]{1,0:T(8,128)(2,1)S(1)}, u32[]{:S(2)}, u32[]{:S(2)}) collective-permute-start(bf16[32,1792]{1,0:T(8,128)(2,1)S(1)} %add_convert_fusion.2), channel_id=1, source_target_pairs={{0,2},{1,3},{2,0},{3,1},{4,6},{5,7},{6,4},{7,5},{8,10},{9,11},{10,... | collective-permute-start | bytes 344072 | tf_op jit(solution)/shard_map/ppermute | solution.py:214
  36.5 9.7 %collective-permute-start.34 = (bf16[32,1792]{1,0:T(8,128)(2,1)S(1)}, bf16[32,1792]{1,0:T(8,128)(2,1)S(1)}, u32[]{:S(2)}, u32[]{:S(2)}) collective-permute-start(bf16[32,1792]{1,0:T(8,128)(2,1)S(1)} %add_convert_fusion.1), channel_id=1, source_target_pairs={{0,18},{1,19},{2,16},{3,17},{4,22},{5,23},{6,20},{7,21},{8,26},{9,... | collective-permute-start | bytes 344072 | tf_op jit(solution)/shard_map/ppermute | solution.py:214
  45.0 1.4 %collective-permute-start.19 = (bf16[32,1792]{1,0:T(8,128)(2,1)S(1)}, bf16[32,1792]{1,0:T(8,128)(2,1)S(1)}, u32[]{:S(2)}, u32[]{:S(2)}) collective-permute-start(bf16[32,1792]{1,0:T(8,128)(2,1)S(1)} %get-tuple-element.36), channel_id=1, source_target_pairs={{0,1},{1,0},{2,3},{3,2},{4,5},{5,4},{6,7},{7,6},{8,9},{9,8},{10,11... | collective-permute-start | bytes 344072 | tf_op jit(solution)/shard_map/ppermute | solution.py:214
  45.1 2.5 %collective-permute-start.21 = (bf16[32,1792]{1,0:T(8,128)(2,1)S(1)}, bf16[32,1792]{1,0:T(8,128)(2,1)S(1)}, u32[]{:S(2)}, u32[]{:S(2)}) collective-permute-start(bf16[32,1792]{1,0:T(8,128)(2,1)S(1)} %get-tuple-element.38), channel_id=1, source_target_pairs={{0,1},{1,0},{2,3},{3,2},{4,5},{5,4},{6,7},{7,6},{8,9},{9,8},{10,11... | collective-permute-start | bytes 344072 | tf_op jit(solution)/shard_map/ppermute | solution.py:214
  45.6 3.3 %collective-permute-start.23 = (bf16[32,1792]{1,0:T(8,128)(2,1)S(1)}, bf16[32,1792]{1,0:T(8,128)(2,1)S(1)}, u32[]{:S(2)}, u32[]{:S(2)}) collective-permute-start(bf16[32,1792]{1,0:T(8,128)(2,1)S(1)} %get-tuple-element.40), channel_id=1, source_target_pairs={{0,1},{1,0},{2,3},{3,2},{4,5},{5,4},{6,7},{7,6},{8,9},{9,8},{10,11... | collective-permute-start | bytes 344072 | tf_op jit(solution)/shard_map/ppermute | solution.py:214
  45.7 6.7 %collective-permute-start.18 = (bf16[32,1792]{1,0:T(8,128)(2,1)S(1)}, bf16[32,1792]{1,0:T(8,128)(2,1)S(1)}, u32[]{:S(2)}, u32[]{:S(2)}) collective-permute-start(bf16[32,1792]{1,0:T(8,128)(2,1)S(1)} %get-tuple-element.34), channel_id=1, source_target_pairs={{0,1},{1,0},{2,3},{3,2},{4,5},{5,4},{6,7},{7,6},{8,9},{9,8},{10,11... | collective-permute-start | bytes 344072 | tf_op jit(solution)/shard_map/ppermute | solution.py:214
  46.5 7.8 %collective-permute-start.20 = (bf16[32,1792]{1,0:T(8,128)(2,1)S(1)}, bf16[32,1792]{1,0:T(8,128)(2,1)S(1)}, u32[]{:S(2)}, u32[]{:S(2)}) collective-permute-start(bf16[32,1792]{1,0:T(8,128)(2,1)S(1)} %add_convert_fusion.8), channel_id=1, source_target_pairs={{0,16},{1,17},{2,18},{3,19},{4,20},{5,21},{6,22},{7,23},{8,24},{9,... | collective-permute-start | bytes 344072 | tf_op jit(solution)/shard_map/ppermute | solution.py:214
  47.6 7.5 %collective-permute-start.22 = (bf16[32,1792]{1,0:T(8,128)(2,1)S(1)}, bf16[32,1792]{1,0:T(8,128)(2,1)S(1)}, u32[]{:S(2)}, u32[]{:S(2)}) collective-permute-start(bf16[32,1792]{1,0:T(8,128)(2,1)S(1)} %add_convert_fusion.7), channel_id=1, source_target_pairs={{0,2},{1,3},{2,0},{3,1},{4,6},{5,7},{6,4},{7,5},{8,10},{9,11},{10,... | collective-permute-start | bytes 344072 | tf_op jit(solution)/shard_map/ppermute | solution.py:214
  48.9 6.6 %collective-permute-start.24 = (bf16[32,1792]{1,0:T(8,128)(2,1)S(1)}, bf16[32,1792]{1,0:T(8,128)(2,1)S(1)}, u32[]{:S(2)}, u32[]{:S(2)}) collective-permute-start(bf16[32,1792]{1,0:T(8,128)(2,1)S(1)} %add_convert_fusion.6), channel_id=1, source_target_pairs={{0,18},{1,19},{2,16},{3,17},{4,22},{5,23},{6,20},{7,21},{8,26},{9,... | collective-permute-start | bytes 344072 | tf_op jit(solution)/shard_map/ppermute | solution.py:214
  50.2 9.4 %collective-permute-start.35 = (bf16[8,1792]{1,0:T(8,128)(2,1)S(1)}, bf16[8,1792]{1,0:T(8,128)(2,1)S(1)}, u32[]{:S(2)}, u32[]{:S(2)}) collective-permute-start(bf16[8,1792]{1,0:T(8,128)(2,1)S(1)} %get-tuple-element.48), channel_id=1, source_target_pairs={{0,8},{1,9},{2,10},{3,11},{4,12},{5,13},{6,14},{7,15},{8,0},{9,1},... | collective-permute-start | bytes 86024 | tf_op jit(solution)/shard_map/ppermute | solution.py:214
  52.4 7.6 %collective-permute-start.36 = (bf16[8,1792]{1,0:T(8,128)(2,1)S(1)}, bf16[8,1792]{1,0:T(8,128)(2,1)S(1)}, u32[]{:S(2)}, u32[]{:S(2)}) collective-permute-start(bf16[8,1792]{1,0:T(8,128)(2,1)S(1)} %get-tuple-element.50), channel_id=1, source_target_pairs={{0,4},{1,5},{2,6},{3,7},{4,0},{5,1},{6,2},{7,3},{8,12},{9,13},{10,... | collective-permute-start | bytes 86024 | tf_op jit(solution)/shard_map/ppermute | solution.py:214
  54.2 5.9 %collective-permute-start.37 = (bf16[8,1792]{1,0:T(8,128)(2,1)S(1)}, bf16[8,1792]{1,0:T(8,128)(2,1)S(1)}, u32[]{:S(2)}, u32[]{:S(2)}) collective-permute-start(bf16[8,1792]{1,0:T(8,128)(2,1)S(1)} %get-tuple-element.49), channel_id=1, source_target_pairs={{0,12},{1,13},{2,14},{3,15},{4,8},{5,9},{6,10},{7,11},{8,4},{9,5},... | collective-permute-start | bytes 86024 | tf_op jit(solution)/shard_map/ppermute | solution.py:214
  55.6 5.2 %collective-permute-start.25 = (bf16[8,1792]{1,0:T(8,128)(2,1)S(1)}, bf16[8,1792]{1,0:T(8,128)(2,1)S(1)}, u32[]{:S(2)}, u32[]{:S(2)}) collective-permute-start(bf16[8,1792]{1,0:T(8,128)(2,1)S(1)} %get-tuple-element.51), channel_id=1, source_target_pairs={{0,8},{1,9},{2,10},{3,11},{4,12},{5,13},{6,14},{7,15},{8,0},{9,1},... | collective-permute-start | bytes 86024 | tf_op jit(solution)/shard_map/ppermute | solution.py:214
  57.8 3.9 %collective-permute-start.26 = (bf16[8,1792]{1,0:T(8,128)(2,1)S(1)}, bf16[8,1792]{1,0:T(8,128)(2,1)S(1)}, u32[]{:S(2)}, u32[]{:S(2)}) collective-permute-start(bf16[8,1792]{1,0:T(8,128)(2,1)S(1)} %get-tuple-element.53), channel_id=1, source_target_pairs={{0,4},{1,5},{2,6},{3,7},{4,0},{5,1},{6,2},{7,3},{8,12},{9,13},{10,... | collective-permute-start | bytes 86024 | tf_op jit(solution)/shard_map/ppermute | solution.py:214
  59.6 5.7 %collective-permute-start.27 = (bf16[8,1792]{1,0:T(8,128)(2,1)S(1)}, bf16[8,1792]{1,0:T(8,128)(2,1)S(1)}, u32[]{:S(2)}, u32[]{:S(2)}) collective-permute-start(bf16[8,1792]{1,0:T(8,128)(2,1)S(1)} %get-tuple-element.52), channel_id=1, source_target_pairs={{0,12},{1,13},{2,14},{3,15},{4,8},{5,9},{6,10},{7,11},{8,4},{9,5},... | collective-permute-start | bytes 86024 | tf_op jit(solution)/shard_map/ppermute | solution.py:214

commit v3 on v2

--- a/solution.py
+++ b/solution.py
@@ -110,10 +110,10 @@
     meta = load_rows(groups, sections, width, pieces, held)
     me = lax.axis_index("expert")
     scale[...] = field_of(meta, me) + field_of(meta, me + experts)
-    for at, size in chunks(hidden.shape[1], 256):
-        g = last_last(held[...], gate[at : at + size, :])
-        u = last_last(held[...], up[at : at + size, :])
-        hidden[:, at : at + size] = (g / (1.0 + jnp.exp(-g)) * u).astype(jnp.bfloat16)
+    for at, size in chunks(hidden.shape[1], 128):
+        g = last_last(gate[at : at + size, :], held[...])
+        u = last_last(up[at : at + size, :], held[...])
+        hidden[:, at : at + size] = (g / (1.0 + jnp.exp(-g)) * u).T.astype(jnp.bfloat16)
 
 
 def down_kernel(groups, sections, width, hidden, scale, down, *outs):
@@ -143,9 +143,9 @@
     slot = jnp.where(weight > 0.0, slot, -1)
     place = lax.broadcasted_iota(jnp.int32, (held.shape[0], gate_saved.shape[0]), 1)
     pick = jnp.where(place == slot, 1.0, 0.0).astype(jnp.bfloat16)
-    for at, size in chunks(grad_gate.shape[1], 256):
+    for at, size in chunks(grad_gate.shape[1], 128):
         part = slice(at, at + size)
-        grad = last_last(held[...], down[part, :]) * weight
+        grad = last_last(down[part, :], held[...]).T * weight
         g = last_first(pick, gate_saved[:, part])
         u = last_first(pick, up_saved[:, part])
         q = 1.0 / (1.0 + jnp.exp(-g))
@@ -230,12 +230,17 @@
     return held.reshape(4 * tokens, cols)
 
 
+def spread_shot(message):
+    parts = [move(message, mask, 32) for mask in Z[::-1]][::-1]
+    return jnp.concatenate([message, *parts], axis=0)
+
+
 def spread_plane(held):
     return [held, move(held, Y, 32), move(held, X, 32), move(held, X ^ Y, 32)]
 
 
 def swap(pieces):
-    return [move(p, CORE, 32) for p in pieces]
+    return [move(p, CORE, 32) for p in pieces[::-1]][::-1]
 
 
 def add(*parts):
@@ -243,12 +248,12 @@
 
 
 def collect_plane(own):
-    return add(own[0], move(own[1], Y, 32), move(own[2], X, 32), move(own[3], X ^ Y, 32))
+    return add(own[0], move(own[3], X ^ Y, 32), move(own[1], Y, 32), move(own[2], X, 32))
 
 
 def collect_line(total, tokens):
     rows = [total[k * tokens : (k + 1) * tokens] for k in range(4)]
-    return add(rows[0], *[move(rows[k + 1], Z[k], 32) for k in range(3)])
+    return add(rows[0], *[move(rows[k + 1], Z[k], 32) for k in (2,1,0)])
 
 
 def spread_any(message, width):
@@ -282,7 +287,7 @@
         done_b = experts_backward(pieces_b, 1, whole, expert_count, capacity, tokens, None, stash, weights)
         return collect_any(done_f), collect_any(done_b)
     order = [c ^ x ^ z for c in (0, CORE) for x in (0, X) for z in (0, *Z)]
-    line_b, line_f = spread_line(message_b), spread_line(message_f)
+    line_b, line_f = spread_shot(message_b), spread_line(message_f)
     plane_b = spread_plane(line_b)
     plane_f = spread_plane(line_f)
     pieces_b = plane_b + swap(plane_b)
@@ -291,7 +296,6 @@
     pieces_f = plane_f + swap(plane_f)
     hidden, scale = forward_hidden(pieces_f, 2, width, expert_count, weights[:2])
     own_b = [add(a, b) for a, b in zip(done_b[:4], swap(done_b[4:]))]
-    done_f0 = None
     done_f = forward_down(pieces_f, 2, width, hidden, scale, weights[2])
     own_f = [add(a, b) for a, b in zip(done_f[:4], swap(done_f[4:]))]
     return collect_line(collect_plane(own_f), tokens), collect_line(collect_plane(own_b), tokens)

time: 66.1 us -> 61.3 us (0.927)
  starting transfers between devices: 37.2 us -> 31.6 us
  waiting for transfers between devices: 11.3 us -> 14 us
  Pallas kernels: 14.8 us -> 13 us
    ppermute x38 -> x39, starting transfers between devices: 37.2 us -> 31.6 us  [move(): return lax.ppermute(value, AXES, [(i, i ^ mask) for i in range(devices)])]
    ppermute x38 -> x39, waiting for transfers between devices: 11.3 us -> 14 us  [move(): return lax.ppermute(value, AXES, [(i, i ^ mask) for i in range(devices)])]
    pallas_call x3, Pallas kernels: 13.7 us -> 11.8 us  [expert_call(): pl.pallas_call(kernel, out_shape=shapes, scratch_shapes=scratch, compiler...]
  transfers between devices with their start and end apart: 38 -> 39, of which waited for: 12 -> 12; matrix products, arithmetic and copies ran while one was open for 2% -> 2% of each run, Pallas kernels for 21% -> 19%
where the time goes in v3:
time: 61.3 us; the launch traced here: 61.1 us
  starting transfers between devices  31.6 us (52%)
  waiting for transfers between devices  14 us (23%)
  Pallas kernels  13 us (21%)
  other arithmetic  1.61 us (3%)
  between operations  0.92 us (2%)
    ppermute x39, starting transfers between devices, move(): return lax.ppermute(value, AXES, [(i, i ^ mask) for i in range(devices)])  31.6 us
    ppermute x39, waiting for transfers between devices, move(): return lax.ppermute(value, AXES, [(i, i ^ mask) for i in range(devices)])  14 us
    pallas_call x3, Pallas kernels, expert_call(): pl.pallas_call(kernel, out_shape=shapes, scratch_shapes=scratch, compiler...  11.8 us
    convert_element_type x10, other arithmetic, add(): return sum((p.astype(jnp.float32) for p in parts)).astype(jnp.bfloat16)  1.58 us
  transfers between devices with their start and end apart: 39, of which 12 were waited for; matrix products, arithmetic and copies ran while one was open for 2% of the time, Pallas kernels for 19%

profile of v3, /device:TPU:0, one launch (start us, length us, event | category | flops | bytes accessed | tf_op | source)
XLA Modules:
  0.0 61.1 jit_solution(3656024743914258993)
XLA Ops:
  0.7 0.0 copy-start.2
  0.7 1.1 %pack.1 = (bf16[8,1920]{1,0:T(8,128)(2,1)S(1)}, bf16[8,1920]{1,0:T(8,128)(2,1)S(1)}) custom-call(bf16[8,1792]{1,0:T(8,128)(2,1)} %refs_0_.1, s32[8,8]{1,0:T(8,128)} %refs_1_.1, f32[8,8]{1,0:T(8,128)} %refs_2_.1, bf16[8,1792]{1,0:T(8,128)(2,1)} %refs_3_.1, s32[8,8]{1,0:T(8,128)} %refs_4_.1, f32[8,8]{1,0:T(8,128)} %refs_5_.1), custom_call_target="tpu_custom_call" | custom-call | flops 40000000000 | bytes 100000000 | tf_op jit(solution)/shard_map/pack/pallas_call | solution.py:57
  1.8 4.1 %collective-permute-start.3 = (bf16[8,1920]{1,0:T(8,128)(2,1)S(1)}, bf16[8,1920]{1,0:T(8,128)(2,1)S(1)}, u32[]{:S(2)}, u32[]{:S(2)}) collective-permute-start(bf16[8,1920]{1,0:T(8,128)(2,1)S(1)} %get-tuple-element.26), channel_id=1, source_target_pairs={{0,8},{1,9},{2,10},{3,11},{4,12},{5,13},{6,14},{7,15},{8,0},{9,1},... | collective-permute-start | bytes 92168 | tf_op jit(solution)/shard_map/ppermute | solution.py:214
  5.9 1.6 %collective-permute-start.4 = (bf16[8,1920]{1,0:T(8,128)(2,1)S(1)}, bf16[8,1920]{1,0:T(8,128)(2,1)S(1)}, u32[]{:S(2)}, u32[]{:S(2)}) collective-permute-start(bf16[8,1920]{1,0:T(8,128)(2,1)S(1)} %get-tuple-element.26), channel_id=1, source_target_pairs={{0,4},{1,5},{2,6},{3,7},{4,0},{5,1},{6,2},{7,3},{8,12},{9,13},{10,... | collective-permute-start | bytes 92168 | tf_op jit(solution)/shard_map/ppermute | solution.py:214
  7.5 0.0 collective-permute-start.5
  7.5 1.9 %collective-permute-start = (bf16[1,8,1920]{2,1,0:T(8,128)(2,1)S(1)}, bf16[1,8,1920]{2,1,0:T(8,128)(2,1)S(1)}, u32[]{:S(2)}, u32[]{:S(2)}) collective-permute-start(bf16[1,8,1920]{2,1,0:T(8,128)(2,1)S(1)} %bitcast.18), channel_id=1, source_target_pairs={{0,8},{1,9},{2,10},{3,11},{4,12},{5,13},{6,14},{7,15},{8,0},{9,1},... | collective-permute-start | bytes 92168 | tf_op jit(solution)/shard_map/ppermute | solution.py:214
  9.4 0.0 collective-permute-done.3
  9.4 0.4 collective-permute-done.4
  9.8 3.4 %collective-permute-done.5 = bf16[8,1920]{1,0:T(8,128)(2,1)S(1)} collective-permute-done((bf16[8,1920]{1,0:T(8,128)(2,1)S(1)}, bf16[8,1920]{1,0:T(8,128)(2,1)S(1)}, u32[]{:S(2)}, u32[]{:S(2)}) %collective-permute-start.5) | collective-permute-done | bytes 30752 | tf_op jit(solution)/shard_map/ppermute | solution.py:214
  13.2 1.5 %collective-permute-start.6 = (bf16[32,1920]{1,0:T(8,128)(2,1)S(1)}, bf16[32,1920]{1,0:T(8,128)(2,1)S(1)}, u32[]{:S(2)}, u32[]{:S(2)}) collective-permute-start(bf16[32,1920]{1,0:T(8,128)(2,1)S(1)} %constant_dynamic-update-slice_fusion.refs_0_), channel_id=1, source_target_pairs={{0,16},{1,17},{2,18},{3,19},{4,20},{5,21},{6,22},{7,23},{8,24},{9,... | collective-permute-start | bytes 368648 | tf_op jit(solution)/shard_map/ppermute | solution.py:214
  14.7 1.5 %collective-permute-start.7 = (bf16[32,1920]{1,0:T(8,128)(2,1)S(1)}, bf16[32,1920]{1,0:T(8,128)(2,1)S(1)}, u32[]{:S(2)}, u32[]{:S(2)}) collective-permute-start(bf16[32,1920]{1,0:T(8,128)(2,1)S(1)} %constant_dynamic-update-slice_fusion.refs_0_), channel_id=1, source_target_pairs={{0,2},{1,3},{2,0},{3,1},{4,6},{5,7},{6,4},{7,5},{8,10},{9,11},{10,... | collective-permute-start | bytes 368648 | tf_op jit(solution)/shard_map/ppermute | solution.py:214
  16.2 0.5 collective-permute-start.8
  16.7 0.0 collective-permute-done
  16.7 0.1 collective-permute-start.1
  16.8 0.1 collective-permute-start.9
  16.9 2.5 %collective-permute-done.6.refs_1_ = bf16[32,1920]{1,0:T(8,128)(2,1)S(1)} collective-permute-done((bf16[32,1920]{1,0:T(8,128)(2,1)S(1)}, bf16[32,1920]{1,0:T(8,128)(2,1)S(1)}, u32[]{:S(2)}, u32[]{:S(2)}) %collective-permute-start.6) | collective-permute-done | bytes 122912 | tf_op jit(solution)/shard_map/ppermute | solution.py:214
  19.4 0.0 collective-permute-start.10
  19.4 0.2 collective-permute-done.7.refs_2_
  19.6 0.3 collective-permute-start.11
  19.9 2.1 %collective-permute-done.8.refs_3_ = bf16[32,1920]{1,0:T(8,128)(2,1)S(1)} collective-permute-done((bf16[32,1920]{1,0:T(8,128)(2,1)S(1)}, bf16[32,1920]{1,0:T(8,128)(2,1)S(1)}, u32[]{:S(2)}, u32[]{:S(2)}) %collective-permute-start.8) | collective-permute-done | bytes 122912 | tf_op jit(solution)/shard_map/ppermute | solution.py:214
  22.0 0.0 collective-permute-start.12
  22.0 0.0 collective-permute-done.1
  22.0 1.5 %collective-permute-start.14 = (bf16[32,1920]{1,0:T(8,128)(2,1)S(1)}, bf16[32,1920]{1,0:T(8,128)(2,1)S(1)}, u32[]{:S(2)}, u32[]{:S(2)}) collective-permute-start(bf16[32,1920]{1,0:T(8,128)(2,1)S(1)} %maximum_bitcast_fusion.refs_0_), channel_id=1, source_target_pairs={{0,18},{1,19},{2,16},{3,17},{4,22},{5,23},{6,20},{7,21},{8,26},{9,... | collective-permute-start | bytes 368648 | tf_op jit(solution)/shard_map/ppermute | solution.py:214
  23.6 0.0 collective-permute-done.9.refs_4_
  23.6 0.5 collective-permute-start.13
  24.1 1.5 %collective-permute-start.2 = (bf16[32,1920]{1,0:T(8,128)(2,1)S(1)}, bf16[32,1920]{1,0:T(8,128)(2,1)S(1)}, u32[]{:S(2)}, u32[]{:S(2)}) collective-permute-start(bf16[32,1920]{1,0:T(8,128)(2,1)S(1)} %maximum_bitcast_fusion.refs_0_), channel_id=1, source_target_pairs={{0,16},{1,17},{2,18},{3,19},{4,20},{5,21},{6,22},{7,23},{8,24},{9,... | collective-permute-start | bytes 368648 | tf_op jit(solution)/shard_map/ppermute | solution.py:214
  25.6 5.4 %experts_backward.1 = (bf16[32,1792]{1,0:T(8,128)(2,1)S(1)}, bf16[32,1792]{1,0:T(8,128)(2,1)S(1)}, bf16[32,1792]{1,0:T(8,128)(2,1)S(1)}, bf16[32,1792]{1,0:T(8,1...) custom-call(bf16[32,1920]{1,0:T(8,128)(2,1)S(1)} %constant_dynamic-u, ...), custom_call_target="tpu_custom_call" | custom-call | flops 3523215360 | bytes 27525120 | tf_op jit(solution)/shard_map/experts_backward/pallas_call | solution.py:167
  31.0 0.1 collective-permute-start.30
  31.1 0.5 collective-permute-start.15
  31.6 0.1 collective-permute-start.32
  31.7 0.4 collective-permute-start.34
  32.1 0.1 collective-permute-start.29
  32.2 0.2 collective-permute-done.30
  32.4 0.2 collective-permute-start.18
  32.7 0.3 collective-permute-done.32
  32.9 0.2 collective-permute-start.17
  33.1 0.4 collective-permute-start.16
  33.6 0.0 slice-start.1
  33.6 1.5 %collective-permute-start.31 = (bf16[32,1792]{1,0:T(8,128)(2,1)S(1)}, bf16[32,1792]{1,0:T(8,128)(2,1)S(1)}, u32[]{:S(2)}, u32[]{:S(2)}) collective-permute-start(bf16[32,1792]{1,0:T(8,128)(2,1)S(1)} %add_convert_fusion.3), channel_id=1, source_target_pairs={{0,18},{1,19},{2,16},{3,17},{4,22},{5,23},{6,20},{7,21},{8,26},{9,... | collective-permute-start | bytes 344072 | tf_op jit(solution)/shard_map/ppermute | solution.py:214
  35.1 0.5 collective-permute-start.33
  35.7 1.5 %collective-permute-start.35 = (bf16[32,1792]{1,0:T(8,128)(2,1)S(1)}, bf16[32,1792]{1,0:T(8,128)(2,1)S(1)}, u32[]{:S(2)}, u32[]{:S(2)}) collective-permute-start(bf16[32,1792]{1,0:T(8,128)(2,1)S(1)} %add_convert_fusion.1), channel_id=1, source_target_pairs={{0,2},{1,3},{2,0},{3,1},{4,6},{5,7},{6,4},{7,5},{8,10},{9,11},{10,... | collective-permute-start | bytes 344072 | tf_op jit(solution)/shard_map/ppermute | solution.py:214
  37.2 5.1 %forward_hidden.1 = (bf16[128,1280]{1,0:T(8,128)(2,1)S(1)}, f32[128,1]{1,0:T(8,128)S(1)}) custom-call(bf16[32,1920]{1,0:T(8,128)(2,1)S(1)} %maximum_bitcast_fusion.refs_0_, bf16[32,1920]{1,0:T(8,128)(2,1)S(1)} %collective-permute-done.2.refs_1_, bf16[32,1920]{1,0:T(8,128)(2,1)S(1)} %collective-permute-done.13.refs_2_, ...), custom_call_target="tpu_custom_call" | custom-call | flops 2348810240 | bytes 18350080 | tf_op jit(solution)/shard_map/forward_hidden/pallas_call | solution.py:167
  42.3 1.4 %forward_down.1 = (bf16[32,1792]{1,0:T(8,128)(2,1)S(1)}, bf16[32,1792]{1,0:T(8,128)(2,1)S(1)}, bf16[32,1792]{1,0:T(8,128)(2,1)S(1)}, bf16[32,1792]{1,0:T(8,128)(...) custom-call(bf16[128,1280]{1,0:T(8,128)(2,1)S(1)} %get-tuple-element, ...), custom_call_target="tpu_custom_call" | custom-call | flops 1174405120 | bytes 9175040 | tf_op jit(solution)/shard_map/forward_down/pallas_call | solution.py:167
  43.7 0.1 collective-permute-start.20
  43.8 0.5 collective-permute-start.22
  44.3 0.1 collective-permute-start.24
  44.3 0.4 collective-permute-start.19
  44.8 0.1 add_convert_fusion
  44.9 0.2 collective-permute-done.20
  45.1 1.5 %collective-permute-start.21 = (bf16[32,1792]{1,0:T(8,128)(2,1)S(1)}, bf16[32,1792]{1,0:T(8,128)(2,1)S(1)}, u32[]{:S(2)}, u32[]{:S(2)}) collective-permute-start(bf16[32,1792]{1,0:T(8,128)(2,1)S(1)} %add_convert_fusion.8), channel_id=1, source_target_pairs={{0,18},{1,19},{2,16},{3,17},{4,22},{5,23},{6,20},{7,21},{8,26},{9,... | collective-permute-start | bytes 344072 | tf_op jit(solution)/shard_map/ppermute | solution.py:214
  46.7 0.6 collective-permute-start.23
  47.3 1.6 %collective-permute-start.25 = (bf16[32,1792]{1,0:T(8,128)(2,1)S(1)}, bf16[32,1792]{1,0:T(8,128)(2,1)S(1)}, u32[]{:S(2)}, u32[]{:S(2)}) collective-permute-start(bf16[32,1792]{1,0:T(8,128)(2,1)S(1)} %add_convert_fusion.6), channel_id=1, source_target_pairs={{0,2},{1,3},{2,0},{3,1},{4,6},{5,7},{6,4},{7,5},{8,10},{9,11},{10,... | collective-permute-start | bytes 344072 | tf_op jit(solution)/shard_map/ppermute | solution.py:214
  48.9 0.6 collective-permute-start.36
  49.5 2.6 %collective-permute-done.21 = bf16[32,1792]{1,0:T(8,128)(2,1)S(1)} collective-permute-done((bf16[32,1792]{1,0:T(8,128)(2,1)S(1)}, bf16[32,1792]{1,0:T(8,128)(2,1)S(1)}, u32[]{:S(2)}, u32[]{:S(2)}) %collective-permute-start.21) | collective-permute-done | bytes 114720 | tf_op jit(solution)/shard_map/ppermute | solution.py:214
  52.1 1.2 %collective-permute-start.38 = (bf16[8,1792]{1,0:T(8,128)(2,1)S(1)}, bf16[8,1792]{1,0:T(8,128)(2,1)S(1)}, u32[]{:S(2)}, u32[]{:S(2)}) collective-permute-start(bf16[8,1792]{1,0:T(8,128)(2,1)S(1)} %get-tuple-element.49), channel_id=1, source_target_pairs={{0,8},{1,9},{2,10},{3,11},{4,12},{5,13},{6,14},{7,15},{8,0},{9,1},... | collective-permute-start | bytes 86024 | tf_op jit(solution)/shard_map/ppermute | solution.py:214
  53.3 0.5 collective-permute-done.23
  53.7 0.1 add_convert_fusion.5
  53.8 0.7 %collective-permute-start.26 = (bf16[8,1792]{1,0:T(8,128)(2,1)S(1)}, bf16[8,1792]{1,0:T(8,128)(2,1)S(1)}, u32[]{:S(2)}, u32[]{:S(2)}) collective-permute-start(bf16[8,1792]{1,0:T(8,128)(2,1)S(1)} %get-tuple-element.51), channel_id=1, source_target_pairs={{0,12},{1,13},{2,14},{3,15},{4,8},{5,9},{6,10},{7,11},{8,4},{9,5},... | collective-permute-start | bytes 86024 | tf_op jit(solution)/shard_map/ppermute | solution.py:214
  54.5 1.2 %collective-permute-start.27 = (bf16[8,1792]{1,0:T(8,128)(2,1)S(1)}, bf16[8,1792]{1,0:T(8,128)(2,1)S(1)}, u32[]{:S(2)}, u32[]{:S(2)}) collective-permute-start(bf16[8,1792]{1,0:T(8,128)(2,1)S(1)} %get-tuple-element.53), channel_id=1, source_target_pairs={{0,4},{1,5},{2,6},{3,7},{4,0},{5,1},{6,2},{7,3},{8,12},{9,13},{10,... | collective-permute-start | bytes 86024 | tf_op jit(solution)/shard_map/ppermute | solution.py:214
  55.7 2.6 %collective-permute-start.28 = (bf16[8,1792]{1,0:T(8,128)(2,1)S(1)}, bf16[8,1792]{1,0:T(8,128)(2,1)S(1)}, u32[]{:S(2)}, u32[]{:S(2)}) collective-permute-start(bf16[8,1792]{1,0:T(8,128)(2,1)S(1)} %get-tuple-element.52), channel_id=1, source_target_pairs={{0,8},{1,9},{2,10},{3,11},{4,12},{5,13},{6,14},{7,15},{8,0},{9,1},... | collective-permute-start | bytes 86024 | tf_op jit(solution)/shard_map/ppermute | solution.py:214
  58.3 0.6 %add_convert_fusion.10 = bf16[8,1792]{1,0:T(8,128)(2,1)} fusion(bf16[8,1792]{1,0:T(8,128)(2,1)S(1)} %collective-permute-done.38, bf16[8,1792]{1,0:T(8,128)(2,1)S(1)} %collective-permute-done.37, bf16[8,1792]{1,0:T(8,128)(2,1)S(1)} %collective-permute-done.36, bf16[32,1792]{1,0:T(8,128)(2,1)S(1)} %add_convert_fusion), kind=kLoop, calls=%fused_computation.12 | loop fusion | flops 114688 | bytes 143360 | tf_op jit(solution)/shard_map/convert_element_type | solution.py:247
  58.9 0.6 %collective-permute-done.26 = bf16[8,1792]{1,0:T(8,128)(2,1)S(1)} collective-permute-done((bf16[8,1792]{1,0:T(8,128)(2,1)S(1)}, bf16[8,1792]{1,0:T(8,128)(2,1)S(1)}, u32[]{:S(2)}, u32[]{:S(2)}) %collective-permute-start.26) | collective-permute-done | bytes 28704 | tf_op jit(solution)/shard_map/ppermute | solution.py:214
  59.6 0.9 %collective-permute-done.28 = bf16[8,1792]{1,0:T(8,128)(2,1)S(1)} collective-permute-done((bf16[8,1792]{1,0:T(8,128)(2,1)S(1)}, bf16[8,1792]{1,0:T(8,128)(2,1)S(1)}, u32[]{:S(2)}, u32[]{:S(2)}) %collective-permute-start.28) | collective-permute-done | bytes 28704 | tf_op jit(solution)/shard_map/ppermute | solution.py:214
  60.5 0.6 %add_convert_fusion.11 = bf16[8,1792]{1,0:T(8,128)(2,1)} fusion(bf16[8,1792]{1,0:T(8,128)(2,1)S(1)} %collective-permute-done.28, bf16[8,1792]{1,0:T(8,128)(2,1)S(1)} %collective-permute-done.27, bf16[8,1792]{1,0:T(8,128)(2,1)S(1)} %collective-permute-done.26, bf16[32,1792]{1,0:T(8,128)(2,1)S(1)} %add_convert_fusion.5), kind=kLoop, calls=%fused_computation.13 | loop fusion | flops 114688 | bytes 143360 | tf_op jit(solution)/shard_map/convert_element_type | solution.py:247
  (53 shorter events, 0.3 us)
Async XLA Ops:
  0.6 25.0 %copy-start = (bf16[1,1280,3584]{2,1,0:T(8,128)(2,1)S(1)}, bf16[1,1280,3584]{2,1,0:T(8,128)(2,1)}, u32[]{:S(2)}) copy-start(bf16[1,1280,3584]{2,1,0:T(8,128)(2,1)} %param.19) | copy-start | bytes 27525124
  0.6 25.0 %copy-start.1 = (bf16[1,1280,3584]{2,1,0:T(8,128)(2,1)S(1)}, bf16[1,1280,3584]{2,1,0:T(8,128)(2,1)}, u32[]{:S(2)}) copy-start(bf16[1,1280,3584]{2,1,0:T(8,128)(2,1)} %param.20) | copy-start | bytes 27525124
  0.7 25.0 %copy-start.2 = (bf16[1,1280,3584]{2,1,0:T(8,128)(2,1)S(1)}, bf16[1,1280,3584]{2,1,0:T(8,128)(2,1)}, u32[]{:S(2)}) copy-start(bf16[1,1280,3584]{2,1,0:T(8,128)(2,1)} %param.21) | copy-start | bytes 27525124
  0.7 25.0 %copy-start.3 = (bf16[1,128,1280]{2,1,0:T(8,128)(2,1)S(1)}, bf16[1,128,1280]{2,1,0:T(8,128)(2,1)}, u32[]{:S(2)}) copy-start(bf16[1,128,1280]{2,1,0:T(8,128)(2,1)} %param.17) | copy-start | bytes 983044
  0.7 25.0 %copy-start.4 = (bf16[1,128,1280]{2,1,0:T(8,128)(2,1)S(1)}, bf16[1,128,1280]{2,1,0:T(8,128)(2,1)}, u32[]{:S(2)}) copy-start(bf16[1,128,1280]{2,1,0:T(8,128)(2,1)} %param.18) | copy-start | bytes 983044
  1.8 7.6 %collective-permute-start.3 = (bf16[8,1920]{1,0:T(8,128)(2,1)S(1)}, bf16[8,1920]{1,0:T(8,128)(2,1)S(1)}, u32[]{:S(2)}, u32[]{:S(2)}) collective-permute-start(bf16[8,1920]{1,0:T(8,128)(2,1)S(1)} %get-tuple-element.26), channel_id=1, source_target_pairs={{0,8},{1,9},{2,10},{3,11},{4,12},{5,13},{6,14},{7,15},{8,0},{9,1},... | collective-permute-start | bytes 92168 | tf_op jit(solution)/shard_map/ppermute | solution.py:214
  5.9 3.9 %collective-permute-start.4 = (bf16[8,1920]{1,0:T(8,128)(2,1)S(1)}, bf16[8,1920]{1,0:T(8,128)(2,1)S(1)}, u32[]{:S(2)}, u32[]{:S(2)}) collective-permute-start(bf16[8,1920]{1,0:T(8,128)(2,1)S(1)} %get-tuple-element.26), channel_id=1, source_target_pairs={{0,4},{1,5},{2,6},{3,7},{4,0},{5,1},{6,2},{7,3},{8,12},{9,13},{10,... | collective-permute-start | bytes 92168 | tf_op jit(solution)/shard_map/ppermute | solution.py:214
  7.5 5.7 %collective-permute-start.5 = (bf16[8,1920]{1,0:T(8,128)(2,1)S(1)}, bf16[8,1920]{1,0:T(8,128)(2,1)S(1)}, u32[]{:S(2)}, u32[]{:S(2)}) collective-permute-start(bf16[8,1920]{1,0:T(8,128)(2,1)S(1)} %get-tuple-element.26), channel_id=1, source_target_pairs={{0,12},{1,13},{2,14},{3,15},{4,8},{5,9},{6,10},{7,11},{8,4},{9,5},... | collective-permute-start | bytes 92168 | tf_op jit(solution)/shard_map/ppermute | solution.py:214
  7.5 9.2 %collective-permute-start = (bf16[1,8,1920]{2,1,0:T(8,128)(2,1)S(1)}, bf16[1,8,1920]{2,1,0:T(8,128)(2,1)S(1)}, u32[]{:S(2)}, u32[]{:S(2)}) collective-permute-start(bf16[1,8,1920]{2,1,0:T(8,128)(2,1)S(1)} %bitcast.18), channel_id=1, source_target_pairs={{0,8},{1,9},{2,10},{3,11},{4,12},{5,13},{6,14},{7,15},{8,0},{9,1},... | collective-permute-start | bytes 92168 | tf_op jit(solution)/shard_map/ppermute | solution.py:214
  13.2 6.2 %collective-permute-start.6 = (bf16[32,1920]{1,0:T(8,128)(2,1)S(1)}, bf16[32,1920]{1,0:T(8,128)(2,1)S(1)}, u32[]{:S(2)}, u32[]{:S(2)}) collective-permute-start(bf16[32,1920]{1,0:T(8,128)(2,1)S(1)} %constant_dynamic-update-slice_fusion.refs_0_), channel_id=1, source_target_pairs={{0,16},{1,17},{2,18},{3,19},{4,20},{5,21},{6,22},{7,23},{8,24},{9,... | collective-permute-start | bytes 368648 | tf_op jit(solution)/shard_map/ppermute | solution.py:214
  14.7 4.9 %collective-permute-start.7 = (bf16[32,1920]{1,0:T(8,128)(2,1)S(1)}, bf16[32,1920]{1,0:T(8,128)(2,1)S(1)}, u32[]{:S(2)}, u32[]{:S(2)}) collective-permute-start(bf16[32,1920]{1,0:T(8,128)(2,1)S(1)} %constant_dynamic-update-slice_fusion.refs_0_), channel_id=1, source_target_pairs={{0,2},{1,3},{2,0},{3,1},{4,6},{5,7},{6,4},{7,5},{8,10},{9,11},{10,... | collective-permute-start | bytes 368648 | tf_op jit(solution)/shard_map/ppermute | solution.py:214
  16.2 5.8 %collective-permute-start.8 = (bf16[32,1920]{1,0:T(8,128)(2,1)S(1)}, bf16[32,1920]{1,0:T(8,128)(2,1)S(1)}, u32[]{:S(2)}, u32[]{:S(2)}) collective-permute-start(bf16[32,1920]{1,0:T(8,128)(2,1)S(1)} %constant_dynamic-update-slice_fusion.refs_0_), channel_id=1, source_target_pairs={{0,18},{1,19},{2,16},{3,17},{4,22},{5,23},{6,20},{7,21},{8,26},{9,... | collective-permute-start | bytes 368648 | tf_op jit(solution)/shard_map/ppermute | solution.py:214
  16.7 5.3 %collective-permute-start.1 = (bf16[2,8,1920]{2,1,0:T(8,128)(2,1)S(1)}, bf16[2,8,1920]{2,1,0:T(8,128)(2,1)S(1)}, u32[]{:S(2)}, u32[]{:S(2)}) collective-permute-start(bf16[2,8,1920]{2,1,0:T(8,128)(2,1)S(1)} %pad_maximum_fusion), channel_id=1, source_target_pairs={{0,4},{1,5},{2,6},{3,7},{4,0},{5,1},{6,2},{7,3},{8,12},{9,13},{10,... | collective-permute-start | bytes 184328 | tf_op jit(solution)/shard_map/ppermute | solution.py:214
  16.8 6.8 %collective-permute-start.9 = (bf16[32,1920]{1,0:T(8,128)(2,1)S(1)}, bf16[32,1920]{1,0:T(8,128)(2,1)S(1)}, u32[]{:S(2)}, u32[]{:S(2)}) collective-permute-start(bf16[32,1920]{1,0:T(8,128)(2,1)S(1)} %constant_dynamic-update-slice_fusion.refs_0_), channel_id=1, source_target_pairs={{0,1},{1,0},{2,3},{3,2},{4,5},{5,4},{6,7},{7,6},{8,9},{9,8},{10,11... | collective-permute-start | bytes 368648 | tf_op jit(solution)/shard_map/ppermute | solution.py:214
  19.4 4.7 %collective-permute-start.10 = (bf16[32,1920]{1,0:T(8,128)(2,1)S(1)}, bf16[32,1920]{1,0:T(8,128)(2,1)S(1)}, u32[]{:S(2)}, u32[]{:S(2)}) collective-permute-start(bf16[32,1920]{1,0:T(8,128)(2,1)S(1)} %collective-permute-done.6.refs_1_), channel_id=1, source_target_pairs={{0,1},{1,0},{2,3},{3,2},{4,5},{5,4},{6,7},{7,6},{8,9},{9,8},{10,11... | collective-permute-start | bytes 368648 | tf_op jit(solution)/shard_map/ppermute | solution.py:214
  19.6 6.0 %collective-permute-start.11 = (bf16[32,1920]{1,0:T(8,128)(2,1)S(1)}, bf16[32,1920]{1,0:T(8,128)(2,1)S(1)}, u32[]{:S(2)}, u32[]{:S(2)}) collective-permute-start(bf16[32,1920]{1,0:T(8,128)(2,1)S(1)} %collective-permute-done.7.refs_2_), channel_id=1, source_target_pairs={{0,1},{1,0},{2,3},{3,2},{4,5},{5,4},{6,7},{7,6},{8,9},{9,8},{10,11... | collective-permute-start | bytes 368648 | tf_op jit(solution)/shard_map/ppermute | solution.py:214
  22.0 3.6 %collective-permute-start.12 = (bf16[32,1920]{1,0:T(8,128)(2,1)S(1)}, bf16[32,1920]{1,0:T(8,128)(2,1)S(1)}, u32[]{:S(2)}, u32[]{:S(2)}) collective-permute-start(bf16[32,1920]{1,0:T(8,128)(2,1)S(1)} %collective-permute-done.8.refs_3_), channel_id=1, source_target_pairs={{0,1},{1,0},{2,3},{3,2},{4,5},{5,4},{6,7},{7,6},{8,9},{9,8},{10,11... | collective-permute-start | bytes 368648 | tf_op jit(solution)/shard_map/ppermute | solution.py:214
  22.0 9.6 %collective-permute-start.14 = (bf16[32,1920]{1,0:T(8,128)(2,1)S(1)}, bf16[32,1920]{1,0:T(8,128)(2,1)S(1)}, u32[]{:S(2)}, u32[]{:S(2)}) collective-permute-start(bf16[32,1920]{1,0:T(8,128)(2,1)S(1)} %maximum_bitcast_fusion.refs_0_), channel_id=1, source_target_pairs={{0,18},{1,19},{2,16},{3,17},{4,22},{5,23},{6,20},{7,21},{8,26},{9,... | collective-permute-start | bytes 368648 | tf_op jit(solution)/shard_map/ppermute | solution.py:214
  23.6 8.1 %collective-permute-start.13 = (bf16[32,1920]{1,0:T(8,128)(2,1)S(1)}, bf16[32,1920]{1,0:T(8,128)(2,1)S(1)}, u32[]{:S(2)}, u32[]{:S(2)}) collective-permute-start(bf16[32,1920]{1,0:T(8,128)(2,1)S(1)} %maximum_bitcast_fusion.refs_0_), channel_id=1, source_target_pairs={{0,2},{1,3},{2,0},{3,1},{4,6},{5,7},{6,4},{7,5},{8,10},{9,11},{10,... | collective-permute-start | bytes 368648 | tf_op jit(solution)/shard_map/ppermute | solution.py:214
  24.1 8.0 %collective-permute-start.2 = (bf16[32,1920]{1,0:T(8,128)(2,1)S(1)}, bf16[32,1920]{1,0:T(8,128)(2,1)S(1)}, u32[]{:S(2)}, u32[]{:S(2)}) collective-permute-start(bf16[32,1920]{1,0:T(8,128)(2,1)S(1)} %maximum_bitcast_fusion.refs_0_), channel_id=1, source_target_pairs={{0,16},{1,17},{2,18},{3,19},{4,20},{5,21},{6,22},{7,23},{8,24},{9,... | collective-permute-start | bytes 368648 | tf_op jit(solution)/shard_map/ppermute | solution.py:214
  31.0 1.4 %collective-permute-start.30 = (bf16[32,1792]{1,0:T(8,128)(2,1)S(1)}, bf16[32,1792]{1,0:T(8,128)(2,1)S(1)}, u32[]{:S(2)}, u32[]{:S(2)}) collective-permute-start(bf16[32,1792]{1,0:T(8,128)(2,1)S(1)} %get-tuple-element.43), channel_id=1, source_target_pairs={{0,1},{1,0},{2,3},{3,2},{4,5},{5,4},{6,7},{7,6},{8,9},{9,8},{10,11... | collective-permute-start | bytes 344072 | tf_op jit(solution)/shard_map/ppermute | solution.py:214
  31.1 2.5 %collective-permute-start.15 = (bf16[32,1920]{1,0:T(8,128)(2,1)S(1)}, bf16[32,1920]{1,0:T(8,128)(2,1)S(1)}, u32[]{:S(2)}, u32[]{:S(2)}) collective-permute-start(bf16[32,1920]{1,0:T(8,128)(2,1)S(1)} %maximum_bitcast_fusion.refs_0_), channel_id=1, source_target_pairs={{0,1},{1,0},{2,3},{3,2},{4,5},{5,4},{6,7},{7,6},{8,9},{9,8},{10,11... | collective-permute-start | bytes 368648 | tf_op jit(solution)/shard_map/ppermute | solution.py:214
  31.6 1.3 %collective-permute-start.32 = (bf16[32,1792]{1,0:T(8,128)(2,1)S(1)}, bf16[32,1792]{1,0:T(8,128)(2,1)S(1)}, u32[]{:S(2)}, u32[]{:S(2)}) collective-permute-start(bf16[32,1792]{1,0:T(8,128)(2,1)S(1)} %get-tuple-element.45), channel_id=1, source_target_pairs={{0,1},{1,0},{2,3},{3,2},{4,5},{5,4},{6,7},{7,6},{8,9},{9,8},{10,11... | collective-permute-start | bytes 344072 | tf_op jit(solution)/shard_map/ppermute | solution.py:214
  31.7 1.5 %collective-permute-start.34 = (bf16[32,1792]{1,0:T(8,128)(2,1)S(1)}, bf16[32,1792]{1,0:T(8,128)(2,1)S(1)}, u32[]{:S(2)}, u32[]{:S(2)}) collective-permute-start(bf16[32,1792]{1,0:T(8,128)(2,1)S(1)} %get-tuple-element.47), channel_id=1, source_target_pairs={{0,1},{1,0},{2,3},{3,2},{4,5},{5,4},{6,7},{7,6},{8,9},{9,8},{10,11... | collective-permute-start | bytes 344072 | tf_op jit(solution)/shard_map/ppermute | solution.py:214
  32.1 11.6 %collective-permute-start.29 = (bf16[32,1792]{1,0:T(8,128)(2,1)S(1)}, bf16[32,1792]{1,0:T(8,128)(2,1)S(1)}, u32[]{:S(2)}, u32[]{:S(2)}) collective-permute-start(bf16[32,1792]{1,0:T(8,128)(2,1)S(1)} %get-tuple-element.41), channel_id=1, source_target_pairs={{0,1},{1,0},{2,3},{3,2},{4,5},{5,4},{6,7},{7,6},{8,9},{9,8},{10,11... | collective-permute-start | bytes 344072 | tf_op jit(solution)/shard_map/ppermute | solution.py:214
  32.4 2.7 %collective-permute-start.18 = (bf16[32,1920]{1,0:T(8,128)(2,1)S(1)}, bf16[32,1920]{1,0:T(8,128)(2,1)S(1)}, u32[]{:S(2)}, u32[]{:S(2)}) collective-permute-start(bf16[32,1920]{1,0:T(8,128)(2,1)S(1)} %collective-permute-done.14.refs_3_), channel_id=1, source_target_pairs={{0,1},{1,0},{2,3},{3,2},{4,5},{5,4},{6,7},{7,6},{8,9},{9,8},{10,11... | collective-permute-start | bytes 368648 | tf_op jit(solution)/shard_map/ppermute | solution.py:214
  32.9 2.8 %collective-permute-start.17 = (bf16[32,1920]{1,0:T(8,128)(2,1)S(1)}, bf16[32,1920]{1,0:T(8,128)(2,1)S(1)}, u32[]{:S(2)}, u32[]{:S(2)}) collective-permute-start(bf16[32,1920]{1,0:T(8,128)(2,1)S(1)} %collective-permute-done.13.refs_2_), channel_id=1, source_target_pairs={{0,1},{1,0},{2,3},{3,2},{4,5},{5,4},{6,7},{7,6},{8,9},{9,8},{10,11... | collective-permute-start | bytes 368648 | tf_op jit(solution)/shard_map/ppermute | solution.py:214
  33.1 4.0 %collective-permute-start.16 = (bf16[32,1920]{1,0:T(8,128)(2,1)S(1)}, bf16[32,1920]{1,0:T(8,128)(2,1)S(1)}, u32[]{:S(2)}, u32[]{:S(2)}) collective-permute-start(bf16[32,1920]{1,0:T(8,128)(2,1)S(1)} %collective-permute-done.2.refs_1_), channel_id=1, source_target_pairs={{0,1},{1,0},{2,3},{3,2},{4,5},{5,4},{6,7},{7,6},{8,9},{9,8},{10,11... | collective-permute-start | bytes 368648 | tf_op jit(solution)/shard_map/ppermute | solution.py:214
  33.5 8.7 %slice-start = ((s8[9175040]{0:T(1024)(128)(4,1)}), s8[4194304]{0:T(1024)(128)(4,1)S(1)}, s32[]{:S(2)}) async-start(s8[9175040]{0:T(1024)(128)(4,1)} %bitcast.13), calls=%async_computation | async-start | bytes 8388608
  33.6 8.7 %slice-start.1 = ((s8[9175040]{0:T(1024)(128)(4,1)}), s8[4194304]{0:T(1024)(128)(4,1)S(1)}, s32[]{:S(2)}) async-start(s8[9175040]{0:T(1024)(128)(4,1)} %bitcast.13), calls=%async_computation.1 | async-start | bytes 8388608
  33.6 8.7 %slice-start.2 = ((s8[9175040]{0:T(1024)(128)(4,1)}), s8[786432]{0:T(1024)(128)(4,1)S(1)}, s32[]{:S(2)}) async-start(s8[9175040]{0:T(1024)(128)(4,1)} %bitcast.13), calls=%async_computation.2 | async-start | bytes 1572864
  33.6 10.6 %collective-permute-start.31 = (bf16[32,1792]{1,0:T(8,128)(2,1)S(1)}, bf16[32,1792]{1,0:T(8,128)(2,1)S(1)}, u32[]{:S(2)}, u32[]{:S(2)}) collective-permute-start(bf16[32,1792]{1,0:T(8,128)(2,1)S(1)} %add_convert_fusion.3), channel_id=1, source_target_pairs={{0,18},{1,19},{2,16},{3,17},{4,22},{5,23},{6,20},{7,21},{8,26},{9,... | collective-permute-start | bytes 344072 | tf_op jit(solution)/shard_map/ppermute | solution.py:214
  35.1 9.2 %collective-permute-start.33 = (bf16[32,1792]{1,0:T(8,128)(2,1)S(1)}, bf16[32,1792]{1,0:T(8,128)(2,1)S(1)}, u32[]{:S(2)}, u32[]{:S(2)}) collective-permute-start(bf16[32,1792]{1,0:T(8,128)(2,1)S(1)} %add_convert_fusion.2), channel_id=1, source_target_pairs={{0,16},{1,17},{2,18},{3,19},{4,20},{5,21},{6,22},{7,23},{8,24},{9,... | collective-permute-start | bytes 344072 | tf_op jit(solution)/shard_map/ppermute | solution.py:214
  35.7 9.1 %collective-permute-start.35 = (bf16[32,1792]{1,0:T(8,128)(2,1)S(1)}, bf16[32,1792]{1,0:T(8,128)(2,1)S(1)}, u32[]{:S(2)}, u32[]{:S(2)}) collective-permute-start(bf16[32,1792]{1,0:T(8,128)(2,1)S(1)} %add_convert_fusion.1), channel_id=1, source_target_pairs={{0,2},{1,3},{2,0},{3,1},{4,6},{5,7},{6,4},{7,5},{8,10},{9,11},{10,... | collective-permute-start | bytes 344072 | tf_op jit(solution)/shard_map/ppermute | solution.py:214
  43.7 1.4 %collective-permute-start.20 = (bf16[32,1792]{1,0:T(8,128)(2,1)S(1)}, bf16[32,1792]{1,0:T(8,128)(2,1)S(1)}, u32[]{:S(2)}, u32[]{:S(2)}) collective-permute-start(bf16[32,1792]{1,0:T(8,128)(2,1)S(1)} %get-tuple-element.36), channel_id=1, source_target_pairs={{0,1},{1,0},{2,3},{3,2},{4,5},{5,4},{6,7},{7,6},{8,9},{9,8},{10,11... | collective-permute-start | bytes 344072 | tf_op jit(solution)/shard_map/ppermute | solution.py:214
  43.8 2.9 %collective-permute-start.22 = (bf16[32,1792]{1,0:T(8,128)(2,1)S(1)}, bf16[32,1792]{1,0:T(8,128)(2,1)S(1)}, u32[]{:S(2)}, u32[]{:S(2)}) collective-permute-start(bf16[32,1792]{1,0:T(8,128)(2,1)S(1)} %get-tuple-element.38), channel_id=1, source_target_pairs={{0,1},{1,0},{2,3},{3,2},{4,5},{5,4},{6,7},{7,6},{8,9},{9,8},{10,11... | collective-permute-start | bytes 344072 | tf_op jit(solution)/shard_map/ppermute | solution.py:214
  44.3 3.0 %collective-permute-start.24 = (bf16[32,1792]{1,0:T(8,128)(2,1)S(1)}, bf16[32,1792]{1,0:T(8,128)(2,1)S(1)}, u32[]{:S(2)}, u32[]{:S(2)}) collective-permute-start(bf16[32,1792]{1,0:T(8,128)(2,1)S(1)} %get-tuple-element.40), channel_id=1, source_target_pairs={{0,1},{1,0},{2,3},{3,2},{4,5},{5,4},{6,7},{7,6},{8,9},{9,8},{10,11... | collective-permute-start | bytes 344072 | tf_op jit(solution)/shard_map/ppermute | solution.py:214
  44.3 5.1 %collective-permute-start.19 = (bf16[32,1792]{1,0:T(8,128)(2,1)S(1)}, bf16[32,1792]{1,0:T(8,128)(2,1)S(1)}, u32[]{:S(2)}, u32[]{:S(2)}) collective-permute-start(bf16[32,1792]{1,0:T(8,128)(2,1)S(1)} %get-tuple-element.34), channel_id=1, source_target_pairs={{0,1},{1,0},{2,3},{3,2},{4,5},{5,4},{6,7},{7,6},{8,9},{9,8},{10,11... | collective-permute-start | bytes 344072 | tf_op jit(solution)/shard_map/ppermute | solution.py:214
  45.1 7.0 %collective-permute-start.21 = (bf16[32,1792]{1,0:T(8,128)(2,1)S(1)}, bf16[32,1792]{1,0:T(8,128)(2,1)S(1)}, u32[]{:S(2)}, u32[]{:S(2)}) collective-permute-start(bf16[32,1792]{1,0:T(8,128)(2,1)S(1)} %add_convert_fusion.8), channel_id=1, source_target_pairs={{0,18},{1,19},{2,16},{3,17},{4,22},{5,23},{6,20},{7,21},{8,26},{9,... | collective-permute-start | bytes 344072 | tf_op jit(solution)/shard_map/ppermute | solution.py:214
  46.7 7.0 %collective-permute-start.23 = (bf16[32,1792]{1,0:T(8,128)(2,1)S(1)}, bf16[32,1792]{1,0:T(8,128)(2,1)S(1)}, u32[]{:S(2)}, u32[]{:S(2)}) collective-permute-start(bf16[32,1792]{1,0:T(8,128)(2,1)S(1)} %add_convert_fusion.7), channel_id=1, source_target_pairs={{0,16},{1,17},{2,18},{3,19},{4,20},{5,21},{6,22},{7,23},{8,24},{9,... | collective-permute-start | bytes 344072 | tf_op jit(solution)/shard_map/ppermute | solution.py:214
  47.3 6.4 %collective-permute-start.25 = (bf16[32,1792]{1,0:T(8,128)(2,1)S(1)}, bf16[32,1792]{1,0:T(8,128)(2,1)S(1)}, u32[]{:S(2)}, u32[]{:S(2)}) collective-permute-start(bf16[32,1792]{1,0:T(8,128)(2,1)S(1)} %add_convert_fusion.6), channel_id=1, source_target_pairs={{0,2},{1,3},{2,0},{3,1},{4,6},{5,7},{6,4},{7,5},{8,10},{9,11},{10,... | collective-permute-start | bytes 344072 | tf_op jit(solution)/shard_map/ppermute | solution.py:214
  48.9 6.9 %collective-permute-start.36 = (bf16[8,1792]{1,0:T(8,128)(2,1)S(1)}, bf16[8,1792]{1,0:T(8,128)(2,1)S(1)}, u32[]{:S(2)}, u32[]{:S(2)}) collective-permute-start(bf16[8,1792]{1,0:T(8,128)(2,1)S(1)} %get-tuple-element.48), channel_id=1, source_target_pairs={{0,12},{1,13},{2,14},{3,15},{4,8},{5,9},{6,10},{7,11},{8,4},{9,5},... | collective-permute-start | bytes 86024 | tf_op jit(solution)/shard_map/ppermute | solution.py:214
  49.5 8.8 %collective-permute-start.37 = (bf16[8,1792]{1,0:T(8,128)(2,1)S(1)}, bf16[8,1792]{1,0:T(8,128)(2,1)S(1)}, u32[]{:S(2)}, u32[]{:S(2)}) collective-permute-start(bf16[8,1792]{1,0:T(8,128)(2,1)S(1)} %get-tuple-element.50), channel_id=1, source_target_pairs={{0,4},{1,5},{2,6},{3,7},{4,0},{5,1},{6,2},{7,3},{8,12},{9,13},{10,... | collective-permute-start | bytes 86024 | tf_op jit(solution)/shard_map/ppermute | solution.py:214
  52.1 6.2 %collective-permute-start.38 = (bf16[8,1792]{1,0:T(8,128)(2,1)S(1)}, bf16[8,1792]{1,0:T(8,128)(2,1)S(1)}, u32[]{:S(2)}, u32[]{:S(2)}) collective-permute-start(bf16[8,1792]{1,0:T(8,128)(2,1)S(1)} %get-tuple-element.49), channel_id=1, source_target_pairs={{0,8},{1,9},{2,10},{3,11},{4,12},{5,13},{6,14},{7,15},{8,0},{9,1},... | collective-permute-start | bytes 86024 | tf_op jit(solution)/shard_map/ppermute | solution.py:214
  53.8 5.7 %collective-permute-start.26 = (bf16[8,1792]{1,0:T(8,128)(2,1)S(1)}, bf16[8,1792]{1,0:T(8,128)(2,1)S(1)}, u32[]{:S(2)}, u32[]{:S(2)}) collective-permute-start(bf16[8,1792]{1,0:T(8,128)(2,1)S(1)} %get-tuple-element.51), channel_id=1, source_target_pairs={{0,12},{1,13},{2,14},{3,15},{4,8},{5,9},{6,10},{7,11},{8,4},{9,5},... | collective-permute-start | bytes 86024 | tf_op jit(solution)/shard_map/ppermute | solution.py:214
  54.5 5.1 %collective-permute-start.27 = (bf16[8,1792]{1,0:T(8,128)(2,1)S(1)}, bf16[8,1792]{1,0:T(8,128)(2,1)S(1)}, u32[]{:S(2)}, u32[]{:S(2)}) collective-permute-start(bf16[8,1792]{1,0:T(8,128)(2,1)S(1)} %get-tuple-element.53), channel_id=1, source_target_pairs={{0,4},{1,5},{2,6},{3,7},{4,0},{5,1},{6,2},{7,3},{8,12},{9,13},{10,... | collective-permute-start | bytes 86024 | tf_op jit(solution)/shard_map/ppermute | solution.py:214
  55.7 4.8 %collective-permute-start.28 = (bf16[8,1792]{1,0:T(8,128)(2,1)S(1)}, bf16[8,1792]{1,0:T(8,128)(2,1)S(1)}, u32[]{:S(2)}, u32[]{:S(2)}) collective-permute-start(bf16[8,1792]{1,0:T(8,128)(2,1)S(1)} %get-tuple-element.52), channel_id=1, source_target_pairs={{0,8},{1,9},{2,10},{3,11},{4,12},{5,13},{6,14},{7,15},{8,0},{9,1},... | collective-permute-start | bytes 86024 | tf_op jit(solution)/shard_map/ppermute | solution.py:214

commit v4 on v3

--- a/solution.py
+++ b/solution.py
@@ -253,7 +253,7 @@
 
 def collect_line(total, tokens):
     rows = [total[k * tokens : (k + 1) * tokens] for k in range(4)]
-    return add(rows[0], *[move(rows[k + 1], Z[k], 32) for k in (2,1,0)])
+    return add(rows[0], *[move(rows[k + 1], Z[k], 32) for k in (2,0,1)])
 
 
 def spread_any(message, width):

time: 61.3 us -> 60.9 us (level)
  no operation moved by 1% of the time
where the time goes in v4:
time: 60.9 us; the launch traced here: 60.8 us
  starting transfers between devices  31.8 us (52%)
  waiting for transfers between devices  13.4 us (22%)
  Pallas kernels  13 us (21%)
  other arithmetic  1.61 us (3%)
  between operations  0.92 us (2%)
    ppermute x39, starting transfers between devices, move(): return lax.ppermute(value, AXES, [(i, i ^ mask) for i in range(devices)])  31.8 us
    ppermute x39, waiting for transfers between devices, move(): return lax.ppermute(value, AXES, [(i, i ^ mask) for i in range(devices)])  13.4 us
    pallas_call x3, Pallas kernels, expert_call(): pl.pallas_call(kernel, out_shape=shapes, scratch_shapes=scratch, compiler...  11.8 us
    convert_element_type x10, other arithmetic, add(): return sum((p.astype(jnp.float32) for p in parts)).astype(jnp.bfloat16)  1.58 us
  transfers between devices with their start and end apart: 39, of which 12 were waited for; matrix products, arithmetic and copies ran while one was open for 2% of the time, Pallas kernels for 19%

profile of v4, /device:TPU:0, one launch (start us, length us, event | category | flops | bytes accessed | tf_op | source)
XLA Modules:
  0.0 60.8 jit_solution(7661817867213548494)
XLA Ops:
  0.7 0.0 copy-start.2
  0.7 1.1 %pack.1 = (bf16[8,1920]{1,0:T(8,128)(2,1)S(1)}, bf16[8,1920]{1,0:T(8,128)(2,1)S(1)}) custom-call(bf16[8,1792]{1,0:T(8,128)(2,1)} %refs_0_.1, s32[8,8]{1,0:T(8,128)} %refs_1_.1, f32[8,8]{1,0:T(8,128)} %refs_2_.1, bf16[8,1792]{1,0:T(8,128)(2,1)} %refs_3_.1, s32[8,8]{1,0:T(8,128)} %refs_4_.1, f32[8,8]{1,0:T(8,128)} %refs_5_.1), custom_call_target="tpu_custom_call" | custom-call | flops 40000000000 | bytes 100000000 | tf_op jit(solution)/shard_map/pack/pallas_call | solution.py:57
  1.8 4.1 %collective-permute-start.3 = (bf16[8,1920]{1,0:T(8,128)(2,1)S(1)}, bf16[8,1920]{1,0:T(8,128)(2,1)S(1)}, u32[]{:S(2)}, u32[]{:S(2)}) collective-permute-start(bf16[8,1920]{1,0:T(8,128)(2,1)S(1)} %get-tuple-element.26), channel_id=1, source_target_pairs={{0,8},{1,9},{2,10},{3,11},{4,12},{5,13},{6,14},{7,15},{8,0},{9,1},... | collective-permute-start | bytes 92168 | tf_op jit(solution)/shard_map/ppermute | solution.py:214
  5.9 1.6 %collective-permute-start.4 = (bf16[8,1920]{1,0:T(8,128)(2,1)S(1)}, bf16[8,1920]{1,0:T(8,128)(2,1)S(1)}, u32[]{:S(2)}, u32[]{:S(2)}) collective-permute-start(bf16[8,1920]{1,0:T(8,128)(2,1)S(1)} %get-tuple-element.26), channel_id=1, source_target_pairs={{0,4},{1,5},{2,6},{3,7},{4,0},{5,1},{6,2},{7,3},{8,12},{9,13},{10,... | collective-permute-start | bytes 92168 | tf_op jit(solution)/shard_map/ppermute | solution.py:214
  7.5 0.0 collective-permute-start.5
  7.5 1.9 %collective-permute-start = (bf16[1,8,1920]{2,1,0:T(8,128)(2,1)S(1)}, bf16[1,8,1920]{2,1,0:T(8,128)(2,1)S(1)}, u32[]{:S(2)}, u32[]{:S(2)}) collective-permute-start(bf16[1,8,1920]{2,1,0:T(8,128)(2,1)S(1)} %bitcast.18), channel_id=1, source_target_pairs={{0,8},{1,9},{2,10},{3,11},{4,12},{5,13},{6,14},{7,15},{8,0},{9,1},... | collective-permute-start | bytes 92168 | tf_op jit(solution)/shard_map/ppermute | solution.py:214
  9.4 0.0 collective-permute-done.3
  9.4 0.4 collective-permute-done.4
  9.8 3.4 %collective-permute-done.5 = bf16[8,1920]{1,0:T(8,128)(2,1)S(1)} collective-permute-done((bf16[8,1920]{1,0:T(8,128)(2,1)S(1)}, bf16[8,1920]{1,0:T(8,128)(2,1)S(1)}, u32[]{:S(2)}, u32[]{:S(2)}) %collective-permute-start.5) | collective-permute-done | bytes 30752 | tf_op jit(solution)/shard_map/ppermute | solution.py:214
  13.2 1.5 %collective-permute-start.6 = (bf16[32,1920]{1,0:T(8,128)(2,1)S(1)}, bf16[32,1920]{1,0:T(8,128)(2,1)S(1)}, u32[]{:S(2)}, u32[]{:S(2)}) collective-permute-start(bf16[32,1920]{1,0:T(8,128)(2,1)S(1)} %constant_dynamic-update-slice_fusion.refs_0_), channel_id=1, source_target_pairs={{0,16},{1,17},{2,18},{3,19},{4,20},{5,21},{6,22},{7,23},{8,24},{9,... | collective-permute-start | bytes 368648 | tf_op jit(solution)/shard_map/ppermute | solution.py:214
  14.7 1.5 %collective-permute-start.7 = (bf16[32,1920]{1,0:T(8,128)(2,1)S(1)}, bf16[32,1920]{1,0:T(8,128)(2,1)S(1)}, u32[]{:S(2)}, u32[]{:S(2)}) collective-permute-start(bf16[32,1920]{1,0:T(8,128)(2,1)S(1)} %constant_dynamic-update-slice_fusion.refs_0_), channel_id=1, source_target_pairs={{0,2},{1,3},{2,0},{3,1},{4,6},{5,7},{6,4},{7,5},{8,10},{9,11},{10,... | collective-permute-start | bytes 368648 | tf_op jit(solution)/shard_map/ppermute | solution.py:214
  16.2 0.5 collective-permute-start.8
  16.7 0.0 collective-permute-done
  16.7 0.1 collective-permute-start.1
  16.8 0.1 collective-permute-start.9
  16.9 2.5 %collective-permute-done.6.refs_1_ = bf16[32,1920]{1,0:T(8,128)(2,1)S(1)} collective-permute-done((bf16[32,1920]{1,0:T(8,128)(2,1)S(1)}, bf16[32,1920]{1,0:T(8,128)(2,1)S(1)}, u32[]{:S(2)}, u32[]{:S(2)}) %collective-permute-start.6) | collective-permute-done | bytes 122912 | tf_op jit(solution)/shard_map/ppermute | solution.py:214
  19.4 0.2 collective-permute-done.7.refs_2_
  19.6 0.3 collective-permute-start.11
  19.9 2.1 %collective-permute-done.8.refs_3_ = bf16[32,1920]{1,0:T(8,128)(2,1)S(1)} collective-permute-done((bf16[32,1920]{1,0:T(8,128)(2,1)S(1)}, bf16[32,1920]{1,0:T(8,128)(2,1)S(1)}, u32[]{:S(2)}, u32[]{:S(2)}) %collective-permute-start.8) | collective-permute-done | bytes 122912 | tf_op jit(solution)/shard_map/ppermute | solution.py:214
  22.0 0.0 collective-permute-start.12
  22.0 0.0 collective-permute-done.1
  22.0 1.5 %collective-permute-start.14 = (bf16[32,1920]{1,0:T(8,128)(2,1)S(1)}, bf16[32,1920]{1,0:T(8,128)(2,1)S(1)}, u32[]{:S(2)}, u32[]{:S(2)}) collective-permute-start(bf16[32,1920]{1,0:T(8,128)(2,1)S(1)} %maximum_bitcast_fusion.refs_0_), channel_id=1, source_target_pairs={{0,18},{1,19},{2,16},{3,17},{4,22},{5,23},{6,20},{7,21},{8,26},{9,... | collective-permute-start | bytes 368648 | tf_op jit(solution)/shard_map/ppermute | solution.py:214
  23.6 0.5 collective-permute-start.13
  24.1 0.0 collective-permute-done.10.refs_5_
  24.1 1.5 %collective-permute-start.2 = (bf16[32,1920]{1,0:T(8,128)(2,1)S(1)}, bf16[32,1920]{1,0:T(8,128)(2,1)S(1)}, u32[]{:S(2)}, u32[]{:S(2)}) collective-permute-start(bf16[32,1920]{1,0:T(8,128)(2,1)S(1)} %maximum_bitcast_fusion.refs_0_), channel_id=1, source_target_pairs={{0,16},{1,17},{2,18},{3,19},{4,20},{5,21},{6,22},{7,23},{8,24},{9,... | collective-permute-start | bytes 368648 | tf_op jit(solution)/shard_map/ppermute | solution.py:214
  25.6 5.4 %experts_backward.1 = (bf16[32,1792]{1,0:T(8,128)(2,1)S(1)}, bf16[32,1792]{1,0:T(8,128)(2,1)S(1)}, bf16[32,1792]{1,0:T(8,128)(2,1)S(1)}, bf16[32,1792]{1,0:T(8,1...) custom-call(bf16[32,1920]{1,0:T(8,128)(2,1)S(1)} %constant_dynamic-u, ...), custom_call_target="tpu_custom_call" | custom-call | flops 3523215360 | bytes 27525120 | tf_op jit(solution)/shard_map/experts_backward/pallas_call | solution.py:167
  31.0 0.1 collective-permute-start.30
  31.1 0.5 collective-permute-start.15
  31.6 0.1 collective-permute-start.32
  31.7 0.4 collective-permute-start.34
  32.1 0.1 collective-permute-start.29
  32.2 0.2 collective-permute-done.30
  32.4 0.2 collective-permute-start.18
  32.7 0.3 collective-permute-done.32
  32.9 0.2 collective-permute-start.17
  33.1 0.4 collective-permute-start.16
  33.6 0.0 slice-start.1
  33.6 1.5 %collective-permute-start.31 = (bf16[32,1792]{1,0:T(8,128)(2,1)S(1)}, bf16[32,1792]{1,0:T(8,128)(2,1)S(1)}, u32[]{:S(2)}, u32[]{:S(2)}) collective-permute-start(bf16[32,1792]{1,0:T(8,128)(2,1)S(1)} %add_convert_fusion.3), channel_id=1, source_target_pairs={{0,18},{1,19},{2,16},{3,17},{4,22},{5,23},{6,20},{7,21},{8,26},{9,... | collective-permute-start | bytes 344072 | tf_op jit(solution)/shard_map/ppermute | solution.py:214
  35.1 0.5 collective-permute-start.33
  35.7 1.5 %collective-permute-start.35 = (bf16[32,1792]{1,0:T(8,128)(2,1)S(1)}, bf16[32,1792]{1,0:T(8,128)(2,1)S(1)}, u32[]{:S(2)}, u32[]{:S(2)}) collective-permute-start(bf16[32,1792]{1,0:T(8,128)(2,1)S(1)} %add_convert_fusion.1), channel_id=1, source_target_pairs={{0,2},{1,3},{2,0},{3,1},{4,6},{5,7},{6,4},{7,5},{8,10},{9,11},{10,... | collective-permute-start | bytes 344072 | tf_op jit(solution)/shard_map/ppermute | solution.py:214
  37.2 5.1 %forward_hidden.1 = (bf16[128,1280]{1,0:T(8,128)(2,1)S(1)}, f32[128,1]{1,0:T(8,128)S(1)}) custom-call(bf16[32,1920]{1,0:T(8,128)(2,1)S(1)} %maximum_bitcast_fusion.refs_0_, bf16[32,1920]{1,0:T(8,128)(2,1)S(1)} %collective-permute-done.2.refs_1_, bf16[32,1920]{1,0:T(8,128)(2,1)S(1)} %collective-permute-done.13.refs_2_, ...), custom_call_target="tpu_custom_call" | custom-call | flops 2348810240 | bytes 18350080 | tf_op jit(solution)/shard_map/forward_hidden/pallas_call | solution.py:167
  42.3 1.4 %forward_down.1 = (bf16[32,1792]{1,0:T(8,128)(2,1)S(1)}, bf16[32,1792]{1,0:T(8,128)(2,1)S(1)}, bf16[32,1792]{1,0:T(8,128)(2,1)S(1)}, bf16[32,1792]{1,0:T(8,128)(...) custom-call(bf16[128,1280]{1,0:T(8,128)(2,1)S(1)} %get-tuple-element, ...), custom_call_target="tpu_custom_call" | custom-call | flops 1174405120 | bytes 9175040 | tf_op jit(solution)/shard_map/forward_down/pallas_call | solution.py:167
  43.7 0.1 collective-permute-start.20
  43.8 0.5 collective-permute-start.22
  44.3 0.1 collective-permute-start.24
  44.3 0.4 collective-permute-start.19
  44.8 0.1 add_convert_fusion
  44.9 0.2 collective-permute-done.20
  45.1 1.5 %collective-permute-start.21 = (bf16[32,1792]{1,0:T(8,128)(2,1)S(1)}, bf16[32,1792]{1,0:T(8,128)(2,1)S(1)}, u32[]{:S(2)}, u32[]{:S(2)}) collective-permute-start(bf16[32,1792]{1,0:T(8,128)(2,1)S(1)} %add_convert_fusion.8), channel_id=1, source_target_pairs={{0,18},{1,19},{2,16},{3,17},{4,22},{5,23},{6,20},{7,21},{8,26},{9,... | collective-permute-start | bytes 344072 | tf_op jit(solution)/shard_map/ppermute | solution.py:214
  46.7 0.6 collective-permute-start.23
  47.3 1.6 %collective-permute-start.25 = (bf16[32,1792]{1,0:T(8,128)(2,1)S(1)}, bf16[32,1792]{1,0:T(8,128)(2,1)S(1)}, u32[]{:S(2)}, u32[]{:S(2)}) collective-permute-start(bf16[32,1792]{1,0:T(8,128)(2,1)S(1)} %add_convert_fusion.6), channel_id=1, source_target_pairs={{0,2},{1,3},{2,0},{3,1},{4,6},{5,7},{6,4},{7,5},{8,10},{9,11},{10,... | collective-permute-start | bytes 344072 | tf_op jit(solution)/shard_map/ppermute | solution.py:214
  48.9 0.6 collective-permute-start.36
  49.5 0.2 collective-permute-start.37
  49.6 2.4 %collective-permute-done.21 = bf16[32,1792]{1,0:T(8,128)(2,1)S(1)} collective-permute-done((bf16[32,1792]{1,0:T(8,128)(2,1)S(1)}, bf16[32,1792]{1,0:T(8,128)(2,1)S(1)}, u32[]{:S(2)}, u32[]{:S(2)}) %collective-permute-start.21) | collective-permute-done | bytes 114720 | tf_op jit(solution)/shard_map/ppermute | solution.py:214
  52.1 1.2 %collective-permute-start.38 = (bf16[8,1792]{1,0:T(8,128)(2,1)S(1)}, bf16[8,1792]{1,0:T(8,128)(2,1)S(1)}, u32[]{:S(2)}, u32[]{:S(2)}) collective-permute-start(bf16[8,1792]{1,0:T(8,128)(2,1)S(1)} %get-tuple-element.49), channel_id=1, source_target_pairs={{0,4},{1,5},{2,6},{3,7},{4,0},{5,1},{6,2},{7,3},{8,12},{9,13},{10,... | collective-permute-start | bytes 86024 | tf_op jit(solution)/shard_map/ppermute | solution.py:214
  53.3 0.5 collective-permute-done.23
  53.7 0.1 add_convert_fusion.5
  53.8 0.7 %collective-permute-start.26 = (bf16[8,1792]{1,0:T(8,128)(2,1)S(1)}, bf16[8,1792]{1,0:T(8,128)(2,1)S(1)}, u32[]{:S(2)}, u32[]{:S(2)}) collective-permute-start(bf16[8,1792]{1,0:T(8,128)(2,1)S(1)} %get-tuple-element.51), channel_id=1, source_target_pairs={{0,12},{1,13},{2,14},{3,15},{4,8},{5,9},{6,10},{7,11},{8,4},{9,5},... | collective-permute-start | bytes 86024 | tf_op jit(solution)/shard_map/ppermute | solution.py:214
  54.5 1.2 %collective-permute-start.27 = (bf16[8,1792]{1,0:T(8,128)(2,1)S(1)}, bf16[8,1792]{1,0:T(8,128)(2,1)S(1)}, u32[]{:S(2)}, u32[]{:S(2)}) collective-permute-start(bf16[8,1792]{1,0:T(8,128)(2,1)S(1)} %get-tuple-element.53), channel_id=1, source_target_pairs={{0,8},{1,9},{2,10},{3,11},{4,12},{5,13},{6,14},{7,15},{8,0},{9,1},... | collective-permute-start | bytes 86024 | tf_op jit(solution)/shard_map/ppermute | solution.py:214
  55.7 2.6 %collective-permute-start.28 = (bf16[8,1792]{1,0:T(8,128)(2,1)S(1)}, bf16[8,1792]{1,0:T(8,128)(2,1)S(1)}, u32[]{:S(2)}, u32[]{:S(2)}) collective-permute-start(bf16[8,1792]{1,0:T(8,128)(2,1)S(1)} %get-tuple-element.52), channel_id=1, source_target_pairs={{0,4},{1,5},{2,6},{3,7},{4,0},{5,1},{6,2},{7,3},{8,12},{9,13},{10,... | collective-permute-start | bytes 86024 | tf_op jit(solution)/shard_map/ppermute | solution.py:214
  58.3 0.6 %add_convert_fusion.10 = bf16[8,1792]{1,0:T(8,128)(2,1)} fusion(bf16[8,1792]{1,0:T(8,128)(2,1)S(1)} %collective-permute-done.38, bf16[8,1792]{1,0:T(8,128)(2,1)S(1)} %collective-permute-done.37, bf16[8,1792]{1,0:T(8,128)(2,1)S(1)} %collective-permute-done.36, bf16[32,1792]{1,0:T(8,128)(2,1)S(1)} %add_convert_fusion), kind=kLoop, calls=%fused_computation.12 | loop fusion | flops 114688 | bytes 143360 | tf_op jit(solution)/shard_map/convert_element_type | solution.py:247
  58.9 0.6 %collective-permute-done.26 = bf16[8,1792]{1,0:T(8,128)(2,1)S(1)} collective-permute-done((bf16[8,1792]{1,0:T(8,128)(2,1)S(1)}, bf16[8,1792]{1,0:T(8,128)(2,1)S(1)}, u32[]{:S(2)}, u32[]{:S(2)}) %collective-permute-start.26) | collective-permute-done | bytes 28704 | tf_op jit(solution)/shard_map/ppermute | solution.py:214
  59.6 0.6 collective-permute-done.28
  60.1 0.6 %add_convert_fusion.11 = bf16[8,1792]{1,0:T(8,128)(2,1)} fusion(bf16[8,1792]{1,0:T(8,128)(2,1)S(1)} %collective-permute-done.28, bf16[8,1792]{1,0:T(8,128)(2,1)S(1)} %collective-permute-done.27, bf16[8,1792]{1,0:T(8,128)(2,1)S(1)} %collective-permute-done.26, bf16[32,1792]{1,0:T(8,128)(2,1)S(1)} %add_convert_fusion.5), kind=kLoop, calls=%fused_computation.13 | loop fusion | flops 114688 | bytes 143360 | tf_op jit(solution)/shard_map/convert_element_type | solution.py:247
  (53 shorter events, 0.3 us)
Async XLA Ops:
  0.6 25.0 %copy-start = (bf16[1,1280,3584]{2,1,0:T(8,128)(2,1)S(1)}, bf16[1,1280,3584]{2,1,0:T(8,128)(2,1)}, u32[]{:S(2)}) copy-start(bf16[1,1280,3584]{2,1,0:T(8,128)(2,1)} %param.19) | copy-start | bytes 27525124
  0.6 25.0 %copy-start.1 = (bf16[1,1280,3584]{2,1,0:T(8,128)(2,1)S(1)}, bf16[1,1280,3584]{2,1,0:T(8,128)(2,1)}, u32[]{:S(2)}) copy-start(bf16[1,1280,3584]{2,1,0:T(8,128)(2,1)} %param.20) | copy-start | bytes 27525124
  0.7 25.0 %copy-start.2 = (bf16[1,1280,3584]{2,1,0:T(8,128)(2,1)S(1)}, bf16[1,1280,3584]{2,1,0:T(8,128)(2,1)}, u32[]{:S(2)}) copy-start(bf16[1,1280,3584]{2,1,0:T(8,128)(2,1)} %param.21) | copy-start | bytes 27525124
  0.7 25.0 %copy-start.3 = (bf16[1,128,1280]{2,1,0:T(8,128)(2,1)S(1)}, bf16[1,128,1280]{2,1,0:T(8,128)(2,1)}, u32[]{:S(2)}) copy-start(bf16[1,128,1280]{2,1,0:T(8,128)(2,1)} %param.17) | copy-start | bytes 983044
  0.7 25.0 %copy-start.4 = (bf16[1,128,1280]{2,1,0:T(8,128)(2,1)S(1)}, bf16[1,128,1280]{2,1,0:T(8,128)(2,1)}, u32[]{:S(2)}) copy-start(bf16[1,128,1280]{2,1,0:T(8,128)(2,1)} %param.18) | copy-start | bytes 983044
  1.8 7.6 %collective-permute-start.3 = (bf16[8,1920]{1,0:T(8,128)(2,1)S(1)}, bf16[8,1920]{1,0:T(8,128)(2,1)S(1)}, u32[]{:S(2)}, u32[]{:S(2)}) collective-permute-start(bf16[8,1920]{1,0:T(8,128)(2,1)S(1)} %get-tuple-element.26), channel_id=1, source_target_pairs={{0,8},{1,9},{2,10},{3,11},{4,12},{5,13},{6,14},{7,15},{8,0},{9,1},... | collective-permute-start | bytes 92168 | tf_op jit(solution)/shard_map/ppermute | solution.py:214
  5.9 3.9 %collective-permute-start.4 = (bf16[8,1920]{1,0:T(8,128)(2,1)S(1)}, bf16[8,1920]{1,0:T(8,128)(2,1)S(1)}, u32[]{:S(2)}, u32[]{:S(2)}) collective-permute-start(bf16[8,1920]{1,0:T(8,128)(2,1)S(1)} %get-tuple-element.26), channel_id=1, source_target_pairs={{0,4},{1,5},{2,6},{3,7},{4,0},{5,1},{6,2},{7,3},{8,12},{9,13},{10,... | collective-permute-start | bytes 92168 | tf_op jit(solution)/shard_map/ppermute | solution.py:214
  7.5 5.7 %collective-permute-start.5 = (bf16[8,1920]{1,0:T(8,128)(2,1)S(1)}, bf16[8,1920]{1,0:T(8,128)(2,1)S(1)}, u32[]{:S(2)}, u32[]{:S(2)}) collective-permute-start(bf16[8,1920]{1,0:T(8,128)(2,1)S(1)} %get-tuple-element.26), channel_id=1, source_target_pairs={{0,12},{1,13},{2,14},{3,15},{4,8},{5,9},{6,10},{7,11},{8,4},{9,5},... | collective-permute-start | bytes 92168 | tf_op jit(solution)/shard_map/ppermute | solution.py:214
  7.5 9.2 %collective-permute-start = (bf16[1,8,1920]{2,1,0:T(8,128)(2,1)S(1)}, bf16[1,8,1920]{2,1,0:T(8,128)(2,1)S(1)}, u32[]{:S(2)}, u32[]{:S(2)}) collective-permute-start(bf16[1,8,1920]{2,1,0:T(8,128)(2,1)S(1)} %bitcast.18), channel_id=1, source_target_pairs={{0,8},{1,9},{2,10},{3,11},{4,12},{5,13},{6,14},{7,15},{8,0},{9,1},... | collective-permute-start | bytes 92168 | tf_op jit(solution)/shard_map/ppermute | solution.py:214
  13.2 6.2 %collective-permute-start.6 = (bf16[32,1920]{1,0:T(8,128)(2,1)S(1)}, bf16[32,1920]{1,0:T(8,128)(2,1)S(1)}, u32[]{:S(2)}, u32[]{:S(2)}) collective-permute-start(bf16[32,1920]{1,0:T(8,128)(2,1)S(1)} %constant_dynamic-update-slice_fusion.refs_0_), channel_id=1, source_target_pairs={{0,16},{1,17},{2,18},{3,19},{4,20},{5,21},{6,22},{7,23},{8,24},{9,... | collective-permute-start | bytes 368648 | tf_op jit(solution)/shard_map/ppermute | solution.py:214
  14.7 4.9 %collective-permute-start.7 = (bf16[32,1920]{1,0:T(8,128)(2,1)S(1)}, bf16[32,1920]{1,0:T(8,128)(2,1)S(1)}, u32[]{:S(2)}, u32[]{:S(2)}) collective-permute-start(bf16[32,1920]{1,0:T(8,128)(2,1)S(1)} %constant_dynamic-update-slice_fusion.refs_0_), channel_id=1, source_target_pairs={{0,2},{1,3},{2,0},{3,1},{4,6},{5,7},{6,4},{7,5},{8,10},{9,11},{10,... | collective-permute-start | bytes 368648 | tf_op jit(solution)/shard_map/ppermute | solution.py:214
  16.2 5.8 %collective-permute-start.8 = (bf16[32,1920]{1,0:T(8,128)(2,1)S(1)}, bf16[32,1920]{1,0:T(8,128)(2,1)S(1)}, u32[]{:S(2)}, u32[]{:S(2)}) collective-permute-start(bf16[32,1920]{1,0:T(8,128)(2,1)S(1)} %constant_dynamic-update-slice_fusion.refs_0_), channel_id=1, source_target_pairs={{0,18},{1,19},{2,16},{3,17},{4,22},{5,23},{6,20},{7,21},{8,26},{9,... | collective-permute-start | bytes 368648 | tf_op jit(solution)/shard_map/ppermute | solution.py:214
  16.7 5.3 %collective-permute-start.1 = (bf16[2,8,1920]{2,1,0:T(8,128)(2,1)S(1)}, bf16[2,8,1920]{2,1,0:T(8,128)(2,1)S(1)}, u32[]{:S(2)}, u32[]{:S(2)}) collective-permute-start(bf16[2,8,1920]{2,1,0:T(8,128)(2,1)S(1)} %pad_maximum_fusion), channel_id=1, source_target_pairs={{0,4},{1,5},{2,6},{3,7},{4,0},{5,1},{6,2},{7,3},{8,12},{9,13},{10,... | collective-permute-start | bytes 184328 | tf_op jit(solution)/shard_map/ppermute | solution.py:214
  16.8 6.8 %collective-permute-start.9 = (bf16[32,1920]{1,0:T(8,128)(2,1)S(1)}, bf16[32,1920]{1,0:T(8,128)(2,1)S(1)}, u32[]{:S(2)}, u32[]{:S(2)}) collective-permute-start(bf16[32,1920]{1,0:T(8,128)(2,1)S(1)} %constant_dynamic-update-slice_fusion.refs_0_), channel_id=1, source_target_pairs={{0,1},{1,0},{2,3},{3,2},{4,5},{5,4},{6,7},{7,6},{8,9},{9,8},{10,11... | collective-permute-start | bytes 368648 | tf_op jit(solution)/shard_map/ppermute | solution.py:214
  19.4 4.7 %collective-permute-start.10 = (bf16[32,1920]{1,0:T(8,128)(2,1)S(1)}, bf16[32,1920]{1,0:T(8,128)(2,1)S(1)}, u32[]{:S(2)}, u32[]{:S(2)}) collective-permute-start(bf16[32,1920]{1,0:T(8,128)(2,1)S(1)} %collective-permute-done.6.refs_1_), channel_id=1, source_target_pairs={{0,1},{1,0},{2,3},{3,2},{4,5},{5,4},{6,7},{7,6},{8,9},{9,8},{10,11... | collective-permute-start | bytes 368648 | tf_op jit(solution)/shard_map/ppermute | solution.py:214
  19.6 6.0 %collective-permute-start.11 = (bf16[32,1920]{1,0:T(8,128)(2,1)S(1)}, bf16[32,1920]{1,0:T(8,128)(2,1)S(1)}, u32[]{:S(2)}, u32[]{:S(2)}) collective-permute-start(bf16[32,1920]{1,0:T(8,128)(2,1)S(1)} %collective-permute-done.7.refs_2_), channel_id=1, source_target_pairs={{0,1},{1,0},{2,3},{3,2},{4,5},{5,4},{6,7},{7,6},{8,9},{9,8},{10,11... | collective-permute-start | bytes 368648 | tf_op jit(solution)/shard_map/ppermute | solution.py:214
  22.0 3.6 %collective-permute-start.12 = (bf16[32,1920]{1,0:T(8,128)(2,1)S(1)}, bf16[32,1920]{1,0:T(8,128)(2,1)S(1)}, u32[]{:S(2)}, u32[]{:S(2)}) collective-permute-start(bf16[32,1920]{1,0:T(8,128)(2,1)S(1)} %collective-permute-done.8.refs_3_), channel_id=1, source_target_pairs={{0,1},{1,0},{2,3},{3,2},{4,5},{5,4},{6,7},{7,6},{8,9},{9,8},{10,11... | collective-permute-start | bytes 368648 | tf_op jit(solution)/shard_map/ppermute | solution.py:214
  22.0 9.6 %collective-permute-start.14 = (bf16[32,1920]{1,0:T(8,128)(2,1)S(1)}, bf16[32,1920]{1,0:T(8,128)(2,1)S(1)}, u32[]{:S(2)}, u32[]{:S(2)}) collective-permute-start(bf16[32,1920]{1,0:T(8,128)(2,1)S(1)} %maximum_bitcast_fusion.refs_0_), channel_id=1, source_target_pairs={{0,18},{1,19},{2,16},{3,17},{4,22},{5,23},{6,20},{7,21},{8,26},{9,... | collective-permute-start | bytes 368648 | tf_op jit(solution)/shard_map/ppermute | solution.py:214
  23.6 8.1 %collective-permute-start.13 = (bf16[32,1920]{1,0:T(8,128)(2,1)S(1)}, bf16[32,1920]{1,0:T(8,128)(2,1)S(1)}, u32[]{:S(2)}, u32[]{:S(2)}) collective-permute-start(bf16[32,1920]{1,0:T(8,128)(2,1)S(1)} %maximum_bitcast_fusion.refs_0_), channel_id=1, source_target_pairs={{0,2},{1,3},{2,0},{3,1},{4,6},{5,7},{6,4},{7,5},{8,10},{9,11},{10,... | collective-permute-start | bytes 368648 | tf_op jit(solution)/shard_map/ppermute | solution.py:214
  24.1 8.0 %collective-permute-start.2 = (bf16[32,1920]{1,0:T(8,128)(2,1)S(1)}, bf16[32,1920]{1,0:T(8,128)(2,1)S(1)}, u32[]{:S(2)}, u32[]{:S(2)}) collective-permute-start(bf16[32,1920]{1,0:T(8,128)(2,1)S(1)} %maximum_bitcast_fusion.refs_0_), channel_id=1, source_target_pairs={{0,16},{1,17},{2,18},{3,19},{4,20},{5,21},{6,22},{7,23},{8,24},{9,... | collective-permute-start | bytes 368648 | tf_op jit(solution)/shard_map/ppermute | solution.py:214
  31.0 1.4 %collective-permute-start.30 = (bf16[32,1792]{1,0:T(8,128)(2,1)S(1)}, bf16[32,1792]{1,0:T(8,128)(2,1)S(1)}, u32[]{:S(2)}, u32[]{:S(2)}) collective-permute-start(bf16[32,1792]{1,0:T(8,128)(2,1)S(1)} %get-tuple-element.43), channel_id=1, source_target_pairs={{0,1},{1,0},{2,3},{3,2},{4,5},{5,4},{6,7},{7,6},{8,9},{9,8},{10,11... | collective-permute-start | bytes 344072 | tf_op jit(solution)/shard_map/ppermute | solution.py:214
  31.1 2.5 %collective-permute-start.15 = (bf16[32,1920]{1,0:T(8,128)(2,1)S(1)}, bf16[32,1920]{1,0:T(8,128)(2,1)S(1)}, u32[]{:S(2)}, u32[]{:S(2)}) collective-permute-start(bf16[32,1920]{1,0:T(8,128)(2,1)S(1)} %maximum_bitcast_fusion.refs_0_), channel_id=1, source_target_pairs={{0,1},{1,0},{2,3},{3,2},{4,5},{5,4},{6,7},{7,6},{8,9},{9,8},{10,11... | collective-permute-start | bytes 368648 | tf_op jit(solution)/shard_map/ppermute | solution.py:214
  31.6 1.3 %collective-permute-start.32 = (bf16[32,1792]{1,0:T(8,128)(2,1)S(1)}, bf16[32,1792]{1,0:T(8,128)(2,1)S(1)}, u32[]{:S(2)}, u32[]{:S(2)}) collective-permute-start(bf16[32,1792]{1,0:T(8,128)(2,1)S(1)} %get-tuple-element.45), channel_id=1, source_target_pairs={{0,1},{1,0},{2,3},{3,2},{4,5},{5,4},{6,7},{7,6},{8,9},{9,8},{10,11... | collective-permute-start | bytes 344072 | tf_op jit(solution)/shard_map/ppermute | solution.py:214
  31.7 1.5 %collective-permute-start.34 = (bf16[32,1792]{1,0:T(8,128)(2,1)S(1)}, bf16[32,1792]{1,0:T(8,128)(2,1)S(1)}, u32[]{:S(2)}, u32[]{:S(2)}) collective-permute-start(bf16[32,1792]{1,0:T(8,128)(2,1)S(1)} %get-tuple-element.47), channel_id=1, source_target_pairs={{0,1},{1,0},{2,3},{3,2},{4,5},{5,4},{6,7},{7,6},{8,9},{9,8},{10,11... | collective-permute-start | bytes 344072 | tf_op jit(solution)/shard_map/ppermute | solution.py:214
  32.1 11.6 %collective-permute-start.29 = (bf16[32,1792]{1,0:T(8,128)(2,1)S(1)}, bf16[32,1792]{1,0:T(8,128)(2,1)S(1)}, u32[]{:S(2)}, u32[]{:S(2)}) collective-permute-start(bf16[32,1792]{1,0:T(8,128)(2,1)S(1)} %get-tuple-element.41), channel_id=1, source_target_pairs={{0,1},{1,0},{2,3},{3,2},{4,5},{5,4},{6,7},{7,6},{8,9},{9,8},{10,11... | collective-permute-start | bytes 344072 | tf_op jit(solution)/shard_map/ppermute | solution.py:214
  32.4 2.7 %collective-permute-start.18 = (bf16[32,1920]{1,0:T(8,128)(2,1)S(1)}, bf16[32,1920]{1,0:T(8,128)(2,1)S(1)}, u32[]{:S(2)}, u32[]{:S(2)}) collective-permute-start(bf16[32,1920]{1,0:T(8,128)(2,1)S(1)} %collective-permute-done.14.refs_3_), channel_id=1, source_target_pairs={{0,1},{1,0},{2,3},{3,2},{4,5},{5,4},{6,7},{7,6},{8,9},{9,8},{10,11... | collective-permute-start | bytes 368648 | tf_op jit(solution)/shard_map/ppermute | solution.py:214
  32.9 2.8 %collective-permute-start.17 = (bf16[32,1920]{1,0:T(8,128)(2,1)S(1)}, bf16[32,1920]{1,0:T(8,128)(2,1)S(1)}, u32[]{:S(2)}, u32[]{:S(2)}) collective-permute-start(bf16[32,1920]{1,0:T(8,128)(2,1)S(1)} %collective-permute-done.13.refs_2_), channel_id=1, source_target_pairs={{0,1},{1,0},{2,3},{3,2},{4,5},{5,4},{6,7},{7,6},{8,9},{9,8},{10,11... | collective-permute-start | bytes 368648 | tf_op jit(solution)/shard_map/ppermute | solution.py:214
  33.1 4.0 %collective-permute-start.16 = (bf16[32,1920]{1,0:T(8,128)(2,1)S(1)}, bf16[32,1920]{1,0:T(8,128)(2,1)S(1)}, u32[]{:S(2)}, u32[]{:S(2)}) collective-permute-start(bf16[32,1920]{1,0:T(8,128)(2,1)S(1)} %collective-permute-done.2.refs_1_), channel_id=1, source_target_pairs={{0,1},{1,0},{2,3},{3,2},{4,5},{5,4},{6,7},{7,6},{8,9},{9,8},{10,11... | collective-permute-start | bytes 368648 | tf_op jit(solution)/shard_map/ppermute | solution.py:214
  33.5 8.7 %slice-start = ((s8[9175040]{0:T(1024)(128)(4,1)}), s8[4194304]{0:T(1024)(128)(4,1)S(1)}, s32[]{:S(2)}) async-start(s8[9175040]{0:T(1024)(128)(4,1)} %bitcast.13), calls=%async_computation | async-start | bytes 8388608
  33.6 8.7 %slice-start.1 = ((s8[9175040]{0:T(1024)(128)(4,1)}), s8[4194304]{0:T(1024)(128)(4,1)S(1)}, s32[]{:S(2)}) async-start(s8[9175040]{0:T(1024)(128)(4,1)} %bitcast.13), calls=%async_computation.1 | async-start | bytes 8388608
  33.6 8.7 %slice-start.2 = ((s8[9175040]{0:T(1024)(128)(4,1)}), s8[786432]{0:T(1024)(128)(4,1)S(1)}, s32[]{:S(2)}) async-start(s8[9175040]{0:T(1024)(128)(4,1)} %bitcast.13), calls=%async_computation.2 | async-start | bytes 1572864
  33.6 10.6 %collective-permute-start.31 = (bf16[32,1792]{1,0:T(8,128)(2,1)S(1)}, bf16[32,1792]{1,0:T(8,128)(2,1)S(1)}, u32[]{:S(2)}, u32[]{:S(2)}) collective-permute-start(bf16[32,1792]{1,0:T(8,128)(2,1)S(1)} %add_convert_fusion.3), channel_id=1, source_target_pairs={{0,18},{1,19},{2,16},{3,17},{4,22},{5,23},{6,20},{7,21},{8,26},{9,... | collective-permute-start | bytes 344072 | tf_op jit(solution)/shard_map/ppermute | solution.py:214
  35.1 9.2 %collective-permute-start.33 = (bf16[32,1792]{1,0:T(8,128)(2,1)S(1)}, bf16[32,1792]{1,0:T(8,128)(2,1)S(1)}, u32[]{:S(2)}, u32[]{:S(2)}) collective-permute-start(bf16[32,1792]{1,0:T(8,128)(2,1)S(1)} %add_convert_fusion.2), channel_id=1, source_target_pairs={{0,16},{1,17},{2,18},{3,19},{4,20},{5,21},{6,22},{7,23},{8,24},{9,... | collective-permute-start | bytes 344072 | tf_op jit(solution)/shard_map/ppermute | solution.py:214
  35.7 9.1 %collective-permute-start.35 = (bf16[32,1792]{1,0:T(8,128)(2,1)S(1)}, bf16[32,1792]{1,0:T(8,128)(2,1)S(1)}, u32[]{:S(2)}, u32[]{:S(2)}) collective-permute-start(bf16[32,1792]{1,0:T(8,128)(2,1)S(1)} %add_convert_fusion.1), channel_id=1, source_target_pairs={{0,2},{1,3},{2,0},{3,1},{4,6},{5,7},{6,4},{7,5},{8,10},{9,11},{10,... | collective-permute-start | bytes 344072 | tf_op jit(solution)/shard_map/ppermute | solution.py:214
  43.7 1.4 %collective-permute-start.20 = (bf16[32,1792]{1,0:T(8,128)(2,1)S(1)}, bf16[32,1792]{1,0:T(8,128)(2,1)S(1)}, u32[]{:S(2)}, u32[]{:S(2)}) collective-permute-start(bf16[32,1792]{1,0:T(8,128)(2,1)S(1)} %get-tuple-element.36), channel_id=1, source_target_pairs={{0,1},{1,0},{2,3},{3,2},{4,5},{5,4},{6,7},{7,6},{8,9},{9,8},{10,11... | collective-permute-start | bytes 344072 | tf_op jit(solution)/shard_map/ppermute | solution.py:214
  43.8 2.9 %collective-permute-start.22 = (bf16[32,1792]{1,0:T(8,128)(2,1)S(1)}, bf16[32,1792]{1,0:T(8,128)(2,1)S(1)}, u32[]{:S(2)}, u32[]{:S(2)}) collective-permute-start(bf16[32,1792]{1,0:T(8,128)(2,1)S(1)} %get-tuple-element.38), channel_id=1, source_target_pairs={{0,1},{1,0},{2,3},{3,2},{4,5},{5,4},{6,7},{7,6},{8,9},{9,8},{10,11... | collective-permute-start | bytes 344072 | tf_op jit(solution)/shard_map/ppermute | solution.py:214
  44.3 3.0 %collective-permute-start.24 = (bf16[32,1792]{1,0:T(8,128)(2,1)S(1)}, bf16[32,1792]{1,0:T(8,128)(2,1)S(1)}, u32[]{:S(2)}, u32[]{:S(2)}) collective-permute-start(bf16[32,1792]{1,0:T(8,128)(2,1)S(1)} %get-tuple-element.40), channel_id=1, source_target_pairs={{0,1},{1,0},{2,3},{3,2},{4,5},{5,4},{6,7},{7,6},{8,9},{9,8},{10,11... | collective-permute-start | bytes 344072 | tf_op jit(solution)/shard_map/ppermute | solution.py:214
  44.3 5.1 %collective-permute-start.19 = (bf16[32,1792]{1,0:T(8,128)(2,1)S(1)}, bf16[32,1792]{1,0:T(8,128)(2,1)S(1)}, u32[]{:S(2)}, u32[]{:S(2)}) collective-permute-start(bf16[32,1792]{1,0:T(8,128)(2,1)S(1)} %get-tuple-element.34), channel_id=1, source_target_pairs={{0,1},{1,0},{2,3},{3,2},{4,5},{5,4},{6,7},{7,6},{8,9},{9,8},{10,11... | collective-permute-start | bytes 344072 | tf_op jit(solution)/shard_map/ppermute | solution.py:214
  45.1 7.0 %collective-permute-start.21 = (bf16[32,1792]{1,0:T(8,128)(2,1)S(1)}, bf16[32,1792]{1,0:T(8,128)(2,1)S(1)}, u32[]{:S(2)}, u32[]{:S(2)}) collective-permute-start(bf16[32,1792]{1,0:T(8,128)(2,1)S(1)} %add_convert_fusion.8), channel_id=1, source_target_pairs={{0,18},{1,19},{2,16},{3,17},{4,22},{5,23},{6,20},{7,21},{8,26},{9,... | collective-permute-start | bytes 344072 | tf_op jit(solution)/shard_map/ppermute | solution.py:214
  46.7 7.0 %collective-permute-start.23 = (bf16[32,1792]{1,0:T(8,128)(2,1)S(1)}, bf16[32,1792]{1,0:T(8,128)(2,1)S(1)}, u32[]{:S(2)}, u32[]{:S(2)}) collective-permute-start(bf16[32,1792]{1,0:T(8,128)(2,1)S(1)} %add_convert_fusion.7), channel_id=1, source_target_pairs={{0,16},{1,17},{2,18},{3,19},{4,20},{5,21},{6,22},{7,23},{8,24},{9,... | collective-permute-start | bytes 344072 | tf_op jit(solution)/shard_map/ppermute | solution.py:214
  47.3 6.4 %collective-permute-start.25 = (bf16[32,1792]{1,0:T(8,128)(2,1)S(1)}, bf16[32,1792]{1,0:T(8,128)(2,1)S(1)}, u32[]{:S(2)}, u32[]{:S(2)}) collective-permute-start(bf16[32,1792]{1,0:T(8,128)(2,1)S(1)} %add_convert_fusion.6), channel_id=1, source_target_pairs={{0,2},{1,3},{2,0},{3,1},{4,6},{5,7},{6,4},{7,5},{8,10},{9,11},{10,... | collective-permute-start | bytes 344072 | tf_op jit(solution)/shard_map/ppermute | solution.py:214
  48.9 6.9 %collective-permute-start.36 = (bf16[8,1792]{1,0:T(8,128)(2,1)S(1)}, bf16[8,1792]{1,0:T(8,128)(2,1)S(1)}, u32[]{:S(2)}, u32[]{:S(2)}) collective-permute-start(bf16[8,1792]{1,0:T(8,128)(2,1)S(1)} %get-tuple-element.48), channel_id=1, source_target_pairs={{0,12},{1,13},{2,14},{3,15},{4,8},{5,9},{6,10},{7,11},{8,4},{9,5},... | collective-permute-start | bytes 86024 | tf_op jit(solution)/shard_map/ppermute | solution.py:214
  49.5 8.8 %collective-permute-start.37 = (bf16[8,1792]{1,0:T(8,128)(2,1)S(1)}, bf16[8,1792]{1,0:T(8,128)(2,1)S(1)}, u32[]{:S(2)}, u32[]{:S(2)}) collective-permute-start(bf16[8,1792]{1,0:T(8,128)(2,1)S(1)} %get-tuple-element.50), channel_id=1, source_target_pairs={{0,8},{1,9},{2,10},{3,11},{4,12},{5,13},{6,14},{7,15},{8,0},{9,1},... | collective-permute-start | bytes 86024 | tf_op jit(solution)/shard_map/ppermute | solution.py:214
  52.1 6.2 %collective-permute-start.38 = (bf16[8,1792]{1,0:T(8,128)(2,1)S(1)}, bf16[8,1792]{1,0:T(8,128)(2,1)S(1)}, u32[]{:S(2)}, u32[]{:S(2)}) collective-permute-start(bf16[8,1792]{1,0:T(8,128)(2,1)S(1)} %get-tuple-element.49), channel_id=1, source_target_pairs={{0,4},{1,5},{2,6},{3,7},{4,0},{5,1},{6,2},{7,3},{8,12},{9,13},{10,... | collective-permute-start | bytes 86024 | tf_op jit(solution)/shard_map/ppermute | solution.py:214
  53.8 5.7 %collective-permute-start.26 = (bf16[8,1792]{1,0:T(8,128)(2,1)S(1)}, bf16[8,1792]{1,0:T(8,128)(2,1)S(1)}, u32[]{:S(2)}, u32[]{:S(2)}) collective-permute-start(bf16[8,1792]{1,0:T(8,128)(2,1)S(1)} %get-tuple-element.51), channel_id=1, source_target_pairs={{0,12},{1,13},{2,14},{3,15},{4,8},{5,9},{6,10},{7,11},{8,4},{9,5},... | collective-permute-start | bytes 86024 | tf_op jit(solution)/shard_map/ppermute | solution.py:214
  54.5 5.1 %collective-permute-start.27 = (bf16[8,1792]{1,0:T(8,128)(2,1)S(1)}, bf16[8,1792]{1,0:T(8,128)(2,1)S(1)}, u32[]{:S(2)}, u32[]{:S(2)}) collective-permute-start(bf16[8,1792]{1,0:T(8,128)(2,1)S(1)} %get-tuple-element.53), channel_id=1, source_target_pairs={{0,8},{1,9},{2,10},{3,11},{4,12},{5,13},{6,14},{7,15},{8,0},{9,1},... | collective-permute-start | bytes 86024 | tf_op jit(solution)/shard_map/ppermute | solution.py:214
  55.7 4.4 %collective-permute-start.28 = (bf16[8,1792]{1,0:T(8,128)(2,1)S(1)}, bf16[8,1792]{1,0:T(8,128)(2,1)S(1)}, u32[]{:S(2)}, u32[]{:S(2)}) collective-permute-start(bf16[8,1792]{1,0:T(8,128)(2,1)S(1)} %get-tuple-element.52), channel_id=1, source_target_pairs={{0,4},{1,5},{2,6},{3,7},{4,0},{5,1},{6,2},{7,3},{8,12},{9,13},{10,... | collective-permute-start | bytes 86024 | tf_op jit(solution)/shard_map/ppermute | solution.py:214

commit v5 on v4

--- a/solution.py
+++ b/solution.py
@@ -168,7 +168,7 @@
         kernel,
         out_shape=shapes,
         scratch_shapes=scratch,
-        compiler_params=pltpu.CompilerParams(vmem_limit_bytes=24 << 20),
+        compiler_params=pltpu.CompilerParams(vmem_limit_bytes=8 << 20),
         cost_estimate=cost,
         name=name,
     )(*given, *weights)
@@ -236,7 +236,8 @@
 
 
 def spread_plane(held):
-    return [held, move(held, Y, 32), move(held, X, 32), move(held, X ^ Y, 32)]
+    diagonal = move(held, X ^ Y, 32)
+    return [held, move(held, Y, 32), move(held, X, 32), diagonal]
 
 
 def swap(pieces):

time: 60.9 us -> 60.9 us (level)
  transfers between devices with their start and end apart: 39 -> 39, of which waited for: 12 -> 12; matrix products, arithmetic and copies ran while one was open for 2% -> 2% of each run, Pallas kernels for 19% -> 20%
where the time goes in v5:
time: 60.9 us; the launch traced here: 60.7 us
  starting transfers between devices  31.8 us (52%)
  waiting for transfers between devices  13.4 us (22%)
  Pallas kernels  13 us (21%)
  other arithmetic  1.62 us (3%)
  between operations  0.87 us (1%)
    ppermute x39, starting transfers between devices, move(): return lax.ppermute(value, AXES, [(i, i ^ mask) for i in range(devices)])  31.8 us
    ppermute x39, waiting for transfers between devices, move(): return lax.ppermute(value, AXES, [(i, i ^ mask) for i in range(devices)])  13.4 us
    pallas_call x3, Pallas kernels, expert_call(): pl.pallas_call(kernel, out_shape=shapes, scratch_shapes=scratch, compiler...  11.8 us
    convert_element_type x10, other arithmetic, add(): return sum((p.astype(jnp.float32) for p in parts)).astype(jnp.bfloat16)  1.59 us
  transfers between devices with their start and end apart: 39, of which 12 were waited for; matrix products, arithmetic and copies ran while one was open for 2% of the time, Pallas kernels for 20%

profile of v5, /device:TPU:0, one launch (start us, length us, event | category | flops | bytes accessed | tf_op | source)
XLA Modules:
  0.0 60.7 jit_solution(4955954202536701368)
XLA Ops:
  0.7 1.1 %pack.1 = (bf16[8,1920]{1,0:T(8,128)(2,1)S(1)}, bf16[8,1920]{1,0:T(8,128)(2,1)S(1)}) custom-call(bf16[8,1792]{1,0:T(8,128)(2,1)} %refs_0_.1, s32[8,8]{1,0:T(8,128)} %refs_1_.1, f32[8,8]{1,0:T(8,128)} %refs_2_.1, bf16[8,1792]{1,0:T(8,128)(2,1)} %refs_3_.1, s32[8,8]{1,0:T(8,128)} %refs_4_.1, f32[8,8]{1,0:T(8,128)} %refs_5_.1), custom_call_target="tpu_custom_call" | custom-call | flops 40000000000 | bytes 100000000 | tf_op jit(solution)/shard_map/pack/pallas_call | solution.py:57
  1.8 4.1 %collective-permute-start.3 = (bf16[8,1920]{1,0:T(8,128)(2,1)S(1)}, bf16[8,1920]{1,0:T(8,128)(2,1)S(1)}, u32[]{:S(2)}, u32[]{:S(2)}) collective-permute-start(bf16[8,1920]{1,0:T(8,128)(2,1)S(1)} %get-tuple-element.26), channel_id=1, source_target_pairs={{0,8},{1,9},{2,10},{3,11},{4,12},{5,13},{6,14},{7,15},{8,0},{9,1},... | collective-permute-start | bytes 92168 | tf_op jit(solution)/shard_map/ppermute | solution.py:214
  5.9 1.6 %collective-permute-start.4 = (bf16[8,1920]{1,0:T(8,128)(2,1)S(1)}, bf16[8,1920]{1,0:T(8,128)(2,1)S(1)}, u32[]{:S(2)}, u32[]{:S(2)}) collective-permute-start(bf16[8,1920]{1,0:T(8,128)(2,1)S(1)} %get-tuple-element.26), channel_id=1, source_target_pairs={{0,4},{1,5},{2,6},{3,7},{4,0},{5,1},{6,2},{7,3},{8,12},{9,13},{10,... | collective-permute-start | bytes 92168 | tf_op jit(solution)/shard_map/ppermute | solution.py:214
  7.5 0.0 collective-permute-start.5
  7.5 1.9 %collective-permute-start = (bf16[1,8,1920]{2,1,0:T(8,128)(2,1)S(1)}, bf16[1,8,1920]{2,1,0:T(8,128)(2,1)S(1)}, u32[]{:S(2)}, u32[]{:S(2)}) collective-permute-start(bf16[1,8,1920]{2,1,0:T(8,128)(2,1)S(1)} %bitcast.16), channel_id=1, source_target_pairs={{0,8},{1,9},{2,10},{3,11},{4,12},{5,13},{6,14},{7,15},{8,0},{9,1},... | collective-permute-start | bytes 92168 | tf_op jit(solution)/shard_map/ppermute | solution.py:214
  9.4 0.0 collective-permute-done.3
  9.4 0.4 collective-permute-done.4
  9.8 3.4 %collective-permute-done.5 = bf16[8,1920]{1,0:T(8,128)(2,1)S(1)} collective-permute-done((bf16[8,1920]{1,0:T(8,128)(2,1)S(1)}, bf16[8,1920]{1,0:T(8,128)(2,1)S(1)}, u32[]{:S(2)}, u32[]{:S(2)}) %collective-permute-start.5) | collective-permute-done | bytes 30752 | tf_op jit(solution)/shard_map/ppermute | solution.py:214
  13.2 1.5 %collective-permute-start.6 = (bf16[32,1920]{1,0:T(8,128)(2,1)S(1)}, bf16[32,1920]{1,0:T(8,128)(2,1)S(1)}, u32[]{:S(2)}, u32[]{:S(2)}) collective-permute-start(bf16[32,1920]{1,0:T(8,128)(2,1)S(1)} %constant_dynamic-update-slice_fusion.refs_0_), channel_id=1, source_target_pairs={{0,16},{1,17},{2,18},{3,19},{4,20},{5,21},{6,22},{7,23},{8,24},{9,... | collective-permute-start | bytes 368648 | tf_op jit(solution)/shard_map/ppermute | solution.py:214
  14.7 1.5 %collective-permute-start.7 = (bf16[32,1920]{1,0:T(8,128)(2,1)S(1)}, bf16[32,1920]{1,0:T(8,128)(2,1)S(1)}, u32[]{:S(2)}, u32[]{:S(2)}) collective-permute-start(bf16[32,1920]{1,0:T(8,128)(2,1)S(1)} %constant_dynamic-update-slice_fusion.refs_0_), channel_id=1, source_target_pairs={{0,2},{1,3},{2,0},{3,1},{4,6},{5,7},{6,4},{7,5},{8,10},{9,11},{10,... | collective-permute-start | bytes 368648 | tf_op jit(solution)/shard_map/ppermute | solution.py:214
  16.2 0.5 collective-permute-start.8
  16.7 0.1 collective-permute-start.1
  16.8 0.1 collective-permute-start.9
  16.9 2.5 %collective-permute-done.6.refs_1_ = bf16[32,1920]{1,0:T(8,128)(2,1)S(1)} collective-permute-done((bf16[32,1920]{1,0:T(8,128)(2,1)S(1)}, bf16[32,1920]{1,0:T(8,128)(2,1)S(1)}, u32[]{:S(2)}, u32[]{:S(2)}) %collective-permute-start.6) | collective-permute-done | bytes 122912 | tf_op jit(solution)/shard_map/ppermute | solution.py:214
  19.4 0.0 collective-permute-start.10
  19.4 0.2 collective-permute-done.7.refs_2_
  19.6 0.3 collective-permute-start.11
  19.9 2.1 %collective-permute-done.8.refs_3_ = bf16[32,1920]{1,0:T(8,128)(2,1)S(1)} collective-permute-done((bf16[32,1920]{1,0:T(8,128)(2,1)S(1)}, bf16[32,1920]{1,0:T(8,128)(2,1)S(1)}, u32[]{:S(2)}, u32[]{:S(2)}) %collective-permute-start.8) | collective-permute-done | bytes 122912 | tf_op jit(solution)/shard_map/ppermute | solution.py:214
  22.0 0.0 collective-permute-start.12
  22.0 0.0 collective-permute-done.1
  22.0 1.5 %collective-permute-start.14 = (bf16[32,1920]{1,0:T(8,128)(2,1)S(1)}, bf16[32,1920]{1,0:T(8,128)(2,1)S(1)}, u32[]{:S(2)}, u32[]{:S(2)}) collective-permute-start(bf16[32,1920]{1,0:T(8,128)(2,1)S(1)} %maximum_bitcast_fusion.refs_0_), channel_id=1, source_target_pairs={{0,18},{1,19},{2,16},{3,17},{4,22},{5,23},{6,20},{7,21},{8,26},{9,... | collective-permute-start | bytes 368648 | tf_op jit(solution)/shard_map/ppermute | solution.py:214
  23.5 0.0 collective-permute-done.9.refs_4_
  23.6 0.5 collective-permute-start.13
  24.1 1.5 %collective-permute-start.2 = (bf16[32,1920]{1,0:T(8,128)(2,1)S(1)}, bf16[32,1920]{1,0:T(8,128)(2,1)S(1)}, u32[]{:S(2)}, u32[]{:S(2)}) collective-permute-start(bf16[32,1920]{1,0:T(8,128)(2,1)S(1)} %maximum_bitcast_fusion.refs_0_), channel_id=1, source_target_pairs={{0,16},{1,17},{2,18},{3,19},{4,20},{5,21},{6,22},{7,23},{8,24},{9,... | collective-permute-start | bytes 368648 | tf_op jit(solution)/shard_map/ppermute | solution.py:214
  25.6 5.4 %experts_backward.1 = (bf16[32,1792]{1,0:T(8,128)(2,1)S(1)}, bf16[32,1792]{1,0:T(8,128)(2,1)S(1)}, bf16[32,1792]{1,0:T(8,128)(2,1)S(1)}, bf16[32,1792]{1,0:T(8,1...) custom-call(bf16[32,1920]{1,0:T(8,128)(2,1)S(1)} %constant_dynamic-u, ...), custom_call_target="tpu_custom_call" | custom-call | flops 3523215360 | bytes 27525120 | tf_op jit(solution)/shard_map/experts_backward/pallas_call | solution.py:167
  31.0 0.1 collective-permute-start.30
  31.1 0.5 collective-permute-start.15
  31.6 0.0 collective-permute-done.14.refs_3_
  31.6 0.1 collective-permute-start.32
  31.7 0.4 collective-permute-start.34
  32.1 0.0 collective-permute-done.2.refs_1_
  32.1 0.1 collective-permute-start.29
  32.2 0.2 collective-permute-done.30
  32.4 0.2 collective-permute-start.18
  32.7 0.3 collective-permute-done.32
  32.9 0.2 collective-permute-start.17
  33.1 0.4 collective-permute-start.16
  33.6 1.5 %collective-permute-start.31 = (bf16[32,1792]{1,0:T(8,128)(2,1)S(1)}, bf16[32,1792]{1,0:T(8,128)(2,1)S(1)}, u32[]{:S(2)}, u32[]{:S(2)}) collective-permute-start(bf16[32,1792]{1,0:T(8,128)(2,1)S(1)} %add_convert_fusion.3), channel_id=1, source_target_pairs={{0,18},{1,19},{2,16},{3,17},{4,22},{5,23},{6,20},{7,21},{8,26},{9,... | collective-permute-start | bytes 344072 | tf_op jit(solution)/shard_map/ppermute | solution.py:214
  35.1 0.5 collective-permute-start.33
  35.7 1.5 %collective-permute-start.35 = (bf16[32,1792]{1,0:T(8,128)(2,1)S(1)}, bf16[32,1792]{1,0:T(8,128)(2,1)S(1)}, u32[]{:S(2)}, u32[]{:S(2)}) collective-permute-start(bf16[32,1792]{1,0:T(8,128)(2,1)S(1)} %add_convert_fusion.1), channel_id=1, source_target_pairs={{0,2},{1,3},{2,0},{3,1},{4,6},{5,7},{6,4},{7,5},{8,10},{9,11},{10,... | collective-permute-start | bytes 344072 | tf_op jit(solution)/shard_map/ppermute | solution.py:214
  37.2 5.1 %forward_hidden.1 = (bf16[128,1280]{1,0:T(8,128)(2,1)S(1)}, f32[128,1]{1,0:T(8,128)S(1)}) custom-call(bf16[32,1920]{1,0:T(8,128)(2,1)S(1)} %maximum_bitcast_fusion.refs_0_, bf16[32,1920]{1,0:T(8,128)(2,1)S(1)} %collective-permute-done.2.refs_1_, bf16[32,1920]{1,0:T(8,128)(2,1)S(1)} %collective-permute-done.13.refs_2_, ...), custom_call_target="tpu_custom_call" | custom-call | flops 2348810240 | bytes 18350080 | tf_op jit(solution)/shard_map/forward_hidden/pallas_call | solution.py:167
  42.2 1.4 %forward_down.1 = (bf16[32,1792]{1,0:T(8,128)(2,1)S(1)}, bf16[32,1792]{1,0:T(8,128)(2,1)S(1)}, bf16[32,1792]{1,0:T(8,128)(2,1)S(1)}, bf16[32,1792]{1,0:T(8,128)(...) custom-call(bf16[128,1280]{1,0:T(8,128)(2,1)S(1)} %get-tuple-element, ...), custom_call_target="tpu_custom_call" | custom-call | flops 1174405120 | bytes 9175040 | tf_op jit(solution)/shard_map/forward_down/pallas_call | solution.py:167
  43.6 0.1 collective-permute-start.20
  43.7 0.5 collective-permute-start.22
  44.2 0.1 collective-permute-start.24
  44.3 0.4 collective-permute-start.19
  44.7 0.1 add_convert_fusion
  44.8 0.2 collective-permute-done.20
  45.0 1.5 %collective-permute-start.21 = (bf16[32,1792]{1,0:T(8,128)(2,1)S(1)}, bf16[32,1792]{1,0:T(8,128)(2,1)S(1)}, u32[]{:S(2)}, u32[]{:S(2)}) collective-permute-start(bf16[32,1792]{1,0:T(8,128)(2,1)S(1)} %add_convert_fusion.8), channel_id=1, source_target_pairs={{0,18},{1,19},{2,16},{3,17},{4,22},{5,23},{6,20},{7,21},{8,26},{9,... | collective-permute-start | bytes 344072 | tf_op jit(solution)/shard_map/ppermute | solution.py:214
  46.6 0.6 collective-permute-start.23
  47.2 1.6 %collective-permute-start.25 = (bf16[32,1792]{1,0:T(8,128)(2,1)S(1)}, bf16[32,1792]{1,0:T(8,128)(2,1)S(1)}, u32[]{:S(2)}, u32[]{:S(2)}) collective-permute-start(bf16[32,1792]{1,0:T(8,128)(2,1)S(1)} %add_convert_fusion.6), channel_id=1, source_target_pairs={{0,2},{1,3},{2,0},{3,1},{4,6},{5,7},{6,4},{7,5},{8,10},{9,11},{10,... | collective-permute-start | bytes 344072 | tf_op jit(solution)/shard_map/ppermute | solution.py:214
  48.8 0.6 collective-permute-start.36
  49.4 0.2 collective-permute-start.37
  49.6 2.4 %collective-permute-done.21 = bf16[32,1792]{1,0:T(8,128)(2,1)S(1)} collective-permute-done((bf16[32,1792]{1,0:T(8,128)(2,1)S(1)}, bf16[32,1792]{1,0:T(8,128)(2,1)S(1)}, u32[]{:S(2)}, u32[]{:S(2)}) %collective-permute-start.21) | collective-permute-done | bytes 114720 | tf_op jit(solution)/shard_map/ppermute | solution.py:214
  52.0 1.2 %collective-permute-start.38 = (bf16[8,1792]{1,0:T(8,128)(2,1)S(1)}, bf16[8,1792]{1,0:T(8,128)(2,1)S(1)}, u32[]{:S(2)}, u32[]{:S(2)}) collective-permute-start(bf16[8,1792]{1,0:T(8,128)(2,1)S(1)} %get-tuple-element.49), channel_id=1, source_target_pairs={{0,4},{1,5},{2,6},{3,7},{4,0},{5,1},{6,2},{7,3},{8,12},{9,13},{10,... | collective-permute-start | bytes 86024 | tf_op jit(solution)/shard_map/ppermute | solution.py:214
  53.2 0.5 collective-permute-done.23
  53.7 0.1 add_convert_fusion.5
  53.8 0.7 %collective-permute-start.26 = (bf16[8,1792]{1,0:T(8,128)(2,1)S(1)}, bf16[8,1792]{1,0:T(8,128)(2,1)S(1)}, u32[]{:S(2)}, u32[]{:S(2)}) collective-permute-start(bf16[8,1792]{1,0:T(8,128)(2,1)S(1)} %get-tuple-element.51), channel_id=1, source_target_pairs={{0,12},{1,13},{2,14},{3,15},{4,8},{5,9},{6,10},{7,11},{8,4},{9,5},... | collective-permute-start | bytes 86024 | tf_op jit(solution)/shard_map/ppermute | solution.py:214
  54.4 1.2 %collective-permute-start.27 = (bf16[8,1792]{1,0:T(8,128)(2,1)S(1)}, bf16[8,1792]{1,0:T(8,128)(2,1)S(1)}, u32[]{:S(2)}, u32[]{:S(2)}) collective-permute-start(bf16[8,1792]{1,0:T(8,128)(2,1)S(1)} %get-tuple-element.53), channel_id=1, source_target_pairs={{0,8},{1,9},{2,10},{3,11},{4,12},{5,13},{6,14},{7,15},{8,0},{9,1},... | collective-permute-start | bytes 86024 | tf_op jit(solution)/shard_map/ppermute | solution.py:214
  55.7 2.5 %collective-permute-start.28 = (bf16[8,1792]{1,0:T(8,128)(2,1)S(1)}, bf16[8,1792]{1,0:T(8,128)(2,1)S(1)}, u32[]{:S(2)}, u32[]{:S(2)}) collective-permute-start(bf16[8,1792]{1,0:T(8,128)(2,1)S(1)} %get-tuple-element.52), channel_id=1, source_target_pairs={{0,4},{1,5},{2,6},{3,7},{4,0},{5,1},{6,2},{7,3},{8,12},{9,13},{10,... | collective-permute-start | bytes 86024 | tf_op jit(solution)/shard_map/ppermute | solution.py:214
  58.2 0.6 %add_convert_fusion.10 = bf16[8,1792]{1,0:T(8,128)(2,1)} fusion(bf16[8,1792]{1,0:T(8,128)(2,1)S(1)} %collective-permute-done.38, bf16[8,1792]{1,0:T(8,128)(2,1)S(1)} %collective-permute-done.37, bf16[8,1792]{1,0:T(8,128)(2,1)S(1)} %collective-permute-done.36, bf16[32,1792]{1,0:T(8,128)(2,1)S(1)} %add_convert_fusion), kind=kLoop, calls=%fused_computation.12 | loop fusion | flops 114688 | bytes 143360 | tf_op jit(solution)/shard_map/convert_element_type | solution.py:248
  58.9 0.6 %collective-permute-done.26 = bf16[8,1792]{1,0:T(8,128)(2,1)S(1)} collective-permute-done((bf16[8,1792]{1,0:T(8,128)(2,1)S(1)}, bf16[8,1792]{1,0:T(8,128)(2,1)S(1)}, u32[]{:S(2)}, u32[]{:S(2)}) %collective-permute-start.26) | collective-permute-done | bytes 28704 | tf_op jit(solution)/shard_map/ppermute | solution.py:214
  59.5 0.6 collective-permute-done.28
  60.1 0.6 %add_convert_fusion.11 = bf16[8,1792]{1,0:T(8,128)(2,1)} fusion(bf16[8,1792]{1,0:T(8,128)(2,1)S(1)} %collective-permute-done.28, bf16[8,1792]{1,0:T(8,128)(2,1)S(1)} %collective-permute-done.27, bf16[8,1792]{1,0:T(8,128)(2,1)S(1)} %collective-permute-done.26, bf16[32,1792]{1,0:T(8,128)(2,1)S(1)} %add_convert_fusion.5), kind=kLoop, calls=%fused_computation.13 | loop fusion | flops 114688 | bytes 143360 | tf_op jit(solution)/shard_map/convert_element_type | solution.py:248
  (46 shorter events, 0.3 us)
Async XLA Ops:
  0.6 25.0 %copy-start = (bf16[1,1280,3584]{2,1,0:T(8,128)(2,1)S(1)}, bf16[1,1280,3584]{2,1,0:T(8,128)(2,1)}, u32[]{:S(2)}) copy-start(bf16[1,1280,3584]{2,1,0:T(8,128)(2,1)} %param.19) | copy-start | bytes 27525124
  0.6 25.0 %copy-start.1 = (bf16[1,1280,3584]{2,1,0:T(8,128)(2,1)S(1)}, bf16[1,1280,3584]{2,1,0:T(8,128)(2,1)}, u32[]{:S(2)}) copy-start(bf16[1,1280,3584]{2,1,0:T(8,128)(2,1)} %param.20) | copy-start | bytes 27525124
  0.7 25.0 %copy-start.2 = (bf16[1,1280,3584]{2,1,0:T(8,128)(2,1)S(1)}, bf16[1,1280,3584]{2,1,0:T(8,128)(2,1)}, u32[]{:S(2)}) copy-start(bf16[1,1280,3584]{2,1,0:T(8,128)(2,1)} %param.21) | copy-start | bytes 27525124
  0.7 25.0 %copy-start.3 = (bf16[1,128,1280]{2,1,0:T(8,128)(2,1)S(1)}, bf16[1,128,1280]{2,1,0:T(8,128)(2,1)}, u32[]{:S(2)}) copy-start(bf16[1,128,1280]{2,1,0:T(8,128)(2,1)} %param.17) | copy-start | bytes 983044
  0.7 25.0 %copy-start.4 = (bf16[1,128,1280]{2,1,0:T(8,128)(2,1)S(1)}, bf16[1,128,1280]{2,1,0:T(8,128)(2,1)}, u32[]{:S(2)}) copy-start(bf16[1,128,1280]{2,1,0:T(8,128)(2,1)} %param.18) | copy-start | bytes 983044
  1.8 7.6 %collective-permute-start.3 = (bf16[8,1920]{1,0:T(8,128)(2,1)S(1)}, bf16[8,1920]{1,0:T(8,128)(2,1)S(1)}, u32[]{:S(2)}, u32[]{:S(2)}) collective-permute-start(bf16[8,1920]{1,0:T(8,128)(2,1)S(1)} %get-tuple-element.26), channel_id=1, source_target_pairs={{0,8},{1,9},{2,10},{3,11},{4,12},{5,13},{6,14},{7,15},{8,0},{9,1},... | collective-permute-start | bytes 92168 | tf_op jit(solution)/shard_map/ppermute | solution.py:214
  5.9 3.9 %collective-permute-start.4 = (bf16[8,1920]{1,0:T(8,128)(2,1)S(1)}, bf16[8,1920]{1,0:T(8,128)(2,1)S(1)}, u32[]{:S(2)}, u32[]{:S(2)}) collective-permute-start(bf16[8,1920]{1,0:T(8,128)(2,1)S(1)} %get-tuple-element.26), channel_id=1, source_target_pairs={{0,4},{1,5},{2,6},{3,7},{4,0},{5,1},{6,2},{7,3},{8,12},{9,13},{10,... | collective-permute-start | bytes 92168 | tf_op jit(solution)/shard_map/ppermute | solution.py:214
  7.5 5.7 %collective-permute-start.5 = (bf16[8,1920]{1,0:T(8,128)(2,1)S(1)}, bf16[8,1920]{1,0:T(8,128)(2,1)S(1)}, u32[]{:S(2)}, u32[]{:S(2)}) collective-permute-start(bf16[8,1920]{1,0:T(8,128)(2,1)S(1)} %get-tuple-element.26), channel_id=1, source_target_pairs={{0,12},{1,13},{2,14},{3,15},{4,8},{5,9},{6,10},{7,11},{8,4},{9,5},... | collective-permute-start | bytes 92168 | tf_op jit(solution)/shard_map/ppermute | solution.py:214
  7.5 9.2 %collective-permute-start = (bf16[1,8,1920]{2,1,0:T(8,128)(2,1)S(1)}, bf16[1,8,1920]{2,1,0:T(8,128)(2,1)S(1)}, u32[]{:S(2)}, u32[]{:S(2)}) collective-permute-start(bf16[1,8,1920]{2,1,0:T(8,128)(2,1)S(1)} %bitcast.16), channel_id=1, source_target_pairs={{0,8},{1,9},{2,10},{3,11},{4,12},{5,13},{6,14},{7,15},{8,0},{9,1},... | collective-permute-start | bytes 92168 | tf_op jit(solution)/shard_map/ppermute | solution.py:214
  13.2 6.2 %collective-permute-start.6 = (bf16[32,1920]{1,0:T(8,128)(2,1)S(1)}, bf16[32,1920]{1,0:T(8,128)(2,1)S(1)}, u32[]{:S(2)}, u32[]{:S(2)}) collective-permute-start(bf16[32,1920]{1,0:T(8,128)(2,1)S(1)} %constant_dynamic-update-slice_fusion.refs_0_), channel_id=1, source_target_pairs={{0,16},{1,17},{2,18},{3,19},{4,20},{5,21},{6,22},{7,23},{8,24},{9,... | collective-permute-start | bytes 368648 | tf_op jit(solution)/shard_map/ppermute | solution.py:214
  14.7 4.9 %collective-permute-start.7 = (bf16[32,1920]{1,0:T(8,128)(2,1)S(1)}, bf16[32,1920]{1,0:T(8,128)(2,1)S(1)}, u32[]{:S(2)}, u32[]{:S(2)}) collective-permute-start(bf16[32,1920]{1,0:T(8,128)(2,1)S(1)} %constant_dynamic-update-slice_fusion.refs_0_), channel_id=1, source_target_pairs={{0,2},{1,3},{2,0},{3,1},{4,6},{5,7},{6,4},{7,5},{8,10},{9,11},{10,... | collective-permute-start | bytes 368648 | tf_op jit(solution)/shard_map/ppermute | solution.py:214
  16.2 5.8 %collective-permute-start.8 = (bf16[32,1920]{1,0:T(8,128)(2,1)S(1)}, bf16[32,1920]{1,0:T(8,128)(2,1)S(1)}, u32[]{:S(2)}, u32[]{:S(2)}) collective-permute-start(bf16[32,1920]{1,0:T(8,128)(2,1)S(1)} %constant_dynamic-update-slice_fusion.refs_0_), channel_id=1, source_target_pairs={{0,18},{1,19},{2,16},{3,17},{4,22},{5,23},{6,20},{7,21},{8,26},{9,... | collective-permute-start | bytes 368648 | tf_op jit(solution)/shard_map/ppermute | solution.py:214
  16.7 5.3 %collective-permute-start.1 = (bf16[2,8,1920]{2,1,0:T(8,128)(2,1)S(1)}, bf16[2,8,1920]{2,1,0:T(8,128)(2,1)S(1)}, u32[]{:S(2)}, u32[]{:S(2)}) collective-permute-start(bf16[2,8,1920]{2,1,0:T(8,128)(2,1)S(1)} %pad_maximum_fusion), channel_id=1, source_target_pairs={{0,4},{1,5},{2,6},{3,7},{4,0},{5,1},{6,2},{7,3},{8,12},{9,13},{10,... | collective-permute-start | bytes 184328 | tf_op jit(solution)/shard_map/ppermute | solution.py:214
  16.8 6.8 %collective-permute-start.9 = (bf16[32,1920]{1,0:T(8,128)(2,1)S(1)}, bf16[32,1920]{1,0:T(8,128)(2,1)S(1)}, u32[]{:S(2)}, u32[]{:S(2)}) collective-permute-start(bf16[32,1920]{1,0:T(8,128)(2,1)S(1)} %constant_dynamic-update-slice_fusion.refs_0_), channel_id=1, source_target_pairs={{0,1},{1,0},{2,3},{3,2},{4,5},{5,4},{6,7},{7,6},{8,9},{9,8},{10,11... | collective-permute-start | bytes 368648 | tf_op jit(solution)/shard_map/ppermute | solution.py:214
  19.4 4.7 %collective-permute-start.10 = (bf16[32,1920]{1,0:T(8,128)(2,1)S(1)}, bf16[32,1920]{1,0:T(8,128)(2,1)S(1)}, u32[]{:S(2)}, u32[]{:S(2)}) collective-permute-start(bf16[32,1920]{1,0:T(8,128)(2,1)S(1)} %collective-permute-done.6.refs_1_), channel_id=1, source_target_pairs={{0,1},{1,0},{2,3},{3,2},{4,5},{5,4},{6,7},{7,6},{8,9},{9,8},{10,11... | collective-permute-start | bytes 368648 | tf_op jit(solution)/shard_map/ppermute | solution.py:214
  19.6 6.0 %collective-permute-start.11 = (bf16[32,1920]{1,0:T(8,128)(2,1)S(1)}, bf16[32,1920]{1,0:T(8,128)(2,1)S(1)}, u32[]{:S(2)}, u32[]{:S(2)}) collective-permute-start(bf16[32,1920]{1,0:T(8,128)(2,1)S(1)} %collective-permute-done.7.refs_2_), channel_id=1, source_target_pairs={{0,1},{1,0},{2,3},{3,2},{4,5},{5,4},{6,7},{7,6},{8,9},{9,8},{10,11... | collective-permute-start | bytes 368648 | tf_op jit(solution)/shard_map/ppermute | solution.py:214
  22.0 3.6 %collective-permute-start.12 = (bf16[32,1920]{1,0:T(8,128)(2,1)S(1)}, bf16[32,1920]{1,0:T(8,128)(2,1)S(1)}, u32[]{:S(2)}, u32[]{:S(2)}) collective-permute-start(bf16[32,1920]{1,0:T(8,128)(2,1)S(1)} %collective-permute-done.8.refs_3_), channel_id=1, source_target_pairs={{0,1},{1,0},{2,3},{3,2},{4,5},{5,4},{6,7},{7,6},{8,9},{9,8},{10,11... | collective-permute-start | bytes 368648 | tf_op jit(solution)/shard_map/ppermute | solution.py:214
  22.0 9.6 %collective-permute-start.14 = (bf16[32,1920]{1,0:T(8,128)(2,1)S(1)}, bf16[32,1920]{1,0:T(8,128)(2,1)S(1)}, u32[]{:S(2)}, u32[]{:S(2)}) collective-permute-start(bf16[32,1920]{1,0:T(8,128)(2,1)S(1)} %maximum_bitcast_fusion.refs_0_), channel_id=1, source_target_pairs={{0,18},{1,19},{2,16},{3,17},{4,22},{5,23},{6,20},{7,21},{8,26},{9,... | collective-permute-start | bytes 368648 | tf_op jit(solution)/shard_map/ppermute | solution.py:214
  23.6 8.1 %collective-permute-start.13 = (bf16[32,1920]{1,0:T(8,128)(2,1)S(1)}, bf16[32,1920]{1,0:T(8,128)(2,1)S(1)}, u32[]{:S(2)}, u32[]{:S(2)}) collective-permute-start(bf16[32,1920]{1,0:T(8,128)(2,1)S(1)} %maximum_bitcast_fusion.refs_0_), channel_id=1, source_target_pairs={{0,2},{1,3},{2,0},{3,1},{4,6},{5,7},{6,4},{7,5},{8,10},{9,11},{10,... | collective-permute-start | bytes 368648 | tf_op jit(solution)/shard_map/ppermute | solution.py:214
  24.1 8.0 %collective-permute-start.2 = (bf16[32,1920]{1,0:T(8,128)(2,1)S(1)}, bf16[32,1920]{1,0:T(8,128)(2,1)S(1)}, u32[]{:S(2)}, u32[]{:S(2)}) collective-permute-start(bf16[32,1920]{1,0:T(8,128)(2,1)S(1)} %maximum_bitcast_fusion.refs_0_), channel_id=1, source_target_pairs={{0,16},{1,17},{2,18},{3,19},{4,20},{5,21},{6,22},{7,23},{8,24},{9,... | collective-permute-start | bytes 368648 | tf_op jit(solution)/shard_map/ppermute | solution.py:214
  31.0 1.4 %collective-permute-start.30 = (bf16[32,1792]{1,0:T(8,128)(2,1)S(1)}, bf16[32,1792]{1,0:T(8,128)(2,1)S(1)}, u32[]{:S(2)}, u32[]{:S(2)}) collective-permute-start(bf16[32,1792]{1,0:T(8,128)(2,1)S(1)} %get-tuple-element.43), channel_id=1, source_target_pairs={{0,1},{1,0},{2,3},{3,2},{4,5},{5,4},{6,7},{7,6},{8,9},{9,8},{10,11... | collective-permute-start | bytes 344072 | tf_op jit(solution)/shard_map/ppermute | solution.py:214
  31.1 2.5 %collective-permute-start.15 = (bf16[32,1920]{1,0:T(8,128)(2,1)S(1)}, bf16[32,1920]{1,0:T(8,128)(2,1)S(1)}, u32[]{:S(2)}, u32[]{:S(2)}) collective-permute-start(bf16[32,1920]{1,0:T(8,128)(2,1)S(1)} %maximum_bitcast_fusion.refs_0_), channel_id=1, source_target_pairs={{0,1},{1,0},{2,3},{3,2},{4,5},{5,4},{6,7},{7,6},{8,9},{9,8},{10,11... | collective-permute-start | bytes 368648 | tf_op jit(solution)/shard_map/ppermute | solution.py:214
  31.6 1.3 %collective-permute-start.32 = (bf16[32,1792]{1,0:T(8,128)(2,1)S(1)}, bf16[32,1792]{1,0:T(8,128)(2,1)S(1)}, u32[]{:S(2)}, u32[]{:S(2)}) collective-permute-start(bf16[32,1792]{1,0:T(8,128)(2,1)S(1)} %get-tuple-element.45), channel_id=1, source_target_pairs={{0,1},{1,0},{2,3},{3,2},{4,5},{5,4},{6,7},{7,6},{8,9},{9,8},{10,11... | collective-permute-start | bytes 344072 | tf_op jit(solution)/shard_map/ppermute | solution.py:214
  31.7 1.5 %collective-permute-start.34 = (bf16[32,1792]{1,0:T(8,128)(2,1)S(1)}, bf16[32,1792]{1,0:T(8,128)(2,1)S(1)}, u32[]{:S(2)}, u32[]{:S(2)}) collective-permute-start(bf16[32,1792]{1,0:T(8,128)(2,1)S(1)} %get-tuple-element.47), channel_id=1, source_target_pairs={{0,1},{1,0},{2,3},{3,2},{4,5},{5,4},{6,7},{7,6},{8,9},{9,8},{10,11... | collective-permute-start | bytes 344072 | tf_op jit(solution)/shard_map/ppermute | solution.py:214
  32.1 11.6 %collective-permute-start.29 = (bf16[32,1792]{1,0:T(8,128)(2,1)S(1)}, bf16[32,1792]{1,0:T(8,128)(2,1)S(1)}, u32[]{:S(2)}, u32[]{:S(2)}) collective-permute-start(bf16[32,1792]{1,0:T(8,128)(2,1)S(1)} %get-tuple-element.41), channel_id=1, source_target_pairs={{0,1},{1,0},{2,3},{3,2},{4,5},{5,4},{6,7},{7,6},{8,9},{9,8},{10,11... | collective-permute-start | bytes 344072 | tf_op jit(solution)/shard_map/ppermute | solution.py:214
  32.4 2.7 %collective-permute-start.18 = (bf16[32,1920]{1,0:T(8,128)(2,1)S(1)}, bf16[32,1920]{1,0:T(8,128)(2,1)S(1)}, u32[]{:S(2)}, u32[]{:S(2)}) collective-permute-start(bf16[32,1920]{1,0:T(8,128)(2,1)S(1)} %collective-permute-done.14.refs_3_), channel_id=1, source_target_pairs={{0,1},{1,0},{2,3},{3,2},{4,5},{5,4},{6,7},{7,6},{8,9},{9,8},{10,11... | collective-permute-start | bytes 368648 | tf_op jit(solution)/shard_map/ppermute | solution.py:214
  32.9 2.7 %collective-permute-start.17 = (bf16[32,1920]{1,0:T(8,128)(2,1)S(1)}, bf16[32,1920]{1,0:T(8,128)(2,1)S(1)}, u32[]{:S(2)}, u32[]{:S(2)}) collective-permute-start(bf16[32,1920]{1,0:T(8,128)(2,1)S(1)} %collective-permute-done.13.refs_2_), channel_id=1, source_target_pairs={{0,1},{1,0},{2,3},{3,2},{4,5},{5,4},{6,7},{7,6},{8,9},{9,8},{10,11... | collective-permute-start | bytes 368648 | tf_op jit(solution)/shard_map/ppermute | solution.py:214
  33.1 4.0 %collective-permute-start.16 = (bf16[32,1920]{1,0:T(8,128)(2,1)S(1)}, bf16[32,1920]{1,0:T(8,128)(2,1)S(1)}, u32[]{:S(2)}, u32[]{:S(2)}) collective-permute-start(bf16[32,1920]{1,0:T(8,128)(2,1)S(1)} %collective-permute-done.2.refs_1_), channel_id=1, source_target_pairs={{0,1},{1,0},{2,3},{3,2},{4,5},{5,4},{6,7},{7,6},{8,9},{9,8},{10,11... | collective-permute-start | bytes 368648 | tf_op jit(solution)/shard_map/ppermute | solution.py:214
  33.6 10.6 %collective-permute-start.31 = (bf16[32,1792]{1,0:T(8,128)(2,1)S(1)}, bf16[32,1792]{1,0:T(8,128)(2,1)S(1)}, u32[]{:S(2)}, u32[]{:S(2)}) collective-permute-start(bf16[32,1792]{1,0:T(8,128)(2,1)S(1)} %add_convert_fusion.3), channel_id=1, source_target_pairs={{0,18},{1,19},{2,16},{3,17},{4,22},{5,23},{6,20},{7,21},{8,26},{9,... | collective-permute-start | bytes 344072 | tf_op jit(solution)/shard_map/ppermute | solution.py:214
  35.1 9.2 %collective-permute-start.33 = (bf16[32,1792]{1,0:T(8,128)(2,1)S(1)}, bf16[32,1792]{1,0:T(8,128)(2,1)S(1)}, u32[]{:S(2)}, u32[]{:S(2)}) collective-permute-start(bf16[32,1792]{1,0:T(8,128)(2,1)S(1)} %add_convert_fusion.2), channel_id=1, source_target_pairs={{0,16},{1,17},{2,18},{3,19},{4,20},{5,21},{6,22},{7,23},{8,24},{9,... | collective-permute-start | bytes 344072 | tf_op jit(solution)/shard_map/ppermute | solution.py:214
  35.7 9.1 %collective-permute-start.35 = (bf16[32,1792]{1,0:T(8,128)(2,1)S(1)}, bf16[32,1792]{1,0:T(8,128)(2,1)S(1)}, u32[]{:S(2)}, u32[]{:S(2)}) collective-permute-start(bf16[32,1792]{1,0:T(8,128)(2,1)S(1)} %add_convert_fusion.1), channel_id=1, source_target_pairs={{0,2},{1,3},{2,0},{3,1},{4,6},{5,7},{6,4},{7,5},{8,10},{9,11},{10,... | collective-permute-start | bytes 344072 | tf_op jit(solution)/shard_map/ppermute | solution.py:214
  43.6 1.4 %collective-permute-start.20 = (bf16[32,1792]{1,0:T(8,128)(2,1)S(1)}, bf16[32,1792]{1,0:T(8,128)(2,1)S(1)}, u32[]{:S(2)}, u32[]{:S(2)}) collective-permute-start(bf16[32,1792]{1,0:T(8,128)(2,1)S(1)} %get-tuple-element.36), channel_id=1, source_target_pairs={{0,1},{1,0},{2,3},{3,2},{4,5},{5,4},{6,7},{7,6},{8,9},{9,8},{10,11... | collective-permute-start | bytes 344072 | tf_op jit(solution)/shard_map/ppermute | solution.py:214
  43.7 2.9 %collective-permute-start.22 = (bf16[32,1792]{1,0:T(8,128)(2,1)S(1)}, bf16[32,1792]{1,0:T(8,128)(2,1)S(1)}, u32[]{:S(2)}, u32[]{:S(2)}) collective-permute-start(bf16[32,1792]{1,0:T(8,128)(2,1)S(1)} %get-tuple-element.38), channel_id=1, source_target_pairs={{0,1},{1,0},{2,3},{3,2},{4,5},{5,4},{6,7},{7,6},{8,9},{9,8},{10,11... | collective-permute-start | bytes 344072 | tf_op jit(solution)/shard_map/ppermute | solution.py:214
  44.2 3.0 %collective-permute-start.24 = (bf16[32,1792]{1,0:T(8,128)(2,1)S(1)}, bf16[32,1792]{1,0:T(8,128)(2,1)S(1)}, u32[]{:S(2)}, u32[]{:S(2)}) collective-permute-start(bf16[32,1792]{1,0:T(8,128)(2,1)S(1)} %get-tuple-element.40), channel_id=1, source_target_pairs={{0,1},{1,0},{2,3},{3,2},{4,5},{5,4},{6,7},{7,6},{8,9},{9,8},{10,11... | collective-permute-start | bytes 344072 | tf_op jit(solution)/shard_map/ppermute | solution.py:214
  44.3 5.1 %collective-permute-start.19 = (bf16[32,1792]{1,0:T(8,128)(2,1)S(1)}, bf16[32,1792]{1,0:T(8,128)(2,1)S(1)}, u32[]{:S(2)}, u32[]{:S(2)}) collective-permute-start(bf16[32,1792]{1,0:T(8,128)(2,1)S(1)} %get-tuple-element.34), channel_id=1, source_target_pairs={{0,1},{1,0},{2,3},{3,2},{4,5},{5,4},{6,7},{7,6},{8,9},{9,8},{10,11... | collective-permute-start | bytes 344072 | tf_op jit(solution)/shard_map/ppermute | solution.py:214
  45.0 7.0 %collective-permute-start.21 = (bf16[32,1792]{1,0:T(8,128)(2,1)S(1)}, bf16[32,1792]{1,0:T(8,128)(2,1)S(1)}, u32[]{:S(2)}, u32[]{:S(2)}) collective-permute-start(bf16[32,1792]{1,0:T(8,128)(2,1)S(1)} %add_convert_fusion.8), channel_id=1, source_target_pairs={{0,18},{1,19},{2,16},{3,17},{4,22},{5,23},{6,20},{7,21},{8,26},{9,... | collective-permute-start | bytes 344072 | tf_op jit(solution)/shard_map/ppermute | solution.py:214
  46.6 7.1 %collective-permute-start.23 = (bf16[32,1792]{1,0:T(8,128)(2,1)S(1)}, bf16[32,1792]{1,0:T(8,128)(2,1)S(1)}, u32[]{:S(2)}, u32[]{:S(2)}) collective-permute-start(bf16[32,1792]{1,0:T(8,128)(2,1)S(1)} %add_convert_fusion.7), channel_id=1, source_target_pairs={{0,16},{1,17},{2,18},{3,19},{4,20},{5,21},{6,22},{7,23},{8,24},{9,... | collective-permute-start | bytes 344072 | tf_op jit(solution)/shard_map/ppermute | solution.py:214
  47.2 6.4 %collective-permute-start.25 = (bf16[32,1792]{1,0:T(8,128)(2,1)S(1)}, bf16[32,1792]{1,0:T(8,128)(2,1)S(1)}, u32[]{:S(2)}, u32[]{:S(2)}) collective-permute-start(bf16[32,1792]{1,0:T(8,128)(2,1)S(1)} %add_convert_fusion.6), channel_id=1, source_target_pairs={{0,2},{1,3},{2,0},{3,1},{4,6},{5,7},{6,4},{7,5},{8,10},{9,11},{10,... | collective-permute-start | bytes 344072 | tf_op jit(solution)/shard_map/ppermute | solution.py:214
  48.8 6.9 %collective-permute-start.36 = (bf16[8,1792]{1,0:T(8,128)(2,1)S(1)}, bf16[8,1792]{1,0:T(8,128)(2,1)S(1)}, u32[]{:S(2)}, u32[]{:S(2)}) collective-permute-start(bf16[8,1792]{1,0:T(8,128)(2,1)S(1)} %get-tuple-element.48), channel_id=1, source_target_pairs={{0,12},{1,13},{2,14},{3,15},{4,8},{5,9},{6,10},{7,11},{8,4},{9,5},... | collective-permute-start | bytes 86024 | tf_op jit(solution)/shard_map/ppermute | solution.py:214
  49.4 8.8 %collective-permute-start.37 = (bf16[8,1792]{1,0:T(8,128)(2,1)S(1)}, bf16[8,1792]{1,0:T(8,128)(2,1)S(1)}, u32[]{:S(2)}, u32[]{:S(2)}) collective-permute-start(bf16[8,1792]{1,0:T(8,128)(2,1)S(1)} %get-tuple-element.50), channel_id=1, source_target_pairs={{0,8},{1,9},{2,10},{3,11},{4,12},{5,13},{6,14},{7,15},{8,0},{9,1},... | collective-permute-start | bytes 86024 | tf_op jit(solution)/shard_map/ppermute | solution.py:214
  52.0 6.2 %collective-permute-start.38 = (bf16[8,1792]{1,0:T(8,128)(2,1)S(1)}, bf16[8,1792]{1,0:T(8,128)(2,1)S(1)}, u32[]{:S(2)}, u32[]{:S(2)}) collective-permute-start(bf16[8,1792]{1,0:T(8,128)(2,1)S(1)} %get-tuple-element.49), channel_id=1, source_target_pairs={{0,4},{1,5},{2,6},{3,7},{4,0},{5,1},{6,2},{7,3},{8,12},{9,13},{10,... | collective-permute-start | bytes 86024 | tf_op jit(solution)/shard_map/ppermute | solution.py:214
  53.8 5.7 %collective-permute-start.26 = (bf16[8,1792]{1,0:T(8,128)(2,1)S(1)}, bf16[8,1792]{1,0:T(8,128)(2,1)S(1)}, u32[]{:S(2)}, u32[]{:S(2)}) collective-permute-start(bf16[8,1792]{1,0:T(8,128)(2,1)S(1)} %get-tuple-element.51), channel_id=1, source_target_pairs={{0,12},{1,13},{2,14},{3,15},{4,8},{5,9},{6,10},{7,11},{8,4},{9,5},... | collective-permute-start | bytes 86024 | tf_op jit(solution)/shard_map/ppermute | solution.py:214
  54.4 5.1 %collective-permute-start.27 = (bf16[8,1792]{1,0:T(8,128)(2,1)S(1)}, bf16[8,1792]{1,0:T(8,128)(2,1)S(1)}, u32[]{:S(2)}, u32[]{:S(2)}) collective-permute-start(bf16[8,1792]{1,0:T(8,128)(2,1)S(1)} %get-tuple-element.53), channel_id=1, source_target_pairs={{0,8},{1,9},{2,10},{3,11},{4,12},{5,13},{6,14},{7,15},{8,0},{9,1},... | collective-permute-start | bytes 86024 | tf_op jit(solution)/shard_map/ppermute | solution.py:214
  55.7 4.4 %collective-permute-start.28 = (bf16[8,1792]{1,0:T(8,128)(2,1)S(1)}, bf16[8,1792]{1,0:T(8,128)(2,1)S(1)}, u32[]{:S(2)}, u32[]{:S(2)}) collective-permute-start(bf16[8,1792]{1,0:T(8,128)(2,1)S(1)} %get-tuple-element.52), channel_id=1, source_target_pairs={{0,4},{1,5},{2,6},{3,7},{4,0},{5,1},{6,2},{7,3},{8,12},{9,13},{10,... | collective-permute-start | bytes 86024 | tf_op jit(solution)/shard_map/ppermute | solution.py:214
